TPU v7x, 32 devices: a whole 2x2x4 slice. The times are simulated.
32 devices in a mesh: facet: 8 (over y, x, core), freq: 4 (over z).
Axes of the slice: x: 2, y: 2, z: 4, core: 2. Of those that a mesh axis runs over, the one named last changes fastest.
Arguments:
- residual: float32 [32, 8, 512, 512], P('freq', 'facet'), may hold values from -3 to 3
- components: bfloat16 [4, 32, 128, 128], P(None, 'freq', 'facet'), may hold values from -6 to 6
- chan_weight: float32 [32], P('freq'), may hold values from 0.3 to 3
- tile_pos: int32 [4, 2], replicated, may hold values from 0 to 1920, as said below
- facet_psf: int32 [8], P('facet'), may hold values from 0 to 3
- psf_spectra: bfloat16 [4, 32, 2, 768, 768], P(None, 'freq', None, 'facet'), may hold values from -48 to 48
Outputs:
- new_residual: float32 [32, 8, 512, 512], P('freq', 'facet')
Inputs may be any that keep to these rules, and one draw needn't show every extreme that they name: `tile_pos`: each row is a tile's top-left pixel (row, column); the row never exceeds 1024 - 128 and the column never exceeds 2048 - 128; some tile lies at the image's right edge and some tile at its top edge.
All inputs are finite; a program needn't handle non-finite values.
Results may differ from a plain program's by a relative error of at most 0.0045.
Values may be sent and summed in bfloat16 or wider, within the bound.
No kernel may reach another device: no remote copies, remote signals or barrier semaphores. Data moves between devices by JAX's collectives and lax.ppermute only.
A program may use at most 256 MiB of HBM per device.

v0:
```python
import functools
import math

import jax
import jax.numpy as jnp
from jax import lax
from jax.experimental import pallas as pl
from jax.experimental.pallas import tpu as pltpu
from jax.sharding import PartitionSpec as P

FCOLS = 4
VMEM_LIMIT = 40 * 1024 * 1024

bf16, f32, i32 = jnp.bfloat16, jnp.float32, jnp.int32


def frequency(chan, total):
    return (2.0 * chan.astype(f32) - (total - 1)) * (1.0 / total)


def moments_kernel(total, weight_ref, comp_ref, out_ref):
    ntile, nch = comp_ref.shape[:2]
    first = lax.axis_index("freq") * nch
    power = [[], [], []]
    gram = [jnp.float32(0.0)] * 5
    for c in range(nch):
        x = frequency(first + c, total)
        w = weight_ref[c]
        terms = (w, w * x, w * x * x)
        for j in range(3):
            power[j].append(terms[j])
            gram[j] = gram[j] + terms[j]
        gram[3] = gram[3] + terms[2] * x
        gram[4] = gram[4] + terms[2] * x * x
    for t in range(ntile):
        acc = [None] * 3
        for c in range(nch):
            comp = comp_ref[t, c].astype(f32)
            for j in range(3):
                term = power[j][c] * comp
                acc[j] = term if c == 0 else acc[j] + term
        for j in range(3):
            out_ref[j * ntile + t] = acc[j]
    for j in range(5):
        out_ref[3 * ntile, j : j + 1] = jnp.full((1, out_ref.shape[2]), gram[j], f32)
    rest = out_ref.shape[1] - 5
    out_ref[3 * ntile, 5:] = jnp.zeros((rest, out_ref.shape[2]), f32)


def solve_kernel(psf_ref, one_ref, two_ref, out_ref):
    ntile = (out_ref.shape[0] - 1) // 3
    gram = one_ref[3 * ntile] + two_ref[3 * ntile]
    g0, g1, g2, g3, g4 = (gram[j : j + 1] for j in range(5))
    c00 = g2 * g4 - g3 * g3
    c01 = g2 * g3 - g1 * g4
    c02 = g1 * g3 - g2 * g2
    c11 = g0 * g4 - g2 * g2
    c12 = g1 * g2 - g0 * g3
    c22 = g0 * g2 - g1 * g1
    det = g0 * c00 + g1 * c01 + g2 * c02
    for t in range(ntile):
        m0, m1, m2 = (one_ref[j * ntile + t] + two_ref[j * ntile + t] for j in range(3))
        out_ref[t] = ((c00 * m0 + c01 * m1 + c02 * m2) / det).astype(bf16)
        out_ref[ntile + t] = ((c01 * m0 + c11 * m1 + c12 * m2) / det).astype(bf16)
        out_ref[2 * ntile + t] = ((c02 * m0 + c12 * m1 + c22 * m2) / det).astype(bf16)
    out_ref[3 * ntile] = jnp.full(out_ref.shape[1:], psf_ref[0].astype(f32), f32).astype(bf16)


def cos_turn(index, frame):
    rest = jnp.abs(index - frame * jnp.floor(index * (1.0 / frame) + 0.5))
    x = (frame // 4 - rest) * (2.0 * math.pi / frame)
    square = x * x
    poly = jnp.full_like(square, 1.0 / math.factorial(13))
    for n in (11, 9, 7, 5, 3, 1):
        poly = poly * square + (-1.0) ** ((n - 1) // 2) / math.factorial(n)
    return poly * x


def lane(shape, axis):
    return lax.broadcasted_iota(i32, shape, axis)


def phases_kernel(frame, fs, pos_ref, row_ref, col_ref, inv_ref, flip_ref):
    na, ntile, two_kb, ts = row_ref.shape
    kb = two_kb // 2
    half, quarter, pad = frame // 2, frame // 4, (frame - fs) // 2
    me = lax.axis_index("facet")
    a_me, b_me = lax.div(me, FCOLS), lax.rem(me, FCOLS)
    pixel = lane((1, ts), 1)
    own = (me * kb + lane((kb, 1), 0)).astype(f32)
    for a in range(na):
        for t in range(ntile):
            oy = pos_ref[t, 0] - jnp.bitwise_xor(a_me, a) * fs + pad
            ok = jnp.where((oy >= 0) & (oy <= frame - ts), 1.0, 0.0).astype(f32)
            index = own * (oy + pixel).astype(f32)
            row_ref[a, t, :kb] = (cos_turn(index, frame) * ok).astype(bf16)
            row_ref[a, t, kb:] = (cos_turn(index + quarter, frame) * ok).astype(bf16)
    spot = lane((1, 2 * half), 1)
    freq = jnp.where(spot > half, spot - half, spot).astype(f32)
    shift = jnp.where(spot > half, quarter, 0).astype(f32)
    down = lane((ts, 1), 0)

    def columns(i, carry):
        b, t = lax.div(i, ntile), lax.rem(i, ntile)
        ox = pos_ref[t, 1] - jnp.bitwise_xor(b_me, b) * fs + pad
        ok = jnp.where((ox >= 0) & (ox <= frame - ts), 1.0, 0.0).astype(f32)
        index = (ox + down).astype(f32) * freq + shift
        col_ref[i] = (cos_turn(index, frame) * ok).astype(bf16)
        return carry

    lax.fori_loop(0, FCOLS * ntile, columns, 0)
    place = (pad + lane((1, fs), 1)).astype(f32)
    block = half // 4

    def inverse(i, carry):
        spot = i * block + lane((block, 1), 0)
        freq = jnp.where(spot > half, spot - half, spot).astype(f32)
        shift = jnp.where(spot > half, -quarter, 0).astype(f32)
        inv_ref[pl.ds(i * block, block)] = cos_turn(freq * place + shift, frame).astype(bf16)
        return carry

    lax.fori_loop(0, 8, inverse, 0)
    source = lax.rem(half - lane((1, half), 1), half)
    flip_ref[...] = jnp.where(lane((half, half), 0) == source, 1.0, 0.0).astype(bf16)


def pixel_phases_kernel(frame, pad, nf, out_ref):
    kb = frame // nf
    me = lax.axis_index("facet")
    column = lane((1, 2 * frame), 1)
    k = jnp.zeros((1, 2 * frame), i32)
    for p in range(2):
        for j in range(nf):
            start = p * frame + j * kb
            here = (column >= start) & (column < start + kb)
            k = jnp.where(here, column - start + jnp.bitwise_xor(me, j) * kb, k)
    shift = jnp.where(column >= frame, frame // 4, 0).astype(f32)
    k = k.astype(f32)
    block = 64

    def some(i, carry):
        place = (pad + i * block + lane((block, 1), 0)).astype(f32)
        out_ref[pl.ds(i * block, block)] = cos_turn(place * k + shift, frame).astype(bf16)
        return carry

    lax.fori_loop(0, out_ref.shape[0] // block, some, 0)


def rows_kernel(total, nch, chan0, psf_of_ref, coef_ref, row_ref, col_ref, inv_ref, flip_ref, psf_ref, *rest):
    out_refs, (lhs_ref, rev_ref, q_ref) = rest[:-3], rest[-3:]
    na, ntile, _, ts = row_ref.shape
    nf = coef_ref.shape[0]
    npsf, kb, frame = psf_ref.shape[0], psf_ref.shape[3], psf_ref.shape[4]
    half = frame // 2
    step = pl.program_id(1)

    @pl.when(step == 0)
    def _():
        x = frequency(lax.axis_index("freq") * nch + chan0 + pl.program_id(0), total)
        for t in range(ntile):
            a0, a1, a2 = (
                jnp.concatenate([coef_ref[f, j * ntile + t].astype(f32) for f in range(nf)], axis=0)
                for j in range(3)
            )
            model = (a0 + a1 * x + a2 * (x * x)).astype(bf16)
            for a in range(na):
                y = jnp.dot(row_ref[a, t], model, preferred_element_type=f32)
                lhs_ref[a * 2 * kb : (a + 1) * 2 * kb, t * ts : (t + 1) * ts] = y.astype(bf16)
        for p in range(npsf):
            for part in range(2):
                turned = jnp.dot(psf_ref[p, 0, part, :, half:], flip_ref[...], preferred_element_type=f32)
                rev_ref[p, part] = turned.astype(bf16)

    both = jnp.dot(lhs_ref[...], col_ref[0], preferred_element_type=f32)
    me = lax.axis_index("facet")
    first = lane((1, half), 1) == 0
    zero = jnp.zeros((kb, half), f32)
    for a in range(na):
        psf = psf_of_ref[jnp.bitwise_xor(me, a * FCOLS + step)]
        top = slice(a * 2 * kb, a * 2 * kb + kb)
        low = slice(a * 2 * kb + kb, (a + 1) * 2 * kb)
        rc, rs = both[top, :half], both[top, half:]
        ic, is_ = both[low, :half], both[low, half:]
        rs0, is0 = jnp.where(first, zero, rs), jnp.where(first, zero, is_)
        up_re, up_im = rc - is0, ic + rs0
        dn_re, dn_im = jnp.where(first, rs, rc + is_), jnp.where(first, is_, ic - rs)
        p_re, p_im = psf_ref[psf, 0, 0, :, :half].astype(f32), psf_ref[psf, 0, 1, :, :half].astype(f32)
        n_re, n_im = rev_ref[psf, 0].astype(f32), rev_ref[psf, 1].astype(f32)
        q_re, q_im = up_re * p_re - up_im * p_im, up_re * p_im + up_im * p_re
        z_re, z_im = dn_re * n_re - dn_im * n_im, dn_re * n_im + dn_im * n_re
        q_ref[top, :half] = (q_re + jnp.where(first, zero, z_re)).astype(bf16)
        q_ref[top, half:] = jnp.where(first, z_re, z_im - q_im).astype(bf16)
        q_ref[low, :half] = (q_im + jnp.where(first, zero, z_im)).astype(bf16)
        q_ref[low, half:] = jnp.where(first, z_im, q_re - z_re).astype(bf16)
    w = jnp.dot(q_ref[...], inv_ref[...], preferred_element_type=f32).astype(bf16)
    for b in range(FCOLS):

        @pl.when(step == b)
        def _():
            for a in range(na):
                for p in range(2):
                    start = (2 * a + p) * kb
                    out_refs[a * FCOLS + b][0, p] = w[start : start + kb]


def pixels_kernel(nf, scale, *refs):
    blocks, table_ref, residual_ref, out_ref = refs[:nf], refs[nf], refs[nf + 1], refs[-1]
    w = jnp.concatenate([blocks[j][0, p] for p in range(2) for j in range(nf)], axis=0)
    conv = jnp.dot(table_ref[...], w, preferred_element_type=f32)
    out_ref[0, 0] = residual_ref[0, 0] - conv * scale


def chunks_of(nch):
    return [(c, 1) for c in range(nch)]


def send_order(nf):
    return sorted(range(1, nf), key=lambda j: (-bin(j >> 1).count("1"), j))


VMEM = pl.BlockSpec(memory_space=pltpu.VMEM)
SMEM = pl.BlockSpec(memory_space=pltpu.SMEM)


def shards(nf, nz, residual, components, chan_weight, tile_pos, facet_psf, psf_spectra):
    ntile, nch, rows, ts = components.shape
    npsf, _, _, kb, frame = psf_spectra.shape
    fs = residual.shape[2]
    pad, half = (frame - fs) // 2, frame // 2
    total = nch * nz
    na = nf // FCOLS

    sums = pl.pallas_call(
        functools.partial(moments_kernel, total),
        out_shape=jax.ShapeDtypeStruct((3 * ntile + 1, rows, ts), f32),
        in_specs=[SMEM, VMEM],
        out_specs=VMEM,
        name="moments",
    )(chan_weight, components)
    row_table, col_table, inv_table, flip = pl.pallas_call(
        functools.partial(phases_kernel, frame, fs),
        out_shape=[
            jax.ShapeDtypeStruct((na, ntile, 2 * kb, ts), bf16),
            jax.ShapeDtypeStruct((FCOLS * ntile, ts, frame), bf16),
            jax.ShapeDtypeStruct((frame, fs), bf16),
            jax.ShapeDtypeStruct((half, half), bf16),
        ],
        in_specs=[SMEM],
        out_specs=[VMEM] * 4,
        compiler_params=pltpu.CompilerParams(vmem_limit_bytes=VMEM_LIMIT),
        name="phases",
    )(tile_pos)
    col_table = col_table.reshape(FCOLS, ntile * ts, frame)
    other = jnp.zeros_like(sums)
    for i in range(nz.bit_length() - 1):
        if i:
            sums = sums + other
        other = lax.ppermute(sums, "freq", [(s, s ^ (1 << i)) for s in range(nz)])
    fit = pl.pallas_call(
        solve_kernel,
        out_shape=jax.ShapeDtypeStruct((3 * ntile + 1, rows, ts), bf16),
        in_specs=[SMEM, VMEM, VMEM],
        out_specs=VMEM,
        name="solve",
    )(facet_psf, sums, other)
    fit = lax.all_gather(fit, "facet", axis=0)
    psf_of = fit[:, 3 * ntile, 0, 0].astype(i32)
    pix_table = pl.pallas_call(
        functools.partial(pixel_phases_kernel, frame, pad, nf),
        out_shape=jax.ShapeDtypeStruct((fs, 2 * frame), bf16),
        out_specs=VMEM,
        name="pixphases",
    )()

    pieces = []
    for chan0, count in chunks_of(nch):
        w = pl.pallas_call(
            functools.partial(rows_kernel, total, nch, chan0),
            grid_spec=pltpu.PrefetchScalarGridSpec(
                num_scalar_prefetch=1,
                grid=(count, FCOLS),
                in_specs=[
                    pl.BlockSpec((nf, 3 * ntile + 1, rows, ts), lambda c, b, s: (0, 0, 0, 0)),
                    pl.BlockSpec((na, ntile, 2 * kb, ts), lambda c, b, s: (0, 0, 0, 0)),
                    pl.BlockSpec((1, ntile * ts, frame), lambda c, b, s: (b, 0, 0)),
                    pl.BlockSpec((frame, fs), lambda c, b, s: (0, 0)),
                    pl.BlockSpec((half, half), lambda c, b, s: (0, 0)),
                    pl.BlockSpec((npsf, 1, 2, kb, frame), lambda c, b, s, c0=chan0: (0, c0 + c, 0, 0, 0)),
                ],
                out_specs=[pl.BlockSpec((1, 2, kb, fs), lambda c, b, s: (c, 0, 0, 0))] * nf,
                scratch_shapes=[
                    pltpu.VMEM((na * 2 * kb, ntile * ts), bf16),
                    pltpu.VMEM((npsf, 2, kb, half), bf16),
                    pltpu.VMEM((na * 2 * kb, frame), bf16),
                ],
            ),
            out_shape=[jax.ShapeDtypeStruct((count, 2, kb, fs), bf16)] * nf,
            cost_estimate=pl.CostEstimate(
                flops=count * nf * 4 * kb * frame * (ntile * ts + fs),
                bytes_accessed=count * (npsf * 4 * kb * frame + nf * 4 * kb * fs) + 8 * ntile * ts * frame,
                transcendentals=0,
            ),
            compiler_params=pltpu.CompilerParams(vmem_limit_bytes=VMEM_LIMIT),
            name="rows",
        )(psf_of, fit, row_table, col_table, inv_table, flip, psf_spectra)
        got = [w[0]] + [None] * (nf - 1)
        for j in send_order(nf):
            got[j] = lax.ppermute(w[j], "facet", [(s, s ^ j) for s in range(nf)])
        pieces.append((chan0, count, got))
    result = None
    for chan0, count, got in pieces:
        image = pl.BlockSpec((1, 1, fs, fs), lambda c, c0=chan0: (c0 + c, 0, 0, 0))
        before = [] if result is None else [result]
        result = pl.pallas_call(
            functools.partial(pixels_kernel, nf, 1.0 / (frame * frame)),
            grid=(count,),
            in_specs=[pl.BlockSpec((1, 2, kb, fs), lambda c: (c, 0, 0, 0))] * nf
            + [pl.BlockSpec((fs, 2 * frame), lambda c: (0, 0)), image]
            + [pl.BlockSpec(memory_space=pl.ANY)] * len(before),
            out_specs=image,
            out_shape=jax.ShapeDtypeStruct(residual.shape, f32),
            input_output_aliases={nf + 2: 0} if before else {},
            cost_estimate=pl.CostEstimate(
                flops=count * 4 * fs * frame * fs,
                bytes_accessed=count * (nf * 4 * kb * fs + 8 * fs * fs),
                transcendentals=0,
            ),
            compiler_params=pltpu.CompilerParams(vmem_limit_bytes=VMEM_LIMIT),
            name="pixels",
        )(*got, pix_table, residual, *before)
    return result


def solution(mesh):
    placed = (
        P("freq", "facet", None, None),
        P(None, "freq", "facet", None),
        P("freq"),
        P(),
        P("facet"),
        P(None, "freq", None, "facet", None),
    )
    nf, nz = mesh.shape["facet"], mesh.shape["freq"]

    def step(*args):
        return shards(nf, nz, *args)

    return jax.shard_map(
        step,
        mesh=mesh,
        in_specs=placed,
        out_specs=P("freq", "facet", None, None),
        check_vma=False,
    )
```

profile of v0, /device:TPU:0, one launch (start us, length us, event | category | flops | bytes accessed | tf_op | source)
XLA Modules:
  0.0 224.4 jit_solution(2255220564479236032)
XLA Ops:
  0.0 1.6 moments.1
  1.6 3.1 %collective-permute-start = (f32[13,16,128]{2,1,0:T(8,128)}, f32[13,16,128]{2,1,0:T(8,128)S(1)}, u32[]{:S(2)}, u32[]{:S(2)}) collective-permute-start(f32[13,16,128]{2,1,0:T(8,128)} %moments.1), channel_id=1, source_target_pairs={{0,1},{1,0},{2,3},{3,2},{4,5},{5,4},{6,7},{7,6},{8,9},{9,8},{10,11... | collective-permute-start | bytes 319496 | tf_op jit(solution)/shard_map/ppermute | solution.py:258
  4.7 3.2 %collective-permute-done = f32[13,16,128]{2,1,0:T(8,128)S(1)} collective-permute-done((f32[13,16,128]{2,1,0:T(8,128)}, f32[13,16,128]{2,1,0:T(8,128)S(1)}, u32[]{:S(2)}, u32[]{:S(2)}) %collective-permute-start) | collective-permute-done | bytes 106528 | tf_op jit(solution)/shard_map/ppermute | solution.py:258
  9.4 2.8 %collective-permute-start.1 = (f32[13,16,128]{2,1,0:T(8,128)}, f32[13,16,128]{2,1,0:T(8,128)}, u32[]{:S(2)}, u32[]{:S(2)}) collective-permute-start(f32[13,16,128]{2,1,0:T(8,128)} %add.3.one_ref), channel_id=1, source_target_pairs={{0,2},{1,3},{2,0},{3,1},{4,6},{5,7},{6,4},{7,5},{8,10},{9,11},{10,... | collective-permute-start | bytes 319496 | tf_op jit(solution)/shard_map/ppermute | solution.py:258
  13.6 8.2 %phases.1 = (bf16[2,4,192,128]{3,2,1,0:T(8,128)(2,1)S(1)}, bf16[16,128,768]{2,1,0:T(8,128)(2,1)S(1)}, bf16[768,512]{1,0:T(8,128)(2,1)S(1)}, bf16[384,384]{1,0:T(8,128)(2,1)S(1)}) custom-call(s32[4,2]{1,0:T(4,128)S(1)} %copy.16.pos_ref), custom_call_target="tpu_custom_call" | custom-call | tf_op jit(solution)/shard_map/phases/pallas_call | solution.py:240
  25.0 10.0 %all-gather = bf16[104,16,128]{2,1,0:T(8,128)(2,1)S(1)} all-gather(bf16[13,16,128]{2,1,0:T(8,128)(2,1)} %solve.1), channel_id=2, replica_groups=mesh['facet'=8,'freq'=4] {'facet'}, dimensions={0}, use_global_device_ids=true | all-gather | bytes 479232 | tf_op jit(solution)/shard_map/all_gather | solution.py:266
  37.3 7.2 %rows.15 = (bf16[1,2,96,512]{3,2,1,0:T(8,128)(2,1)S(1)}, bf16[1,2,96,512]{3,2,1,0:T(8,128)(2,1)S(1)}, bf16[1,2,96,512]{3,2,1,0:T(8,128)(2,1)S(1)}, bf16[1,2,96,5...) custom-call(s32[8]{0:T(128)S(1)} %fusion.psf_of_ref, ...), custom_call_target="tpu_custom_call" | custom-call | flops 2415919104 | bytes 5898240 | tf_op jit(solution)/shard_map/rows/pallas_call | solution.py:277
  50.5 7.2 %rows.14 = (bf16[1,2,96,512]{3,2,1,0:T(8,128)(2,1)S(1)}, bf16[1,2,96,512]{3,2,1,0:T(8,128)(2,1)S(1)}, bf16[1,2,96,512]{3,2,1,0:T(8,128)(2,1)S(1)}, bf16[1,2,96,5...) custom-call(s32[8]{0:T(128)S(1)} %fusion.psf_of_ref, ...), custom_call_target="tpu_custom_call" | custom-call | flops 2415919104 | bytes 5898240 | tf_op jit(solution)/shard_map/rows/pallas_call | solution.py:277
  62.7 4.1 %collective-permute-done.55.refs_5_ = bf16[1,2,96,512]{3,2,1,0:T(8,128)(2,1)S(1)} collective-permute-done((bf16[1,2,96,512]{3,2,1,0:T(8,128)(2,1)S(1)}, bf16[1,2,96,512]{3,2,1,0:T(8,128)(2,1)S(1)}, u32[]{:S(2)}, u32[]{:S(2)}) %collective-permute-start.55) | collective-permute-done | bytes 196640 | tf_op jit(solution)/shard_map/ppermute | solution.py:308
  68.9 7.2 %rows.13 = (bf16[1,2,96,512]{3,2,1,0:T(8,128)(2,1)S(1)}, bf16[1,2,96,512]{3,2,1,0:T(8,128)(2,1)S(1)}, bf16[1,2,96,512]{3,2,1,0:T(8,128)(2,1)S(1)}, bf16[1,2,96,5...) custom-call(s32[8]{0:T(128)S(1)} %fusion.psf_of_ref, ...), custom_call_target="tpu_custom_call" | custom-call | flops 2415919104 | bytes 5898240 | tf_op jit(solution)/shard_map/rows/pallas_call | solution.py:277
  81.3 11.0 %collective-permute-done.48.refs_5_ = bf16[1,2,96,512]{3,2,1,0:T(8,128)(2,1)S(1)} collective-permute-done((bf16[1,2,96,512]{3,2,1,0:T(8,128)(2,1)S(1)}, bf16[1,2,96,512]{3,2,1,0:T(8,128)(2,1)S(1)}, u32[]{:S(2)}, u32[]{:S(2)}) %collective-permute-start.48) | collective-permute-done | bytes 196640 | tf_op jit(solution)/shard_map/ppermute | solution.py:308
  97.7 7.2 %rows.12 = (bf16[1,2,96,512]{3,2,1,0:T(8,128)(2,1)S(1)}, bf16[1,2,96,512]{3,2,1,0:T(8,128)(2,1)S(1)}, bf16[1,2,96,512]{3,2,1,0:T(8,128)(2,1)S(1)}, bf16[1,2,96,5...) custom-call(s32[8]{0:T(128)S(1)} %fusion.psf_of_ref, ...), custom_call_target="tpu_custom_call" | custom-call | flops 2415919104 | bytes 5898240 | tf_op jit(solution)/shard_map/rows/pallas_call | solution.py:277
  105.5 4.0 %collective-permute-done.40.refs_4_ = bf16[1,2,96,512]{3,2,1,0:T(8,128)(2,1)S(1)} collective-permute-done((bf16[1,2,96,512]{3,2,1,0:T(8,128)(2,1)S(1)}, bf16[1,2,96,512]{3,2,1,0:T(8,128)(2,1)S(1)}, u32[]{:S(2)}, u32[]{:S(2)}) %collective-permute-start.40) | collective-permute-done | bytes 196640 | tf_op jit(solution)/shard_map/ppermute | solution.py:308
  110.2 2.4 %collective-permute-done.41.refs_5_ = bf16[1,2,96,512]{3,2,1,0:T(8,128)(2,1)S(1)} collective-permute-done((bf16[1,2,96,512]{3,2,1,0:T(8,128)(2,1)S(1)}, bf16[1,2,96,512]{3,2,1,0:T(8,128)(2,1)S(1)}, u32[]{:S(2)}, u32[]{:S(2)}) %collective-permute-start.41) | collective-permute-done | bytes 196640 | tf_op jit(solution)/shard_map/ppermute | solution.py:308
  115.0 8.2 %rows.11 = (bf16[1,2,96,512]{3,2,1,0:T(8,128)(2,1)S(1)}, bf16[1,2,96,512]{3,2,1,0:T(8,128)(2,1)S(1)}, bf16[1,2,96,512]{3,2,1,0:T(8,128)(2,1)S(1)}, bf16[1,2,96,5...) custom-call(s32[8]{0:T(128)S(1)} %fusion.psf_of_ref, ...), custom_call_target="tpu_custom_call" | custom-call | flops 2415919104 | bytes 5898240 | tf_op jit(solution)/shard_map/rows/pallas_call | solution.py:277
  124.8 1.6 collective-permute-start.36
  128.3 8.0 %rows.10 = (bf16[1,2,96,512]{3,2,1,0:T(8,128)(2,1)S(1)}, bf16[1,2,96,512]{3,2,1,0:T(8,128)(2,1)}, bf16[1,2,96,512]{3,2,1,0:T(8,128)(2,1)S(1)}, bf16[1,2,96,512]{...) custom-call(s32[8]{0:T(128)S(1)} %fusion.psf_of_ref, ...), custom_call_target="tpu_custom_call" | custom-call | flops 2415919104 | bytes 5898240 | tf_op jit(solution)/shard_map/rows/pallas_call | solution.py:277
  149.4 3.7 %pixphases.1.refs_8_ = bf16[512,1536]{1,0:T(8,128)(2,1)} custom-call(), custom_call_target="tpu_custom_call" | custom-call | tf_op jit(solution)/shard_map/pixphases/pallas_call | solution.py:268
  153.1 5.2 %collective-permute-done.26.refs_4_ = bf16[1,2,96,512]{3,2,1,0:T(8,128)(2,1)} collective-permute-done((bf16[1,2,96,512]{3,2,1,0:T(8,128)(2,1)}, bf16[1,2,96,512]{3,2,1,0:T(8,128)(2,1)}, u32[]{:S(2)}, u32[]{:S(2)}) %collective-permute-start.26) | collective-permute-done | bytes 196640 | tf_op jit(solution)/shard_map/ppermute | solution.py:308
  159.7 1.8 collective-permute-done.27.refs_5_
  168.8 7.5 %rows.9 = (bf16[1,2,96,512]{3,2,1,0:T(8,128)(2,1)S(1)}, bf16[1,2,96,512]{3,2,1,0:T(8,128)(2,1)S(1)}, bf16[1,2,96,512]{3,2,1,0:T(8,128)(2,1)S(1)}, bf16[1,2,96,51...) custom-call(s32[8]{0:T(128)S(1)} %fusion.psf_of_ref, ...), custom_call_target="tpu_custom_call" | custom-call | flops 2415919104 | bytes 5898240 | tf_op jit(solution)/shard_map/rows/pallas_call | solution.py:277
  181.5 7.2 %rows.8 = (bf16[1,2,96,512]{3,2,1,0:T(8,128)(2,1)S(1)}, bf16[1,2,96,512]{3,2,1,0:T(8,128)(2,1)S(1)}, bf16[1,2,96,512]{3,2,1,0:T(8,128)(2,1)S(1)}, bf16[1,2,96,51...) custom-call(s32[8]{0:T(128)S(1)} %fusion.psf_of_ref, ...), custom_call_target="tpu_custom_call" | custom-call | flops 2415919104 | bytes 5898240 | tf_op jit(solution)/shard_map/rows/pallas_call | solution.py:277
  188.9 2.0 pixels.8.refs_10_
  194.8 2.0 pixels.9.refs_10_
  196.9 2.0 pixels.10.refs_10_
  199.0 2.0 pixels.11.refs_10_
  202.8 2.1 collective-permute-start.6
  207.3 3.2 %pixels.12.refs_10_ = f32[8,1,512,512]{3,2,1,0:T(8,128)} custom-call(bf16[1,2,96,512]{3,2,1,0:T(8,128)(2,1)S(1)} %copy-done.58, bf16[1,2,96,512]{3,2,1,0:T(8,128)(2,1)S(1)} %copy-done.68, bf16[1,2,96,512]{3,2,1,0:T(8,128)(2,1)S(1)} %copy-done.72, bf16[1,2,96,512]{3,2,1,0:T(8,128)(2,1)S(1)} %copy-done.76, ...), custom_call_target="tpu_custom_call", output_to_operand_aliasing={{}: (10, {})} | custom-call | flops 805306368 | bytes 3670016 | tf_op jit(solution)/shard_map/pixels/pallas_call | solution.py:314
  210.5 2.9 %pixels.13.refs_10_ = f32[8,1,512,512]{3,2,1,0:T(8,128)} custom-call(bf16[1,2,96,512]{3,2,1,0:T(8,128)(2,1)S(1)} %copy-done.78, bf16[1,2,96,512]{3,2,1,0:T(8,128)(2,1)} %collective-permute-done.16.refs_1_, bf16[1,2,96,512]{3,2,1,0:T(8,128)(2,1)S(1)} %collective-permute-done.17.refs_2_, ...), custom_call_target="tpu_custom_call", output_to_operand_aliasing={{}: (10, {})} | custom-call | flops 805306368 | bytes 3670016 | tf_op jit(solution)/shard_map/pixels/pallas_call | solution.py:314
  213.4 2.0 pixels.14.refs_10_
  215.4 7.1 %collective-permute-done.6.refs_5_ = bf16[1,2,96,512]{3,2,1,0:T(8,128)(2,1)S(1)} collective-permute-done((bf16[1,2,96,512]{3,2,1,0:T(8,128)(2,1)S(1)}, bf16[1,2,96,512]{3,2,1,0:T(8,128)(2,1)S(1)}, u32[]{:S(2)}, u32[]{:S(2)}) %collective-permute-start.6) | collective-permute-done | bytes 196640 | tf_op jit(solution)/shard_map/ppermute | solution.py:308
  222.4 2.0 pixels.15
  (293 shorter events, 73.3 us)
Async XLA Ops:
  48.3 18.5 %collective-permute-start.55 = (bf16[1,2,96,512]{3,2,1,0:T(8,128)(2,1)S(1)}, bf16[1,2,96,512]{3,2,1,0:T(8,128)(2,1)S(1)}, u32[]{:S(2)}, u32[]{:S(2)}) collective-permute-start(bf16[1,2,96,512]{3,2,1,0:T(8,128)(2,1)S(1)} %get-tuple-element.138), channel_id=1, source_target_pairs={{0,20},{4,16},{8,28},{12,24},{16,4},{20,0},{24,12},{28,8},{1,21},{... | collective-permute-start | bytes 589832 | tf_op jit(solution)/shard_map/ppermute | solution.py:308
  49.1 19.0 %collective-permute-start.56 = (bf16[1,2,96,512]{3,2,1,0:T(8,128)(2,1)S(1)}, bf16[1,2,96,512]{3,2,1,0:T(8,128)(2,1)S(1)}, u32[]{:S(2)}, u32[]{:S(2)}) collective-permute-start(bf16[1,2,96,512]{3,2,1,0:T(8,128)(2,1)S(1)} %get-tuple-element.139), channel_id=1, source_target_pairs={{0,24},{4,28},{8,16},{12,20},{16,8},{20,12},{24,0},{28,4},{1,25},{... | collective-permute-start | bytes 589832 | tf_op jit(solution)/shard_map/ppermute | solution.py:308
  58.5 18.3 %collective-permute-start.57 = (bf16[1,2,96,512]{3,2,1,0:T(8,128)(2,1)S(1)}, bf16[1,2,96,512]{3,2,1,0:T(8,128)(2,1)S(1)}, u32[]{:S(2)}, u32[]{:S(2)}) collective-permute-start(bf16[1,2,96,512]{3,2,1,0:T(8,128)(2,1)S(1)} %get-tuple-element.140), channel_id=1, source_target_pairs={{0,28},{4,24},{8,20},{12,16},{16,12},{20,8},{24,4},{28,0},{1,29},{... | collective-permute-start | bytes 589832 | tf_op jit(solution)/shard_map/ppermute | solution.py:308
  60.2 17.3 %collective-permute-start.44 = (bf16[1,2,96,512]{3,2,1,0:T(8,128)(2,1)S(1)}, bf16[1,2,96,512]{3,2,1,0:T(8,128)(2,1)S(1)}, u32[]{:S(2)}, u32[]{:S(2)}) collective-permute-start(bf16[1,2,96,512]{3,2,1,0:T(8,128)(2,1)S(1)} %get-tuple-element.126), channel_id=1, source_target_pairs={{0,4},{4,0},{8,12},{12,8},{16,20},{20,16},{24,28},{28,24},{1,5},{5... | collective-permute-start | bytes 589832 | tf_op jit(solution)/shard_map/ppermute | solution.py:308
  61.5 17.4 %collective-permute-start.45 = (bf16[1,2,96,512]{3,2,1,0:T(8,128)(2,1)S(1)}, bf16[1,2,96,512]{3,2,1,0:T(8,128)(2,1)S(1)}, u32[]{:S(2)}, u32[]{:S(2)}) collective-permute-start(bf16[1,2,96,512]{3,2,1,0:T(8,128)(2,1)S(1)} %get-tuple-element.127), channel_id=1, source_target_pairs={{0,8},{4,12},{8,0},{12,4},{16,24},{20,28},{24,16},{28,20},{1,9},{5... | collective-permute-start | bytes 589832 | tf_op jit(solution)/shard_map/ppermute | solution.py:308
  76.8 15.6 %collective-permute-start.48 = (bf16[1,2,96,512]{3,2,1,0:T(8,128)(2,1)S(1)}, bf16[1,2,96,512]{3,2,1,0:T(8,128)(2,1)S(1)}, u32[]{:S(2)}, u32[]{:S(2)}) collective-permute-start(bf16[1,2,96,512]{3,2,1,0:T(8,128)(2,1)S(1)} %get-tuple-element.130), channel_id=1, source_target_pairs={{0,20},{4,16},{8,28},{12,24},{16,4},{20,0},{24,12},{28,8},{1,21},{... | collective-permute-start | bytes 589832 | tf_op jit(solution)/shard_map/ppermute | solution.py:308
  77.4 15.9 %collective-permute-start.49 = (bf16[1,2,96,512]{3,2,1,0:T(8,128)(2,1)S(1)}, bf16[1,2,96,512]{3,2,1,0:T(8,128)(2,1)S(1)}, u32[]{:S(2)}, u32[]{:S(2)}) collective-permute-start(bf16[1,2,96,512]{3,2,1,0:T(8,128)(2,1)S(1)} %get-tuple-element.131), channel_id=1, source_target_pairs={{0,24},{4,28},{8,16},{12,20},{16,8},{20,12},{24,0},{28,4},{1,25},{... | collective-permute-start | bytes 589832 | tf_op jit(solution)/shard_map/ppermute | solution.py:308
  78.9 15.2 %collective-permute-start.50 = (bf16[1,2,96,512]{3,2,1,0:T(8,128)(2,1)S(1)}, bf16[1,2,96,512]{3,2,1,0:T(8,128)(2,1)S(1)}, u32[]{:S(2)}, u32[]{:S(2)}) collective-permute-start(bf16[1,2,96,512]{3,2,1,0:T(8,128)(2,1)S(1)} %get-tuple-element.132), channel_id=1, source_target_pairs={{0,28},{4,24},{8,20},{12,16},{16,12},{20,8},{24,4},{28,0},{1,29},{... | collective-permute-start | bytes 589832 | tf_op jit(solution)/shard_map/ppermute | solution.py:308
  80.5 16.1 %collective-permute-start.38 = (bf16[1,2,96,512]{3,2,1,0:T(8,128)(2,1)S(1)}, bf16[1,2,96,512]{3,2,1,0:T(8,128)(2,1)S(1)}, u32[]{:S(2)}, u32[]{:S(2)}) collective-permute-start(bf16[1,2,96,512]{3,2,1,0:T(8,128)(2,1)S(1)} %get-tuple-element.119), channel_id=1, source_target_pairs={{0,8},{4,12},{8,0},{12,4},{16,24},{20,28},{24,16},{28,20},{1,9},{5... | collective-permute-start | bytes 589832 | tf_op jit(solution)/shard_map/ppermute | solution.py:308
  93.3 16.2 %collective-permute-start.40 = (bf16[1,2,96,512]{3,2,1,0:T(8,128)(2,1)S(1)}, bf16[1,2,96,512]{3,2,1,0:T(8,128)(2,1)S(1)}, u32[]{:S(2)}, u32[]{:S(2)}) collective-permute-start(bf16[1,2,96,512]{3,2,1,0:T(8,128)(2,1)S(1)} %get-tuple-element.121), channel_id=1, source_target_pairs={{0,16},{4,20},{8,24},{12,28},{16,0},{20,4},{24,8},{28,12},{1,17},{... | collective-permute-start | bytes 589832 | tf_op jit(solution)/shard_map/ppermute | solution.py:308
  94.2 18.5 %collective-permute-start.41 = (bf16[1,2,96,512]{3,2,1,0:T(8,128)(2,1)S(1)}, bf16[1,2,96,512]{3,2,1,0:T(8,128)(2,1)S(1)}, u32[]{:S(2)}, u32[]{:S(2)}) collective-permute-start(bf16[1,2,96,512]{3,2,1,0:T(8,128)(2,1)S(1)} %get-tuple-element.122), channel_id=1, source_target_pairs={{0,20},{4,16},{8,28},{12,24},{16,4},{20,0},{24,12},{28,8},{1,21},{... | collective-permute-start | bytes 589832 | tf_op jit(solution)/shard_map/ppermute | solution.py:308
  95.1 18.5 %collective-permute-start.42 = (bf16[1,2,96,512]{3,2,1,0:T(8,128)(2,1)S(1)}, bf16[1,2,96,512]{3,2,1,0:T(8,128)(2,1)S(1)}, u32[]{:S(2)}, u32[]{:S(2)}) collective-permute-start(bf16[1,2,96,512]{3,2,1,0:T(8,128)(2,1)S(1)} %get-tuple-element.123), channel_id=1, source_target_pairs={{0,24},{4,28},{8,16},{12,20},{16,8},{20,12},{24,0},{28,4},{1,25},{... | collective-permute-start | bytes 589832 | tf_op jit(solution)/shard_map/ppermute | solution.py:308
  96.6 18.4 %collective-permute-start.43 = (bf16[1,2,96,512]{3,2,1,0:T(8,128)(2,1)S(1)}, bf16[1,2,96,512]{3,2,1,0:T(8,128)(2,1)S(1)}, u32[]{:S(2)}, u32[]{:S(2)}) collective-permute-start(bf16[1,2,96,512]{3,2,1,0:T(8,128)(2,1)S(1)} %get-tuple-element.124), channel_id=1, source_target_pairs={{0,28},{4,24},{8,20},{12,16},{16,12},{20,8},{24,4},{28,0},{1,29},{... | collective-permute-start | bytes 589832 | tf_op jit(solution)/shard_map/ppermute | solution.py:308
  105.0 18.2 %collective-permute-start.30 = (bf16[1,2,96,512]{3,2,1,0:T(8,128)(2,1)S(1)}, bf16[1,2,96,512]{3,2,1,0:T(8,128)(2,1)S(1)}, u32[]{:S(2)}, u32[]{:S(2)}) collective-permute-start(bf16[1,2,96,512]{3,2,1,0:T(8,128)(2,1)S(1)} %get-tuple-element.110), channel_id=1, source_target_pairs={{0,4},{4,0},{8,12},{12,8},{16,20},{20,16},{24,28},{28,24},{1,5},{5... | collective-permute-start | bytes 589832 | tf_op jit(solution)/shard_map/ppermute | solution.py:308
  109.5 15.3 %collective-permute-start.31 = (bf16[1,2,96,512]{3,2,1,0:T(8,128)(2,1)S(1)}, bf16[1,2,96,512]{3,2,1,0:T(8,128)(2,1)S(1)}, u32[]{:S(2)}, u32[]{:S(2)}) collective-permute-start(bf16[1,2,96,512]{3,2,1,0:T(8,128)(2,1)S(1)} %get-tuple-element.111), channel_id=1, source_target_pairs={{0,8},{4,12},{8,0},{12,4},{16,24},{20,28},{24,16},{28,20},{1,9},{5... | collective-permute-start | bytes 589832 | tf_op jit(solution)/shard_map/ppermute | solution.py:308
  123.2 17.9 %collective-permute-start.35 = (bf16[1,2,96,512]{3,2,1,0:T(8,128)(2,1)S(1)}, bf16[1,2,96,512]{3,2,1,0:T(8,128)(2,1)S(1)}, u32[]{:S(2)}, u32[]{:S(2)}) collective-permute-start(bf16[1,2,96,512]{3,2,1,0:T(8,128)(2,1)S(1)} %get-tuple-element.115), channel_id=1, source_target_pairs={{0,24},{4,28},{8,16},{12,20},{16,8},{20,12},{24,0},{28,4},{1,25},{... | collective-permute-start | bytes 589832 | tf_op jit(solution)/shard_map/ppermute | solution.py:308
  124.8 18.3 %collective-permute-start.36 = (bf16[1,2,96,512]{3,2,1,0:T(8,128)(2,1)S(1)}, bf16[1,2,96,512]{3,2,1,0:T(8,128)(2,1)S(1)}, u32[]{:S(2)}, u32[]{:S(2)}) collective-permute-start(bf16[1,2,96,512]{3,2,1,0:T(8,128)(2,1)S(1)} %get-tuple-element.116), channel_id=1, source_target_pairs={{0,28},{4,24},{8,20},{12,16},{16,12},{20,8},{24,4},{28,0},{1,29},{... | collective-permute-start | bytes 589832 | tf_op jit(solution)/shard_map/ppermute | solution.py:308
  126.4 17.9 %collective-permute-start.23 = (bf16[1,2,96,512]{3,2,1,0:T(8,128)(2,1)S(1)}, bf16[1,2,96,512]{3,2,1,0:T(8,128)(2,1)S(1)}, u32[]{:S(2)}, u32[]{:S(2)}) collective-permute-start(bf16[1,2,96,512]{3,2,1,0:T(8,128)(2,1)S(1)} %get-tuple-element.102), channel_id=1, source_target_pairs={{0,4},{4,0},{8,12},{12,8},{16,20},{20,16},{24,28},{28,24},{1,5},{5... | collective-permute-start | bytes 589832 | tf_op jit(solution)/shard_map/ppermute | solution.py:308
  126.5 20.1 %collective-permute-start.24 = (bf16[1,2,96,512]{3,2,1,0:T(8,128)(2,1)S(1)}, bf16[1,2,96,512]{3,2,1,0:T(8,128)(2,1)S(1)}, u32[]{:S(2)}, u32[]{:S(2)}) collective-permute-start(bf16[1,2,96,512]{3,2,1,0:T(8,128)(2,1)S(1)} %get-tuple-element.103), channel_id=1, source_target_pairs={{0,8},{4,12},{8,0},{12,4},{16,24},{20,28},{24,16},{28,20},{1,9},{5... | collective-permute-start | bytes 589832 | tf_op jit(solution)/shard_map/ppermute | solution.py:308
  127.8 20.5 %collective-permute-start.25 = (bf16[1,2,96,512]{3,2,1,0:T(8,128)(2,1)S(1)}, bf16[1,2,96,512]{3,2,1,0:T(8,128)(2,1)S(1)}, u32[]{:S(2)}, u32[]{:S(2)}) collective-permute-start(bf16[1,2,96,512]{3,2,1,0:T(8,128)(2,1)S(1)} %get-tuple-element.104), channel_id=1, source_target_pairs={{0,12},{4,8},{8,4},{12,0},{16,28},{20,24},{24,20},{28,16},{1,13},{... | collective-permute-start | bytes 589832 | tf_op jit(solution)/shard_map/ppermute | solution.py:308
  141.9 16.5 %collective-permute-start.26 = (bf16[1,2,96,512]{3,2,1,0:T(8,128)(2,1)}, bf16[1,2,96,512]{3,2,1,0:T(8,128)(2,1)}, u32[]{:S(2)}, u32[]{:S(2)}) collective-permute-start(bf16[1,2,96,512]{3,2,1,0:T(8,128)(2,1)} %get-tuple-element.105), channel_id=1, source_target_pairs={{0,16},{4,20},{8,24},{12,28},{16,0},{20,4},{24,8},{28,12},{1,17},{... | collective-permute-start | bytes 589832 | tf_op jit(solution)/shard_map/ppermute | solution.py:308
  143.8 17.6 %collective-permute-start.27 = (bf16[1,2,96,512]{3,2,1,0:T(8,128)(2,1)}, bf16[1,2,96,512]{3,2,1,0:T(8,128)(2,1)}, u32[]{:S(2)}, u32[]{:S(2)}) collective-permute-start(bf16[1,2,96,512]{3,2,1,0:T(8,128)(2,1)} %get-tuple-element.106), channel_id=1, source_target_pairs={{0,20},{4,16},{8,28},{12,24},{16,4},{20,0},{24,12},{28,8},{1,21},{... | collective-permute-start | bytes 589832 | tf_op jit(solution)/shard_map/ppermute | solution.py:308
  145.0 17.7 %collective-permute-start.28 = (bf16[1,2,96,512]{3,2,1,0:T(8,128)(2,1)}, bf16[1,2,96,512]{3,2,1,0:T(8,128)(2,1)}, u32[]{:S(2)}, u32[]{:S(2)}) collective-permute-start(bf16[1,2,96,512]{3,2,1,0:T(8,128)(2,1)} %get-tuple-element.107), channel_id=1, source_target_pairs={{0,24},{4,28},{8,16},{12,20},{16,8},{20,12},{24,0},{28,4},{1,25},{... | collective-permute-start | bytes 589832 | tf_op jit(solution)/shard_map/ppermute | solution.py:308
  147.2 16.4 %collective-permute-start.29 = (bf16[1,2,96,512]{3,2,1,0:T(8,128)(2,1)}, bf16[1,2,96,512]{3,2,1,0:T(8,128)(2,1)}, u32[]{:S(2)}, u32[]{:S(2)}) collective-permute-start(bf16[1,2,96,512]{3,2,1,0:T(8,128)(2,1)} %get-tuple-element.108), channel_id=1, source_target_pairs={{0,28},{4,24},{8,20},{12,16},{16,12},{20,8},{24,4},{28,0},{1,29},{... | collective-permute-start | bytes 589832 | tf_op jit(solution)/shard_map/ppermute | solution.py:308
  149.0 15.2 %collective-permute-start.16 = (bf16[1,2,96,512]{3,2,1,0:T(8,128)(2,1)}, bf16[1,2,96,512]{3,2,1,0:T(8,128)(2,1)}, u32[]{:S(2)}, u32[]{:S(2)}) collective-permute-start(bf16[1,2,96,512]{3,2,1,0:T(8,128)(2,1)} %get-tuple-element.94), channel_id=1, source_target_pairs={{0,4},{4,0},{8,12},{12,8},{16,20},{20,16},{24,28},{28,24},{1,5},{5... | collective-permute-start | bytes 589832 | tf_op jit(solution)/shard_map/ppermute | solution.py:308
  158.4 18.0 %collective-permute-start.17 = (bf16[1,2,96,512]{3,2,1,0:T(8,128)(2,1)}, bf16[1,2,96,512]{3,2,1,0:T(8,128)(2,1)S(1)}, u32[]{:S(2)}, u32[]{:S(2)}) collective-permute-start(bf16[1,2,96,512]{3,2,1,0:T(8,128)(2,1)} %copy-done.89), channel_id=1, source_target_pairs={{0,8},{4,12},{8,0},{12,4},{16,24},{20,28},{24,16},{28,20},{1,9},{5... | collective-permute-start | bytes 589832 | tf_op jit(solution)/shard_map/ppermute | solution.py:308
  161.4 16.5 %collective-permute-start.18 = (bf16[1,2,96,512]{3,2,1,0:T(8,128)(2,1)}, bf16[1,2,96,512]{3,2,1,0:T(8,128)(2,1)S(1)}, u32[]{:S(2)}, u32[]{:S(2)}) collective-permute-start(bf16[1,2,96,512]{3,2,1,0:T(8,128)(2,1)} %copy-done.88), channel_id=1, source_target_pairs={{0,12},{4,8},{8,4},{12,0},{16,28},{20,24},{24,20},{28,16},{1,13},{... | collective-permute-start | bytes 589832 | tf_op jit(solution)/shard_map/ppermute | solution.py:308
  162.7 15.9 %collective-permute-start.19 = (bf16[1,2,96,512]{3,2,1,0:T(8,128)(2,1)}, bf16[1,2,96,512]{3,2,1,0:T(8,128)(2,1)S(1)}, u32[]{:S(2)}, u32[]{:S(2)}) collective-permute-start(bf16[1,2,96,512]{3,2,1,0:T(8,128)(2,1)} %copy-done.87), channel_id=1, source_target_pairs={{0,16},{4,20},{8,24},{12,28},{16,0},{20,4},{24,8},{28,12},{1,17},{... | collective-permute-start | bytes 589832 | tf_op jit(solution)/shard_map/ppermute | solution.py:308
  163.6 15.9 %collective-permute-start.20 = (bf16[1,2,96,512]{3,2,1,0:T(8,128)(2,1)}, bf16[1,2,96,512]{3,2,1,0:T(8,128)(2,1)S(1)}, u32[]{:S(2)}, u32[]{:S(2)}) collective-permute-start(bf16[1,2,96,512]{3,2,1,0:T(8,128)(2,1)} %copy-done.86), channel_id=1, source_target_pairs={{0,20},{4,16},{8,28},{12,24},{16,4},{20,0},{24,12},{28,8},{1,21},{... | collective-permute-start | bytes 589832 | tf_op jit(solution)/shard_map/ppermute | solution.py:308
  164.2 16.0 %collective-permute-start.21 = (bf16[1,2,96,512]{3,2,1,0:T(8,128)(2,1)}, bf16[1,2,96,512]{3,2,1,0:T(8,128)(2,1)S(1)}, u32[]{:S(2)}, u32[]{:S(2)}) collective-permute-start(bf16[1,2,96,512]{3,2,1,0:T(8,128)(2,1)} %copy-done.85), channel_id=1, source_target_pairs={{0,24},{4,28},{8,16},{12,20},{16,8},{20,12},{24,0},{28,4},{1,25},{... | collective-permute-start | bytes 589832 | tf_op jit(solution)/shard_map/ppermute | solution.py:308
  202.8 19.6 %collective-permute-start.6 = (bf16[1,2,96,512]{3,2,1,0:T(8,128)(2,1)S(1)}, bf16[1,2,96,512]{3,2,1,0:T(8,128)(2,1)S(1)}, u32[]{:S(2)}, u32[]{:S(2)}) collective-permute-start(bf16[1,2,96,512]{3,2,1,0:T(8,128)(2,1)S(1)} %get-tuple-element.82), channel_id=1, source_target_pairs={{0,20},{4,16},{8,28},{12,24},{16,4},{20,0},{24,12},{28,8},{1,21},{... | collective-permute-start | bytes 589832 | tf_op jit(solution)/shard_map/ppermute | solution.py:308
  204.9 17.5 %collective-permute-start.7 = (bf16[1,2,96,512]{3,2,1,0:T(8,128)(2,1)S(1)}, bf16[1,2,96,512]{3,2,1,0:T(8,128)(2,1)S(1)}, u32[]{:S(2)}, u32[]{:S(2)}) collective-permute-start(bf16[1,2,96,512]{3,2,1,0:T(8,128)(2,1)S(1)} %get-tuple-element.83), channel_id=1, source_target_pairs={{0,24},{4,28},{8,16},{12,20},{16,8},{20,12},{24,0},{28,4},{1,25},{... | collective-permute-start | bytes 589832 | tf_op jit(solution)/shard_map/ppermute | solution.py:308
  (118 other events, 1468.2 us)
where the time goes:
time: 225 us; the launch traced here: 224 us
  Pallas kernels  92.7 us (41%)
  starting transfers between devices  58.9 us (26%)
  waiting for transfers between devices  39.9 us (18%)
  local copies, waits for them, and re-layouts  19.5 us (9%)
  blocking collectives  9.97 us (4%)
    pallas_call x8, Pallas kernels, shards(): pl.pallas_call(functools.partial(rows_kernel, total, nch, chan0), grid_sp...  59.7 us
    ppermute x56, starting transfers between devices, shards(): got[j] = lax.ppermute(w[j], 'facet', [(s, s ^ j) for s in range(nf)])  53.1 us
    ppermute x56, waiting for transfers between devices, shards(): got[j] = lax.ppermute(w[j], 'facet', [(s, s ^ j) for s in range(nf)])  36.8 us
    unnamed x185, local copies, waits for them, and re-layouts  19.5 us
    pallas_call x8, Pallas kernels, shards(): pl.pallas_call(functools.partial(pixels_kernel, nf, 1.0 / (frame * frame)...  17.8 us
    all_gather x1, blocking collectives, shards(): fit = lax.all_gather(fit, 'facet', axis=0)  9.97 us
    pallas_call x1, Pallas kernels, shards(): pl.pallas_call(functools.partial(phases_kernel, frame, fs), out_shape=[ja...  8.22 us
    ppermute x2, starting transfers between devices, shards(): other = lax.ppermute(sums, 'freq', [(s, s ^ 1 << i) for s in range(nz)])  5.81 us
  transfers between devices with their start and end apart: 58, of which 9 were waited for; matrix products, arithmetic and copies ran while one was open for 0% of the time, Pallas kernels for 36%

commit v1 on v0

--- a/solution.py
+++ b/solution.py
@@ -9,7 +9,8 @@
 from jax.sharding import PartitionSpec as P
 
 FCOLS = 4
-VMEM_LIMIT = 40 * 1024 * 1024
+VMEM_LIMIT = 20 * 1024 * 1024
+SMALL_LIMIT = 12 * 1024 * 1024
 
 bf16, f32, i32 = jnp.bfloat16, jnp.float32, jnp.int32
 
@@ -80,12 +81,12 @@
     return lax.broadcasted_iota(i32, shape, axis)
 
 
-def phases_kernel(frame, fs, pos_ref, row_ref, col_ref, inv_ref, flip_ref):
+def row_phases_kernel(frame, fs, pos_ref, row_ref, inv_ref, flip_ref):
     na, ntile, two_kb, ts = row_ref.shape
     kb = two_kb // 2
     half, quarter, pad = frame // 2, frame // 4, (frame - fs) // 2
     me = lax.axis_index("facet")
-    a_me, b_me = lax.div(me, FCOLS), lax.rem(me, FCOLS)
+    a_me = lax.div(me, FCOLS)
     pixel = lane((1, ts), 1)
     own = (me * kb + lane((kb, 1), 0)).astype(f32)
     for a in range(na):
@@ -95,20 +96,6 @@
             index = own * (oy + pixel).astype(f32)
             row_ref[a, t, :kb] = (cos_turn(index, frame) * ok).astype(bf16)
             row_ref[a, t, kb:] = (cos_turn(index + quarter, frame) * ok).astype(bf16)
-    spot = lane((1, 2 * half), 1)
-    freq = jnp.where(spot > half, spot - half, spot).astype(f32)
-    shift = jnp.where(spot > half, quarter, 0).astype(f32)
-    down = lane((ts, 1), 0)
-
-    def columns(i, carry):
-        b, t = lax.div(i, ntile), lax.rem(i, ntile)
-        ox = pos_ref[t, 1] - jnp.bitwise_xor(b_me, b) * fs + pad
-        ok = jnp.where((ox >= 0) & (ox <= frame - ts), 1.0, 0.0).astype(f32)
-        index = (ox + down).astype(f32) * freq + shift
-        col_ref[i] = (cos_turn(index, frame) * ok).astype(bf16)
-        return carry
-
-    lax.fori_loop(0, FCOLS * ntile, columns, 0)
     place = (pad + lane((1, fs), 1)).astype(f32)
     block = half // 4
 
@@ -122,6 +109,29 @@
     lax.fori_loop(0, 8, inverse, 0)
     source = lax.rem(half - lane((1, half), 1), half)
     flip_ref[...] = jnp.where(lane((half, half), 0) == source, 1.0, 0.0).astype(bf16)
+
+
+def column_phases_kernel(frame, fs, pos_ref, col_ref, cos_ref, sin_ref):
+    ntile, ts = pos_ref.shape[0], col_ref.shape[1]
+    half, quarter, pad = frame // 2, frame // 4, (frame - fs) // 2
+    b_me = lax.rem(lax.axis_index("facet"), FCOLS)
+    spot = lane((1, 2 * half), 1)
+    freq = jnp.where(spot > half, spot - half, spot).astype(f32)
+    shift = jnp.where(spot > half, quarter, 0).astype(f32)
+    grain = lane((ts, 1), 0).astype(f32) * freq
+    cos_ref[...] = cos_turn(grain, frame)
+    sin_ref[...] = cos_turn(grain - quarter, frame)
+
+    def columns(i, carry):
+        b, t = lax.div(i, ntile), lax.rem(i, ntile)
+        ox = pos_ref[t, 1] - jnp.bitwise_xor(b_me, b) * fs + pad
+        ok = jnp.where((ox >= 0) & (ox <= frame - ts), 1.0, 0.0).astype(f32)
+        index = ox.astype(f32) * freq + shift
+        cos_ox, sin_ox = cos_turn(index, frame) * ok, cos_turn(index - quarter, frame) * ok
+        col_ref[i] = (cos_ox * cos_ref[...] - sin_ox * sin_ref[...]).astype(bf16)
+        return carry
+
+    lax.fori_loop(0, FCOLS * ntile, columns, 0)
 
 
 def pixel_phases_kernel(frame, pad, nf, out_ref):
@@ -146,7 +156,7 @@
     lax.fori_loop(0, out_ref.shape[0] // block, some, 0)
 
 
-def rows_kernel(total, nch, chan0, psf_of_ref, coef_ref, row_ref, col_ref, inv_ref, flip_ref, psf_ref, *rest):
+def rows_kernel(total, nch, chan0, b0, psf_of_ref, coef_ref, row_ref, col_ref, inv_ref, flip_ref, psf_ref, *rest):
     out_refs, (lhs_ref, rev_ref, q_ref) = rest[:-3], rest[-3:]
     na, ntile, _, ts = row_ref.shape
     nf = coef_ref.shape[0]
@@ -176,7 +186,7 @@
     first = lane((1, half), 1) == 0
     zero = jnp.zeros((kb, half), f32)
     for a in range(na):
-        psf = psf_of_ref[jnp.bitwise_xor(me, a * FCOLS + step)]
+        psf = psf_of_ref[jnp.bitwise_xor(me, a * FCOLS + b0 + step)]
         top = slice(a * 2 * kb, a * 2 * kb + kb)
         low = slice(a * 2 * kb + kb, (a + 1) * 2 * kb)
         rc, rs = both[top, :half], both[top, half:]
@@ -193,14 +203,15 @@
         q_ref[low, :half] = (q_im + jnp.where(first, zero, z_im)).astype(bf16)
         q_ref[low, half:] = jnp.where(first, z_im, q_re - z_re).astype(bf16)
     w = jnp.dot(q_ref[...], inv_ref[...], preferred_element_type=f32).astype(bf16)
-    for b in range(FCOLS):
+    width = len(out_refs) // na
+    for b in range(width):
 
         @pl.when(step == b)
         def _():
             for a in range(na):
                 for p in range(2):
                     start = (2 * a + p) * kb
-                    out_refs[a * FCOLS + b][0, p] = w[start : start + kb]
+                    out_refs[a * width + b][0, p] = w[start : start + kb]
 
 
 def pixels_kernel(nf, scale, *refs):
@@ -211,18 +222,27 @@
 
 
 def chunks_of(nch):
-    return [(c, 1) for c in range(nch)]
-
-
-def send_order(nf):
-    return sorted(range(1, nf), key=lambda j: (-bin(j >> 1).count("1"), j))
+    sizes, left = [], nch
+    while left:
+        sizes.append(2 if len(sizes) >= 2 and left > 3 else 1)
+        left -= sizes[-1]
+    return [(sum(sizes[:i]), n, [(0, FCOLS)]) for i, n in enumerate(sizes)]
+
+
+def send_order(members):
+    return sorted((j for j in members if j), key=lambda j: (-bin(j >> 1).count("1"), j))
 
 
 VMEM = pl.BlockSpec(memory_space=pltpu.VMEM)
 SMEM = pl.BlockSpec(memory_space=pltpu.SMEM)
 
 
+def in_hbm(x):
+    return pltpu.with_memory_space_constraint(x, pltpu.HBM)
+
+
 def shards(nf, nz, residual, components, chan_weight, tile_pos, facet_psf, psf_spectra):
+    residual, psf_spectra = in_hbm(residual), in_hbm(psf_spectra)
     ntile, nch, rows, ts = components.shape
     npsf, _, _, kb, frame = psf_spectra.shape
     fs = residual.shape[2]
@@ -237,19 +257,28 @@
         out_specs=VMEM,
         name="moments",
     )(chan_weight, components)
-    row_table, col_table, inv_table, flip = pl.pallas_call(
-        functools.partial(phases_kernel, frame, fs),
+    row_table, inv_table, flip = pl.pallas_call(
+        functools.partial(row_phases_kernel, frame, fs),
         out_shape=[
             jax.ShapeDtypeStruct((na, ntile, 2 * kb, ts), bf16),
-            jax.ShapeDtypeStruct((FCOLS * ntile, ts, frame), bf16),
             jax.ShapeDtypeStruct((frame, fs), bf16),
             jax.ShapeDtypeStruct((half, half), bf16),
         ],
         in_specs=[SMEM],
-        out_specs=[VMEM] * 4,
-        compiler_params=pltpu.CompilerParams(vmem_limit_bytes=VMEM_LIMIT),
-        name="phases",
+        out_specs=[VMEM] * 3,
+        compiler_params=pltpu.CompilerParams(vmem_limit_bytes=SMALL_LIMIT),
+        name="rowphases",
     )(tile_pos)
+    col_table = pl.pallas_call(
+        functools.partial(column_phases_kernel, frame, fs),
+        out_shape=jax.ShapeDtypeStruct((FCOLS * ntile, ts, frame), bf16),
+        in_specs=[SMEM],
+        out_specs=VMEM,
+        scratch_shapes=[pltpu.VMEM((ts, frame), f32)] * 2,
+        compiler_params=pltpu.CompilerParams(vmem_limit_bytes=SMALL_LIMIT),
+        name="colphases",
+    )(tile_pos)
+    row_table, inv_table, flip = in_hbm(row_table), in_hbm(inv_table), in_hbm(flip)
     col_table = col_table.reshape(FCOLS, ntile * ts, frame)
     other = jnp.zeros_like(sums)
     for i in range(nz.bit_length() - 1):
@@ -273,39 +302,44 @@
     )()
 
     pieces = []
-    for chan0, count in chunks_of(nch):
-        w = pl.pallas_call(
-            functools.partial(rows_kernel, total, nch, chan0),
-            grid_spec=pltpu.PrefetchScalarGridSpec(
-                num_scalar_prefetch=1,
-                grid=(count, FCOLS),
-                in_specs=[
-                    pl.BlockSpec((nf, 3 * ntile + 1, rows, ts), lambda c, b, s: (0, 0, 0, 0)),
-                    pl.BlockSpec((na, ntile, 2 * kb, ts), lambda c, b, s: (0, 0, 0, 0)),
-                    pl.BlockSpec((1, ntile * ts, frame), lambda c, b, s: (b, 0, 0)),
-                    pl.BlockSpec((frame, fs), lambda c, b, s: (0, 0)),
-                    pl.BlockSpec((half, half), lambda c, b, s: (0, 0)),
-                    pl.BlockSpec((npsf, 1, 2, kb, frame), lambda c, b, s, c0=chan0: (0, c0 + c, 0, 0, 0)),
-                ],
-                out_specs=[pl.BlockSpec((1, 2, kb, fs), lambda c, b, s: (c, 0, 0, 0))] * nf,
-                scratch_shapes=[
-                    pltpu.VMEM((na * 2 * kb, ntile * ts), bf16),
-                    pltpu.VMEM((npsf, 2, kb, half), bf16),
-                    pltpu.VMEM((na * 2 * kb, frame), bf16),
-                ],
-            ),
-            out_shape=[jax.ShapeDtypeStruct((count, 2, kb, fs), bf16)] * nf,
-            cost_estimate=pl.CostEstimate(
-                flops=count * nf * 4 * kb * frame * (ntile * ts + fs),
-                bytes_accessed=count * (npsf * 4 * kb * frame + nf * 4 * kb * fs) + 8 * ntile * ts * frame,
-                transcendentals=0,
-            ),
-            compiler_params=pltpu.CompilerParams(vmem_limit_bytes=VMEM_LIMIT),
-            name="rows",
-        )(psf_of, fit, row_table, col_table, inv_table, flip, psf_spectra)
-        got = [w[0]] + [None] * (nf - 1)
-        for j in send_order(nf):
-            got[j] = lax.ppermute(w[j], "facet", [(s, s ^ j) for s in range(nf)])
+    for chan0, count, groups in chunks_of(nch):
+        got = [None] * nf
+        for b0, width in groups:
+            members = [a * FCOLS + b0 + b for a in range(na) for b in range(width)]
+            w = pl.pallas_call(
+                functools.partial(rows_kernel, total, nch, chan0, b0),
+                grid_spec=pltpu.PrefetchScalarGridSpec(
+                    num_scalar_prefetch=1,
+                    grid=(count, width),
+                    in_specs=[
+                        pl.BlockSpec((nf, 3 * ntile + 1, rows, ts), lambda c, b, s: (0, 0, 0, 0)),
+                        pl.BlockSpec((na, ntile, 2 * kb, ts), lambda c, b, s: (0, 0, 0, 0)),
+                        pl.BlockSpec((1, ntile * ts, frame), lambda c, b, s, b0=b0: (b0 + b, 0, 0)),
+                        pl.BlockSpec((frame, fs), lambda c, b, s: (0, 0)),
+                        pl.BlockSpec((half, half), lambda c, b, s: (0, 0)),
+                        pl.BlockSpec((npsf, 1, 2, kb, frame), lambda c, b, s, c0=chan0: (0, c0 + c, 0, 0, 0)),
+                    ],
+                    out_specs=[pl.BlockSpec((1, 2, kb, fs), lambda c, b, s: (c, 0, 0, 0))] * (na * width),
+                    scratch_shapes=[
+                        pltpu.VMEM((na * 2 * kb, ntile * ts), bf16),
+                        pltpu.VMEM((npsf, 2, kb, half), bf16),
+                        pltpu.VMEM((na * 2 * kb, frame), bf16),
+                    ],
+                ),
+                out_shape=[jax.ShapeDtypeStruct((count, 2, kb, fs), bf16)] * (na * width),
+                cost_estimate=pl.CostEstimate(
+                    flops=count * na * width * 4 * kb * frame * (ntile * ts + fs),
+                    bytes_accessed=count * (npsf * 4 * kb * frame + na * width * 4 * kb * fs)
+                    + 2 * width * ntile * ts * frame,
+                    transcendentals=0,
+                ),
+                compiler_params=pltpu.CompilerParams(vmem_limit_bytes=VMEM_LIMIT),
+                name="rows",
+            )(psf_of, fit, row_table, col_table, inv_table, flip, psf_spectra)
+            for i, j in enumerate(members):
+                got[j] = w[i]
+            for j in send_order(members):
+                got[j] = lax.ppermute(got[j], "facet", [(s, s ^ j) for s in range(nf)])
         pieces.append((chan0, count, got))
     result = None
     for chan0, count, got in pieces:

time: 225 us -> 221 us (0.982)
  starting transfers between devices: 58.9 us -> 45.5 us
  local copies, waits for them, and re-layouts: 19.5 us -> 25.4 us
  waiting for transfers between devices: 39.9 us -> 44.9 us
    ppermute x56 -> x42, starting transfers between devices: 53.1 us -> 39.6 us  [shards(): got[j] = lax.ppermute(got[j], 'facet', [(s, s ^ j) for s in range(nf)])]
    unnamed x185 -> x167, local copies, waits for them, and re-layouts: 19.5 us -> 25.4 us
    ppermute x56 -> x42, waiting for transfers between devices: 36.8 us -> 41.7 us  [shards(): got[j] = lax.ppermute(got[j], 'facet', [(s, s ^ j) for s in range(nf)])]
    pallas_call x9 -> x8, Pallas kernels: 68 us -> 63.2 us  [the longest x6 57.8 us: shards(): pl.pallas_call(functools.partial(rows_kernel, total, nch, chan0, b0), gri...]
    pallas_call x8 -> x6, Pallas kernels: 17.8 us -> 21.8 us  [shards(): pl.pallas_call(functools.partial(pixels_kernel, nf, 1.0 / (frame * frame)...]
  transfers between devices with their start and end apart: 58 -> 44, of which waited for: 9 -> 8; matrix products, arithmetic and copies ran while one was open for 0% -> 0% of each run, Pallas kernels for 36% -> 35%
where the time goes in v1:
time: 221 us; the launch traced here: 220 us
  Pallas kernels  92 us (42%)
  starting transfers between devices  45.5 us (21%)
  waiting for transfers between devices  44.9 us (20%)
  local copies, waits for them, and re-layouts  25.4 us (11%)
  blocking collectives  9.97 us (5%)
    pallas_call x6, Pallas kernels, shards(): pl.pallas_call(functools.partial(rows_kernel, total, nch, chan0, b0), gri...  57.8 us
    ppermute x42, waiting for transfers between devices, shards(): got[j] = lax.ppermute(got[j], 'facet', [(s, s ^ j) for s in range(nf)])  41.7 us
    ppermute x42, starting transfers between devices, shards(): got[j] = lax.ppermute(got[j], 'facet', [(s, s ^ j) for s in range(nf)])  39.6 us
    unnamed x167, local copies, waits for them, and re-layouts  25.4 us
    pallas_call x6, Pallas kernels, shards(): pl.pallas_call(functools.partial(pixels_kernel, nf, 1.0 / (frame * frame)...  21.8 us
    all_gather x1, blocking collectives, shards(): fit = lax.all_gather(fit, 'facet', axis=0)  9.97 us
    ppermute x2, starting transfers between devices, shards(): other = lax.ppermute(sums, 'freq', [(s, s ^ 1 << i) for s in range(nz)])  5.87 us
  transfers between devices with their start and end apart: 44, of which 8 were waited for; matrix products, arithmetic and copies ran while one was open for 0% of the time, Pallas kernels for 35%

profile of v1, /device:TPU:0, one launch (start us, length us, event | category | flops | bytes accessed | tf_op | source)
XLA Modules:
  0.0 220.2 jit_solution(16783365024532478066)
XLA Ops:
  0.0 1.6 moments.1
  1.6 3.1 %collective-permute-start = (f32[13,16,128]{2,1,0:T(8,128)}, f32[13,16,128]{2,1,0:T(8,128)S(1)}, u32[]{:S(2)}, u32[]{:S(2)}) collective-permute-start(f32[13,16,128]{2,1,0:T(8,128)} %moments.1), channel_id=1, source_target_pairs={{0,1},{1,0},{2,3},{3,2},{4,5},{5,4},{6,7},{7,6},{8,9},{9,8},{10,11... | collective-permute-start | bytes 319496 | tf_op jit(solution)/shard_map/ppermute | solution.py:287
  4.7 3.2 %collective-permute-done = f32[13,16,128]{2,1,0:T(8,128)S(1)} collective-permute-done((f32[13,16,128]{2,1,0:T(8,128)}, f32[13,16,128]{2,1,0:T(8,128)S(1)}, u32[]{:S(2)}, u32[]{:S(2)}) %collective-permute-start) | collective-permute-done | bytes 106528 | tf_op jit(solution)/shard_map/ppermute | solution.py:287
  8.8 2.8 %collective-permute-start.1 = (f32[13,16,128]{2,1,0:T(8,128)S(1)}, f32[13,16,128]{2,1,0:T(8,128)S(1)}, u32[]{:S(2)}, u32[]{:S(2)}) collective-permute-start(f32[13,16,128]{2,1,0:T(8,128)S(1)} %add.3.one_ref), channel_id=1, source_target_pairs={{0,2},{1,3},{2,0},{3,1},{4,6},{5,7},{6,4},{7,5},{8,10},{9,11},{10,... | collective-permute-start | bytes 319496 | tf_op jit(solution)/shard_map/ppermute | solution.py:287
  12.4 2.7 %rowphases.1 = (bf16[2,4,192,128]{3,2,1,0:T(8,128)(2,1)S(1)}, bf16[768,512]{1,0:T(8,128)(2,1)S(1)}, bf16[384,384]{1,0:T(8,128)(2,1)S(1)}) custom-call(s32[4,2]{1,0:T(4,128)S(1)} %copy.16.pos_ref), custom_call_target="tpu_custom_call" | custom-call | tf_op jit(solution)/shard_map/rowphases/pallas_call | solution.py:260
  17.4 2.7 %colphases.1 = bf16[16,128,768]{2,1,0:T(8,128)(2,1)S(1)} custom-call(s32[4,2]{1,0:T(4,128)S(1)} %copy.16.pos_ref), custom_call_target="tpu_custom_call" | custom-call | tf_op jit(solution)/shard_map/colphases/pallas_call | solution.py:272
  21.4 1.6 solve.1
  23.0 10.0 %all-gather = bf16[104,16,128]{2,1,0:T(8,128)(2,1)S(1)} all-gather(bf16[13,16,128]{2,1,0:T(8,128)(2,1)} %solve.1), channel_id=2, replica_groups=mesh['facet'=8,'freq'=4] {'facet'}, dimensions={0}, use_global_device_ids=true | all-gather | bytes 479232 | tf_op jit(solution)/shard_map/all_gather | solution.py:295
  33.2 7.6 %rows.11 = (bf16[1,2,96,512]{3,2,1,0:T(8,128)(2,1)S(1)}, bf16[1,2,96,512]{3,2,1,0:T(8,128)(2,1)S(1)}, bf16[1,2,96,512]{3,2,1,0:T(8,128)(2,1)S(1)}, bf16[1,2,96,5...) custom-call(s32[8]{0:T(128)S(1)} %fusion.psf_of_ref, ...), custom_call_target="tpu_custom_call" | custom-call | flops 2415919104 | bytes 5898240 | tf_op jit(solution)/shard_map/rows/pallas_call | solution.py:309
  46.2 2.9 %collective-permute-done.38.refs_2_ = bf16[1,2,96,512]{3,2,1,0:T(8,128)(2,1)S(1)} collective-permute-done((bf16[1,2,96,512]{3,2,1,0:T(8,128)(2,1)S(1)}, bf16[1,2,96,512]{3,2,1,0:T(8,128)(2,1)S(1)}, u32[]{:S(2)}, u32[]{:S(2)}) %collective-permute-start.38) | collective-permute-done | bytes 196640 | tf_op jit(solution)/shard_map/ppermute | solution.py:342
  49.0 7.6 %rows.10 = (bf16[1,2,96,512]{3,2,1,0:T(8,128)(2,1)S(1)}, bf16[1,2,96,512]{3,2,1,0:T(8,128)(2,1)S(1)}, bf16[1,2,96,512]{3,2,1,0:T(8,128)(2,1)S(1)}, bf16[1,2,96,5...) custom-call(s32[8]{0:T(128)S(1)} %fusion.psf_of_ref, ...), custom_call_target="tpu_custom_call" | custom-call | flops 2415919104 | bytes 5898240 | tf_op jit(solution)/shard_map/rows/pallas_call | solution.py:309
  57.3 1.5 collective-permute-start.30
  60.1 2.4 %collective-permute-done.41.refs_5_ = bf16[1,2,96,512]{3,2,1,0:T(8,128)(2,1)S(1)} collective-permute-done((bf16[1,2,96,512]{3,2,1,0:T(8,128)(2,1)S(1)}, bf16[1,2,96,512]{3,2,1,0:T(8,128)(2,1)S(1)}, u32[]{:S(2)}, u32[]{:S(2)}) %collective-permute-start.41) | collective-permute-done | bytes 196640 | tf_op jit(solution)/shard_map/ppermute | solution.py:342
  65.2 7.6 %rows.7 = (bf16[1,2,96,512]{3,2,1,0:T(8,128)(2,1)S(1)}, bf16[1,2,96,512]{3,2,1,0:T(8,128)(2,1)S(1)}, bf16[1,2,96,512]{3,2,1,0:T(8,128)(2,1)S(1)}, bf16[1,2,96,51...) custom-call(s32[8]{0:T(128)S(1)} %fusion.psf_of_ref, ...), custom_call_target="tpu_custom_call" | custom-call | flops 2415919104 | bytes 5898240 | tf_op jit(solution)/shard_map/rows/pallas_call | solution.py:309
  75.0 1.5 collective-permute-start.36
  78.7 7.6 %rows.6 = (bf16[1,2,96,512]{3,2,1,0:T(8,128)(2,1)S(1)}, bf16[1,2,96,512]{3,2,1,0:T(8,128)(2,1)S(1)}, bf16[1,2,96,512]{3,2,1,0:T(8,128)(2,1)S(1)}, bf16[1,2,96,51...) custom-call(s32[8]{0:T(128)S(1)} %fusion.psf_of_ref, ...), custom_call_target="tpu_custom_call" | custom-call | flops 2415919104 | bytes 5898240 | tf_op jit(solution)/shard_map/rows/pallas_call | solution.py:309
  96.3 13.0 %rows.9 = (bf16[2,2,96,512]{3,2,1,0:T(8,128)(2,1)S(1)}, bf16[2,2,96,512]{3,2,1,0:T(8,128)(2,1)S(1)}, bf16[2,2,96,512]{3,2,1,0:T(8,128)(2,1)S(1)}, bf16[2,2,96,51...) custom-call(s32[8]{0:T(128)S(1)} %fusion.psf_of_ref, ...), custom_call_target="tpu_custom_call" | custom-call | flops 4831838208 | bytes 8650752 | tf_op jit(solution)/shard_map/rows/pallas_call | solution.py:309
  114.8 14.4 %rows.8 = (bf16[2,2,96,512]{3,2,1,0:T(8,128)(2,1)S(1)}, bf16[2,2,96,512]{3,2,1,0:T(8,128)(2,1)S(1)}, bf16[2,2,96,512]{3,2,1,0:T(8,128)(2,1)S(1)}, bf16[2,2,96,51...) custom-call(s32[8]{0:T(128)S(1)} %fusion.psf_of_ref, ...), custom_call_target="tpu_custom_call" | custom-call | flops 4831838208 | bytes 8650752 | tf_op jit(solution)/shard_map/rows/pallas_call | solution.py:309
  129.2 5.1 %collective-permute-done.3.refs_2_ = bf16[1,2,96,512]{3,2,1,0:T(8,128)(2,1)S(1)} collective-permute-done((bf16[1,2,96,512]{3,2,1,0:T(8,128)(2,1)S(1)}, bf16[1,2,96,512]{3,2,1,0:T(8,128)(2,1)S(1)}, u32[]{:S(2)}, u32[]{:S(2)}) %collective-permute-start.3) | collective-permute-done | bytes 196640 | tf_op jit(solution)/shard_map/ppermute | solution.py:342
  138.0 1.7 collective-permute-start.29
  142.5 20.2 %collective-permute-done.27.refs_5_ = bf16[2,2,96,512]{3,2,1,0:T(8,128)(2,1)S(1)} collective-permute-done((bf16[2,2,96,512]{3,2,1,0:T(8,128)(2,1)S(1)}, bf16[2,2,96,512]{3,2,1,0:T(8,128)(2,1)S(1)}, u32[]{:S(2)}, u32[]{:S(2)}) %collective-permute-start.27) | collective-permute-done | bytes 393248 | tf_op jit(solution)/shard_map/ppermute | solution.py:342
  168.6 3.7 %pixphases.1.refs_8_ = bf16[512,1536]{1,0:T(8,128)(2,1)} custom-call(), custom_call_target="tpu_custom_call" | custom-call | tf_op jit(solution)/shard_map/pixphases/pallas_call | solution.py:297
  181.2 3.3 %pixels.6.refs_10_ = f32[8,1,512,512]{3,2,1,0:T(8,128)} custom-call(bf16[1,2,96,512]{3,2,1,0:T(8,128)(2,1)S(1)} %copy-done.18, bf16[1,2,96,512]{3,2,1,0:T(8,128)(2,1)S(1)} %copy-done.20, bf16[1,2,96,512]{3,2,1,0:T(8,128)(2,1)S(1)} %copy-done.22, bf16[1,2,96,512]{3,2,1,0:T(8,128)(2,1)S(1)} %copy-done.24, bf16[1,2,96,512]{3,2,1,0:T(8,128)(2,1)S(1)} %copy-done.28, ...), custom_call_target="tpu_custom_call" | custom-call | flops 805306368 | bytes 3670016 | tf_op jit(solution)/shard_map/pixels/pallas_call | solution.py:348
  184.6 3.3 %pixels.7.refs_10_ = f32[8,1,512,512]{3,2,1,0:T(8,128)} custom-call(bf16[1,2,96,512]{3,2,1,0:T(8,128)(2,1)S(1)} %copy-done.40, bf16[1,2,96,512]{3,2,1,0:T(8,128)(2,1)S(1)} %copy-done.44, bf16[1,2,96,512]{3,2,1,0:T(8,128)(2,1)S(1)} %copy-done.48, bf16[1,2,96,512]{3,2,1,0:T(8,128)(2,1)S(1)} %copy-done.50, ...), custom_call_target="tpu_custom_call", output_to_operand_aliasing={{}: (10, {})} | custom-call | flops 805306368 | bytes 3670016 | tf_op jit(solution)/shard_map/pixels/pallas_call | solution.py:348
  188.0 4.3 %pixels.8.refs_10_ = f32[8,1,512,512]{3,2,1,0:T(8,128)} custom-call(bf16[2,2,96,512]{3,2,1,0:T(8,128)(2,1)S(1)} %copy-done.6, bf16[2,2,96,512]{3,2,1,0:T(8,128)(2,1)S(1)} %copy-done.8, bf16[2,2,96,512]{3,2,1,0:T(8,128)(2,1)S(1)} %copy-done.10, bf16[2,2,96,512]{3,2,1,0:T(8,128)(2,1)S(1)} %copy-done.12, ...), custom_call_target="tpu_custom_call", output_to_operand_aliasing={{}: (10, {})} | custom-call | flops 1610612736 | bytes 7340032 | tf_op jit(solution)/shard_map/pixels/pallas_call | solution.py:348
  194.6 5.6 %collective-permute-done.20.refs_5_ = bf16[2,2,96,512]{3,2,1,0:T(8,128)(2,1)S(1)} collective-permute-done((bf16[2,2,96,512]{3,2,1,0:T(8,128)(2,1)}, bf16[2,2,96,512]{3,2,1,0:T(8,128)(2,1)S(1)}, u32[]{:S(2)}, u32[]{:S(2)}) %collective-permute-start.20) | collective-permute-done | bytes 393248 | tf_op jit(solution)/shard_map/ppermute | solution.py:342
  201.0 1.5 collective-permute-start.7
  203.7 4.4 %pixels.9.refs_10_ = f32[8,1,512,512]{3,2,1,0:T(8,128)} custom-call(bf16[2,2,96,512]{3,2,1,0:T(8,128)(2,1)S(1)} %get-tuple-element.75.refs_0_, bf16[2,2,96,512]{3,2,1,0:T(8,128)(2,1)S(1)} %collective-permute-done.16.refs_1_, bf16[2,2,96,512]{3,2,1,0:T(8,128)(2,1)S(1)} %collective-permute-done.17.refs_2_, ...), custom_call_target="tpu_custom_call", output_to_operand_aliasing={{}: (10, {})} | custom-call | flops 1610612736 | bytes 7340032 | tf_op jit(solution)/shard_map/pixels/pallas_call | solution.py:348
  208.2 3.3 %pixels.10.refs_10_ = f32[8,1,512,512]{3,2,1,0:T(8,128)} custom-call(bf16[1,2,96,512]{3,2,1,0:T(8,128)(2,1)S(1)} %copy-done.26, bf16[1,2,96,512]{3,2,1,0:T(8,128)(2,1)S(1)} %copy-done.64, bf16[1,2,96,512]{3,2,1,0:T(8,128)(2,1)S(1)} %copy-done.38, bf16[1,2,96,512]{3,2,1,0:T(8,128)(2,1)S(1)} %copy-done.42, ...), custom_call_target="tpu_custom_call", output_to_operand_aliasing={{}: (10, {})} | custom-call | flops 805306368 | bytes 3670016 | tf_op jit(solution)/shard_map/pixels/pallas_call | solution.py:348
  211.6 1.9 collective-permute-done.5.refs_4_
  213.5 3.5 %collective-permute-done.6.refs_5_ = bf16[1,2,96,512]{3,2,1,0:T(8,128)(2,1)S(1)} collective-permute-done((bf16[1,2,96,512]{3,2,1,0:T(8,128)(2,1)S(1)}, bf16[1,2,96,512]{3,2,1,0:T(8,128)(2,1)S(1)}, u32[]{:S(2)}, u32[]{:S(2)}) %collective-permute-start.6) | collective-permute-done | bytes 196640 | tf_op jit(solution)/shard_map/ppermute | solution.py:342
  217.1 3.2 %pixels.11 = f32[8,1,512,512]{3,2,1,0:T(8,128)} custom-call(bf16[1,2,96,512]{3,2,1,0:T(8,128)(2,1)S(1)} %copy-done.36, bf16[1,2,96,512]{3,2,1,0:T(8,128)(2,1)S(1)} %copy-done.56, bf16[1,2,96,512]{3,2,1,0:T(8,128)(2,1)S(1)} %copy-done.70, bf16[1,2,96,512]{3,2,1,0:T(8,128)(2,1)S(1)} %collective-permute-done.4.refs_3_, ...), custom_call_target="tpu_custom_call", output_to_operand_aliasing={{}: (10, {})} | custom-call | flops 805306368 | bytes 3670016 | tf_op jit(solution)/shard_map/pixels/pallas_call | solution.py:348
  (243 shorter events, 60.0 us)
Async XLA Ops:
  44.0 18.5 %collective-permute-start.41 = (bf16[1,2,96,512]{3,2,1,0:T(8,128)(2,1)S(1)}, bf16[1,2,96,512]{3,2,1,0:T(8,128)(2,1)S(1)}, u32[]{:S(2)}, u32[]{:S(2)}) collective-permute-start(bf16[1,2,96,512]{3,2,1,0:T(8,128)(2,1)S(1)} %get-tuple-element.104), channel_id=1, source_target_pairs={{0,20},{4,16},{8,28},{12,24},{16,4},{20,0},{24,12},{28,8},{1,21},{... | collective-permute-start | bytes 589832 | tf_op jit(solution)/shard_map/ppermute | solution.py:342
  44.7 19.0 %collective-permute-start.42 = (bf16[1,2,96,512]{3,2,1,0:T(8,128)(2,1)S(1)}, bf16[1,2,96,512]{3,2,1,0:T(8,128)(2,1)S(1)}, u32[]{:S(2)}, u32[]{:S(2)}) collective-permute-start(bf16[1,2,96,512]{3,2,1,0:T(8,128)(2,1)S(1)} %get-tuple-element.105), channel_id=1, source_target_pairs={{0,24},{4,28},{8,16},{12,20},{16,8},{20,12},{24,0},{28,4},{1,25},{... | collective-permute-start | bytes 589832 | tf_op jit(solution)/shard_map/ppermute | solution.py:342
  57.3 16.2 %collective-permute-start.30 = (bf16[1,2,96,512]{3,2,1,0:T(8,128)(2,1)S(1)}, bf16[1,2,96,512]{3,2,1,0:T(8,128)(2,1)S(1)}, u32[]{:S(2)}, u32[]{:S(2)}) collective-permute-start(bf16[1,2,96,512]{3,2,1,0:T(8,128)(2,1)S(1)} %get-tuple-element.92), channel_id=1, source_target_pairs={{0,4},{4,0},{8,12},{12,8},{16,20},{20,16},{24,28},{28,24},{1,5},{5... | collective-permute-start | bytes 589832 | tf_op jit(solution)/shard_map/ppermute | solution.py:342
  58.8 16.2 %collective-permute-start.31 = (bf16[1,2,96,512]{3,2,1,0:T(8,128)(2,1)S(1)}, bf16[1,2,96,512]{3,2,1,0:T(8,128)(2,1)S(1)}, u32[]{:S(2)}, u32[]{:S(2)}) collective-permute-start(bf16[1,2,96,512]{3,2,1,0:T(8,128)(2,1)S(1)} %get-tuple-element.93), channel_id=1, source_target_pairs={{0,8},{4,12},{8,0},{12,4},{16,24},{20,28},{24,16},{28,20},{1,9},{5... | collective-permute-start | bytes 589832 | tf_op jit(solution)/shard_map/ppermute | solution.py:342
  73.5 16.9 %collective-permute-start.35 = (bf16[1,2,96,512]{3,2,1,0:T(8,128)(2,1)S(1)}, bf16[1,2,96,512]{3,2,1,0:T(8,128)(2,1)S(1)}, u32[]{:S(2)}, u32[]{:S(2)}) collective-permute-start(bf16[1,2,96,512]{3,2,1,0:T(8,128)(2,1)S(1)} %get-tuple-element.97), channel_id=1, source_target_pairs={{0,24},{4,28},{8,16},{12,20},{16,8},{20,12},{24,0},{28,4},{1,25},{... | collective-permute-start | bytes 589832 | tf_op jit(solution)/shard_map/ppermute | solution.py:342
  75.0 17.5 %collective-permute-start.36 = (bf16[1,2,96,512]{3,2,1,0:T(8,128)(2,1)S(1)}, bf16[1,2,96,512]{3,2,1,0:T(8,128)(2,1)S(1)}, u32[]{:S(2)}, u32[]{:S(2)}) collective-permute-start(bf16[1,2,96,512]{3,2,1,0:T(8,128)(2,1)S(1)} %get-tuple-element.98), channel_id=1, source_target_pairs={{0,28},{4,24},{8,20},{12,16},{16,12},{20,8},{24,4},{28,0},{1,29},{... | collective-permute-start | bytes 589832 | tf_op jit(solution)/shard_map/ppermute | solution.py:342
  76.5 18.0 %collective-permute-start.10 = (bf16[1,2,96,512]{3,2,1,0:T(8,128)(2,1)S(1)}, bf16[1,2,96,512]{3,2,1,0:T(8,128)(2,1)S(1)}, u32[]{:S(2)}, u32[]{:S(2)}) collective-permute-start(bf16[1,2,96,512]{3,2,1,0:T(8,128)(2,1)S(1)} %get-tuple-element.69), channel_id=1, source_target_pairs={{0,8},{4,12},{8,0},{12,4},{16,24},{20,28},{24,16},{28,20},{1,9},{5... | collective-permute-start | bytes 589832 | tf_op jit(solution)/shard_map/ppermute | solution.py:342
  77.3 18.1 %collective-permute-start.11 = (bf16[1,2,96,512]{3,2,1,0:T(8,128)(2,1)S(1)}, bf16[1,2,96,512]{3,2,1,0:T(8,128)(2,1)S(1)}, u32[]{:S(2)}, u32[]{:S(2)}) collective-permute-start(bf16[1,2,96,512]{3,2,1,0:T(8,128)(2,1)S(1)} %get-tuple-element.70), channel_id=1, source_target_pairs={{0,12},{4,8},{8,4},{12,0},{16,28},{20,24},{24,20},{28,16},{1,13},{... | collective-permute-start | bytes 589832 | tf_op jit(solution)/shard_map/ppermute | solution.py:342
  77.9 18.2 %collective-permute-start.12 = (bf16[1,2,96,512]{3,2,1,0:T(8,128)(2,1)S(1)}, bf16[1,2,96,512]{3,2,1,0:T(8,128)(2,1)S(1)}, u32[]{:S(2)}, u32[]{:S(2)}) collective-permute-start(bf16[1,2,96,512]{3,2,1,0:T(8,128)(2,1)S(1)} %get-tuple-element.71), channel_id=1, source_target_pairs={{0,16},{4,20},{8,24},{12,28},{16,0},{20,4},{24,8},{28,12},{1,17},{... | collective-permute-start | bytes 589832 | tf_op jit(solution)/shard_map/ppermute | solution.py:342
  91.1 18.3 %collective-permute-start.13 = (bf16[1,2,96,512]{3,2,1,0:T(8,128)(2,1)S(1)}, bf16[1,2,96,512]{3,2,1,0:T(8,128)(2,1)S(1)}, u32[]{:S(2)}, u32[]{:S(2)}) collective-permute-start(bf16[1,2,96,512]{3,2,1,0:T(8,128)(2,1)S(1)} %get-tuple-element.72), channel_id=1, source_target_pairs={{0,20},{4,16},{8,28},{12,24},{16,4},{20,0},{24,12},{28,8},{1,21},{... | collective-permute-start | bytes 589832 | tf_op jit(solution)/shard_map/ppermute | solution.py:342
  93.1 17.5 %collective-permute-start.14 = (bf16[1,2,96,512]{3,2,1,0:T(8,128)(2,1)S(1)}, bf16[1,2,96,512]{3,2,1,0:T(8,128)(2,1)S(1)}, u32[]{:S(2)}, u32[]{:S(2)}) collective-permute-start(bf16[1,2,96,512]{3,2,1,0:T(8,128)(2,1)S(1)} %get-tuple-element.73), channel_id=1, source_target_pairs={{0,24},{4,28},{8,16},{12,20},{16,8},{20,12},{24,0},{28,4},{1,25},{... | collective-permute-start | bytes 589832 | tf_op jit(solution)/shard_map/ppermute | solution.py:342
  94.6 16.9 %collective-permute-start.15 = (bf16[1,2,96,512]{3,2,1,0:T(8,128)(2,1)S(1)}, bf16[1,2,96,512]{3,2,1,0:T(8,128)(2,1)S(1)}, u32[]{:S(2)}, u32[]{:S(2)}) collective-permute-start(bf16[1,2,96,512]{3,2,1,0:T(8,128)(2,1)S(1)} %get-tuple-element.74), channel_id=1, source_target_pairs={{0,28},{4,24},{8,20},{12,16},{16,12},{20,8},{24,4},{28,0},{1,29},{... | collective-permute-start | bytes 589832 | tf_op jit(solution)/shard_map/ppermute | solution.py:342
  95.4 16.6 %collective-permute-start.9 = (bf16[1,2,96,512]{3,2,1,0:T(8,128)(2,1)S(1)}, bf16[1,2,96,512]{3,2,1,0:T(8,128)(2,1)S(1)}, u32[]{:S(2)}, u32[]{:S(2)}) collective-permute-start(bf16[1,2,96,512]{3,2,1,0:T(8,128)(2,1)S(1)} %get-tuple-element.68), channel_id=1, source_target_pairs={{0,4},{4,0},{8,12},{12,8},{16,20},{20,16},{24,28},{28,24},{1,5},{5... | collective-permute-start | bytes 589832 | tf_op jit(solution)/shard_map/ppermute | solution.py:342
  96.2 17.3 %collective-permute-start.2 = (bf16[1,2,96,512]{3,2,1,0:T(8,128)(2,1)S(1)}, bf16[1,2,96,512]{3,2,1,0:T(8,128)(2,1)S(1)}, u32[]{:S(2)}, u32[]{:S(2)}) collective-permute-start(bf16[1,2,96,512]{3,2,1,0:T(8,128)(2,1)S(1)} %get-tuple-element.60), channel_id=1, source_target_pairs={{0,4},{4,0},{8,12},{12,8},{16,20},{20,16},{24,28},{28,24},{1,5},{5... | collective-permute-start | bytes 589832 | tf_op jit(solution)/shard_map/ppermute | solution.py:342
  110.1 24.9 %collective-permute-start.23 = (bf16[2,2,96,512]{3,2,1,0:T(8,128)(2,1)S(1)}, bf16[2,2,96,512]{3,2,1,0:T(8,128)(2,1)S(1)}, u32[]{:S(2)}, u32[]{:S(2)}) collective-permute-start(bf16[2,2,96,512]{3,2,1,0:T(8,128)(2,1)S(1)} %get-tuple-element.84), channel_id=1, source_target_pairs={{0,4},{4,0},{8,12},{12,8},{16,20},{20,16},{24,28},{28,24},{1,5},{5... | collective-permute-start | bytes 1179656 | tf_op jit(solution)/shard_map/ppermute | solution.py:342
  110.6 26.6 %collective-permute-start.24 = (bf16[2,2,96,512]{3,2,1,0:T(8,128)(2,1)S(1)}, bf16[2,2,96,512]{3,2,1,0:T(8,128)(2,1)S(1)}, u32[]{:S(2)}, u32[]{:S(2)}) collective-permute-start(bf16[2,2,96,512]{3,2,1,0:T(8,128)(2,1)S(1)} %get-tuple-element.85), channel_id=1, source_target_pairs={{0,8},{4,12},{8,0},{12,4},{16,24},{20,28},{24,16},{28,20},{1,9},{5... | collective-permute-start | bytes 1179656 | tf_op jit(solution)/shard_map/ppermute | solution.py:342
  111.4 28.2 %collective-permute-start.25 = (bf16[2,2,96,512]{3,2,1,0:T(8,128)(2,1)S(1)}, bf16[2,2,96,512]{3,2,1,0:T(8,128)(2,1)S(1)}, u32[]{:S(2)}, u32[]{:S(2)}) collective-permute-start(bf16[2,2,96,512]{3,2,1,0:T(8,128)(2,1)S(1)} %get-tuple-element.86), channel_id=1, source_target_pairs={{0,12},{4,8},{8,4},{12,0},{16,28},{20,24},{24,20},{28,16},{1,13},{... | collective-permute-start | bytes 1179656 | tf_op jit(solution)/shard_map/ppermute | solution.py:342
  112.8 27.7 %collective-permute-start.26 = (bf16[2,2,96,512]{3,2,1,0:T(8,128)(2,1)S(1)}, bf16[2,2,96,512]{3,2,1,0:T(8,128)(2,1)S(1)}, u32[]{:S(2)}, u32[]{:S(2)}) collective-permute-start(bf16[2,2,96,512]{3,2,1,0:T(8,128)(2,1)S(1)} %get-tuple-element.87), channel_id=1, source_target_pairs={{0,16},{4,20},{8,24},{12,28},{16,0},{20,4},{24,8},{28,12},{1,17},{... | collective-permute-start | bytes 1179656 | tf_op jit(solution)/shard_map/ppermute | solution.py:342
  113.5 20.9 %collective-permute-start.3 = (bf16[1,2,96,512]{3,2,1,0:T(8,128)(2,1)S(1)}, bf16[1,2,96,512]{3,2,1,0:T(8,128)(2,1)S(1)}, u32[]{:S(2)}, u32[]{:S(2)}) collective-permute-start(bf16[1,2,96,512]{3,2,1,0:T(8,128)(2,1)S(1)} %get-tuple-element.61), channel_id=1, source_target_pairs={{0,8},{4,12},{8,0},{12,4},{16,24},{20,28},{24,16},{28,20},{1,9},{5... | collective-permute-start | bytes 589832 | tf_op jit(solution)/shard_map/ppermute | solution.py:342
  135.0 27.7 %collective-permute-start.27 = (bf16[2,2,96,512]{3,2,1,0:T(8,128)(2,1)S(1)}, bf16[2,2,96,512]{3,2,1,0:T(8,128)(2,1)S(1)}, u32[]{:S(2)}, u32[]{:S(2)}) collective-permute-start(bf16[2,2,96,512]{3,2,1,0:T(8,128)(2,1)S(1)} %get-tuple-element.88), channel_id=1, source_target_pairs={{0,20},{4,16},{8,28},{12,24},{16,4},{20,0},{24,12},{28,8},{1,21},{... | collective-permute-start | bytes 1179656 | tf_op jit(solution)/shard_map/ppermute | solution.py:342
  135.8 27.6 %collective-permute-start.28 = (bf16[2,2,96,512]{3,2,1,0:T(8,128)(2,1)S(1)}, bf16[2,2,96,512]{3,2,1,0:T(8,128)(2,1)S(1)}, u32[]{:S(2)}, u32[]{:S(2)}) collective-permute-start(bf16[2,2,96,512]{3,2,1,0:T(8,128)(2,1)S(1)} %get-tuple-element.89), channel_id=1, source_target_pairs={{0,24},{4,28},{8,16},{12,20},{16,8},{20,12},{24,0},{28,4},{1,25},{... | collective-permute-start | bytes 1179656 | tf_op jit(solution)/shard_map/ppermute | solution.py:342
  138.0 25.9 %collective-permute-start.29 = (bf16[2,2,96,512]{3,2,1,0:T(8,128)(2,1)S(1)}, bf16[2,2,96,512]{3,2,1,0:T(8,128)(2,1)S(1)}, u32[]{:S(2)}, u32[]{:S(2)}) collective-permute-start(bf16[2,2,96,512]{3,2,1,0:T(8,128)(2,1)S(1)} %get-tuple-element.90), channel_id=1, source_target_pairs={{0,28},{4,24},{8,20},{12,16},{16,12},{20,8},{24,4},{28,0},{1,29},{... | collective-permute-start | bytes 1179656 | tf_op jit(solution)/shard_map/ppermute | solution.py:342
  140.4 25.7 %collective-permute-start.16 = (bf16[2,2,96,512]{3,2,1,0:T(8,128)(2,1)S(1)}, bf16[2,2,96,512]{3,2,1,0:T(8,128)(2,1)S(1)}, u32[]{:S(2)}, u32[]{:S(2)}) collective-permute-start(bf16[2,2,96,512]{3,2,1,0:T(8,128)(2,1)S(1)} %get-tuple-element.76), channel_id=1, source_target_pairs={{0,4},{4,0},{8,12},{12,8},{16,20},{20,16},{24,28},{28,24},{1,5},{5... | collective-permute-start | bytes 1179656 | tf_op jit(solution)/shard_map/ppermute | solution.py:342
  141.2 26.4 %collective-permute-start.17 = (bf16[2,2,96,512]{3,2,1,0:T(8,128)(2,1)S(1)}, bf16[2,2,96,512]{3,2,1,0:T(8,128)(2,1)S(1)}, u32[]{:S(2)}, u32[]{:S(2)}) collective-permute-start(bf16[2,2,96,512]{3,2,1,0:T(8,128)(2,1)S(1)} %get-tuple-element.77), channel_id=1, source_target_pairs={{0,8},{4,12},{8,0},{12,4},{16,24},{20,28},{24,16},{28,20},{1,9},{5... | collective-permute-start | bytes 1179656 | tf_op jit(solution)/shard_map/ppermute | solution.py:342
  162.7 29.6 %collective-permute-start.18 = (bf16[2,2,96,512]{3,2,1,0:T(8,128)(2,1)}, bf16[2,2,96,512]{3,2,1,0:T(8,128)(2,1)S(1)}, u32[]{:S(2)}, u32[]{:S(2)}) collective-permute-start(bf16[2,2,96,512]{3,2,1,0:T(8,128)(2,1)} %get-tuple-element.78), channel_id=1, source_target_pairs={{0,12},{4,8},{8,4},{12,0},{16,28},{20,24},{24,20},{28,16},{1,13},{... | collective-permute-start | bytes 1179656 | tf_op jit(solution)/shard_map/ppermute | solution.py:342
  163.4 30.0 %collective-permute-start.19 = (bf16[2,2,96,512]{3,2,1,0:T(8,128)(2,1)}, bf16[2,2,96,512]{3,2,1,0:T(8,128)(2,1)S(1)}, u32[]{:S(2)}, u32[]{:S(2)}) collective-permute-start(bf16[2,2,96,512]{3,2,1,0:T(8,128)(2,1)} %get-tuple-element.79), channel_id=1, source_target_pairs={{0,16},{4,20},{8,24},{12,28},{16,0},{20,4},{24,8},{28,12},{1,17},{... | collective-permute-start | bytes 1179656 | tf_op jit(solution)/shard_map/ppermute | solution.py:342
  164.7 35.5 %collective-permute-start.20 = (bf16[2,2,96,512]{3,2,1,0:T(8,128)(2,1)}, bf16[2,2,96,512]{3,2,1,0:T(8,128)(2,1)S(1)}, u32[]{:S(2)}, u32[]{:S(2)}) collective-permute-start(bf16[2,2,96,512]{3,2,1,0:T(8,128)(2,1)} %get-tuple-element.80), channel_id=1, source_target_pairs={{0,20},{4,16},{8,28},{12,24},{16,4},{20,0},{24,12},{28,8},{1,21},{... | collective-permute-start | bytes 1179656 | tf_op jit(solution)/shard_map/ppermute | solution.py:342
  166.1 34.9 %collective-permute-start.21 = (bf16[2,2,96,512]{3,2,1,0:T(8,128)(2,1)}, bf16[2,2,96,512]{3,2,1,0:T(8,128)(2,1)S(1)}, u32[]{:S(2)}, u32[]{:S(2)}) collective-permute-start(bf16[2,2,96,512]{3,2,1,0:T(8,128)(2,1)} %get-tuple-element.81), channel_id=1, source_target_pairs={{0,24},{4,28},{8,16},{12,20},{16,8},{20,12},{24,0},{28,4},{1,25},{... | collective-permute-start | bytes 1179656 | tf_op jit(solution)/shard_map/ppermute | solution.py:342
  167.6 34.9 %collective-permute-start.22 = (bf16[2,2,96,512]{3,2,1,0:T(8,128)(2,1)}, bf16[2,2,96,512]{3,2,1,0:T(8,128)(2,1)}, u32[]{:S(2)}, u32[]{:S(2)}) collective-permute-start(bf16[2,2,96,512]{3,2,1,0:T(8,128)(2,1)} %get-tuple-element.82), channel_id=1, source_target_pairs={{0,28},{4,24},{8,20},{12,16},{16,12},{20,8},{24,4},{28,0},{1,29},{... | collective-permute-start | bytes 1179656 | tf_op jit(solution)/shard_map/ppermute | solution.py:342
  192.3 19.3 %collective-permute-start.4 = (bf16[1,2,96,512]{3,2,1,0:T(8,128)(2,1)S(1)}, bf16[1,2,96,512]{3,2,1,0:T(8,128)(2,1)S(1)}, u32[]{:S(2)}, u32[]{:S(2)}) collective-permute-start(bf16[1,2,96,512]{3,2,1,0:T(8,128)(2,1)S(1)} %copy-done.80), channel_id=1, source_target_pairs={{0,12},{4,8},{8,4},{12,0},{16,28},{20,24},{24,20},{28,16},{1,13},{... | collective-permute-start | bytes 589832 | tf_op jit(solution)/shard_map/ppermute | solution.py:342
  193.4 20.1 %collective-permute-start.5 = (bf16[1,2,96,512]{3,2,1,0:T(8,128)(2,1)S(1)}, bf16[1,2,96,512]{3,2,1,0:T(8,128)(2,1)S(1)}, u32[]{:S(2)}, u32[]{:S(2)}) collective-permute-start(bf16[1,2,96,512]{3,2,1,0:T(8,128)(2,1)S(1)} %copy-done.78), channel_id=1, source_target_pairs={{0,16},{4,20},{8,24},{12,28},{16,0},{20,4},{24,8},{28,12},{1,17},{... | collective-permute-start | bytes 589832 | tf_op jit(solution)/shard_map/ppermute | solution.py:342
  200.2 16.9 %collective-permute-start.6 = (bf16[1,2,96,512]{3,2,1,0:T(8,128)(2,1)S(1)}, bf16[1,2,96,512]{3,2,1,0:T(8,128)(2,1)S(1)}, u32[]{:S(2)}, u32[]{:S(2)}) collective-permute-start(bf16[1,2,96,512]{3,2,1,0:T(8,128)(2,1)S(1)} %copy-done.76), channel_id=1, source_target_pairs={{0,20},{4,16},{8,28},{12,24},{16,4},{20,0},{24,12},{28,8},{1,21},{... | collective-permute-start | bytes 589832 | tf_op jit(solution)/shard_map/ppermute | solution.py:342
  (95 other events, 827.3 us)

commit v2 on v1

--- a/solution.py
+++ b/solution.py
@@ -91,7 +91,7 @@
     own = (me * kb + lane((kb, 1), 0)).astype(f32)
     for a in range(na):
         for t in range(ntile):
-            oy = pos_ref[t, 0] - jnp.bitwise_xor(a_me, a) * fs + pad
+            oy = pos_ref[0, t] - jnp.bitwise_xor(a_me, a) * fs + pad
             ok = jnp.where((oy >= 0) & (oy <= frame - ts), 1.0, 0.0).astype(f32)
             index = own * (oy + pixel).astype(f32)
             row_ref[a, t, :kb] = (cos_turn(index, frame) * ok).astype(bf16)
@@ -112,7 +112,7 @@
 
 
 def column_phases_kernel(frame, fs, pos_ref, col_ref, cos_ref, sin_ref):
-    ntile, ts = pos_ref.shape[0], col_ref.shape[1]
+    ntile, ts = pos_ref.shape[1], col_ref.shape[1]
     half, quarter, pad = frame // 2, frame // 4, (frame - fs) // 2
     b_me = lax.rem(lax.axis_index("facet"), FCOLS)
     spot = lane((1, 2 * half), 1)
@@ -124,7 +124,7 @@
 
     def columns(i, carry):
         b, t = lax.div(i, ntile), lax.rem(i, ntile)
-        ox = pos_ref[t, 1] - jnp.bitwise_xor(b_me, b) * fs + pad
+        ox = pos_ref[1, t] - jnp.bitwise_xor(b_me, b) * fs + pad
         ok = jnp.where((ox >= 0) & (ox <= frame - ts), 1.0, 0.0).astype(f32)
         index = ox.astype(f32) * freq + shift
         cos_ox, sin_ox = cos_turn(index, frame) * ok, cos_turn(index - quarter, frame) * ok
@@ -134,18 +134,22 @@
     lax.fori_loop(0, FCOLS * ntile, columns, 0)
 
 
-def pixel_phases_kernel(frame, pad, nf, out_ref):
-    kb = frame // nf
+def pixel_phases_kernel(frame, pad, nf, kb, out_ref):
     me = lax.axis_index("facet")
-    column = lane((1, 2 * frame), 1)
-    k = jnp.zeros((1, 2 * frame), i32)
-    for p in range(2):
-        for j in range(nf):
-            start = p * frame + j * kb
-            here = (column >= start) & (column < start + kb)
-            k = jnp.where(here, column - start + jnp.bitwise_xor(me, j) * kb, k)
-    shift = jnp.where(column >= frame, frame // 4, 0).astype(f32)
-    k = k.astype(f32)
+    width = out_ref.shape[1]
+    rows = width // nf
+    column = lane((1, width), 1)
+    inner, base = column, jnp.zeros((1, width), i32)
+    for j in range(nf):
+        here = (column >= j * rows) & (column < (j + 1) * rows)
+        inner = jnp.where(here, column - j * rows, inner)
+        base = jnp.where(here, jnp.bitwise_xor(me, j) * kb, base)
+    count = kb if rows == 2 * kb else kb // 2
+    k = jnp.where(inner < count, inner, inner - count)
+    k = jnp.where(inner < 2 * count, k, count)
+    minus_sin = ((inner >= count) & (inner < 2 * count)) | (inner == 2 * count + 1)
+    shift = jnp.where(minus_sin, frame // 4, 0).astype(f32)
+    k = (base + k).astype(f32)
     block = 64
 
     def some(i, carry):
@@ -156,13 +160,19 @@
     lax.fori_loop(0, out_ref.shape[0] // block, some, 0)
 
 
-def rows_kernel(total, nch, chan0, b0, psf_of_ref, coef_ref, row_ref, col_ref, inv_ref, flip_ref, psf_ref, *rest):
-    out_refs, (lhs_ref, rev_ref, q_ref) = rest[:-3], rest[-3:]
+def rows_kernel(total, nch, chan0, paired, psf_of_ref, coef_ref, row_ref, col_ref, inv_ref, flip_ref, psf_ref, *rest):
+    far_ref, rest = (rest[0], rest[1:]) if paired else (None, rest)
+    out_refs, (lhs_ref, psf_up_ref, psf_dn_ref, q_ref) = rest[:-4], rest[-4:]
     na, ntile, _, ts = row_ref.shape
     nf = coef_ref.shape[0]
     npsf, kb, frame = psf_ref.shape[0], psf_ref.shape[3], psf_ref.shape[4]
+    rb = lhs_ref.shape[0] // (2 * na)
     half = frame // 2
     step = pl.program_id(1)
+    first = lane((1, half), 1) == 0
+
+    def turned(x):
+        return jnp.dot(x[:, half:], flip_ref[...], preferred_element_type=f32)
 
     @pl.when(step == 0)
     def _():
@@ -174,63 +184,98 @@
             )
             model = (a0 + a1 * x + a2 * (x * x)).astype(bf16)
             for a in range(na):
-                y = jnp.dot(row_ref[a, t], model, preferred_element_type=f32)
-                lhs_ref[a * 2 * kb : (a + 1) * 2 * kb, t * ts : (t + 1) * ts] = y.astype(bf16)
+                y = jnp.dot(row_ref[a, t], model, preferred_element_type=f32).astype(bf16)
+                start, cols = a * 2 * rb, slice(t * ts, (t + 1) * ts)
+                lhs_ref[start : start + rb, cols] = y[:rb]
+                lhs_ref[start + rb : start + 2 * rb, cols] = y[kb : kb + rb]
+        if paired:
+            count = kb // 2
+            i, m = lane((rb, count), 0), lane((rb, count), 1)
+            mirror = jnp.where((i >= 1) & (i < count) & (m == count - i), 1.0, 0.0).astype(bf16)
         for p in range(npsf):
             for part in range(2):
-                turned = jnp.dot(psf_ref[p, 0, part, :, half:], flip_ref[...], preferred_element_type=f32)
-                rev_ref[p, part] = turned.astype(bf16)
+                psf = psf_ref[p, 0, part, :rb]
+                up, dn = psf[:, :half], turned(psf)
+                if paired:
+                    far = jnp.dot(mirror, far_ref[p, 0, part], preferred_element_type=f32).astype(bf16)
+                    far_up, far_dn = far[:, :half].astype(f32), turned(far)
+                    sign = 1.0 - 2.0 * part
+                    up = up.astype(f32) + sign * jnp.where(first, far_up, far_dn)
+                    dn = dn + sign * jnp.where(first, far_dn, far_up)
+                psf_up_ref[p, part] = up.astype(psf_up_ref.dtype)
+                psf_dn_ref[p, part] = dn.astype(psf_dn_ref.dtype)
 
     both = jnp.dot(lhs_ref[...], col_ref[0], preferred_element_type=f32)
     me = lax.axis_index("facet")
-    first = lane((1, half), 1) == 0
-    zero = jnp.zeros((kb, half), f32)
+    zero = jnp.zeros((rb, half), f32)
     for a in range(na):
-        psf = psf_of_ref[jnp.bitwise_xor(me, a * FCOLS + b0 + step)]
-        top = slice(a * 2 * kb, a * 2 * kb + kb)
-        low = slice(a * 2 * kb + kb, (a + 1) * 2 * kb)
+        psf = psf_of_ref[jnp.bitwise_xor(me, a * FCOLS + step)]
+        top = slice(a * 2 * rb, a * 2 * rb + rb)
+        low = slice(a * 2 * rb + rb, (a + 1) * 2 * rb)
         rc, rs = both[top, :half], both[top, half:]
         ic, is_ = both[low, :half], both[low, half:]
         rs0, is0 = jnp.where(first, zero, rs), jnp.where(first, zero, is_)
         up_re, up_im = rc - is0, ic + rs0
         dn_re, dn_im = jnp.where(first, rs, rc + is_), jnp.where(first, is_, ic - rs)
-        p_re, p_im = psf_ref[psf, 0, 0, :, :half].astype(f32), psf_ref[psf, 0, 1, :, :half].astype(f32)
-        n_re, n_im = rev_ref[psf, 0].astype(f32), rev_ref[psf, 1].astype(f32)
+        p_re, p_im = psf_up_ref[psf, 0].astype(f32), psf_up_ref[psf, 1].astype(f32)
+        n_re, n_im = psf_dn_ref[psf, 0].astype(f32), psf_dn_ref[psf, 1].astype(f32)
         q_re, q_im = up_re * p_re - up_im * p_im, up_re * p_im + up_im * p_re
         z_re, z_im = dn_re * n_re - dn_im * n_im, dn_re * n_im + dn_im * n_re
         q_ref[top, :half] = (q_re + jnp.where(first, zero, z_re)).astype(bf16)
         q_ref[top, half:] = jnp.where(first, z_re, z_im - q_im).astype(bf16)
         q_ref[low, :half] = (q_im + jnp.where(first, zero, z_im)).astype(bf16)
         q_ref[low, half:] = jnp.where(first, z_im, q_re - z_re).astype(bf16)
-    w = jnp.dot(q_ref[...], inv_ref[...], preferred_element_type=f32).astype(bf16)
-    width = len(out_refs) // na
-    for b in range(width):
+    w = jnp.dot(q_ref[...], inv_ref[...], preferred_element_type=f32)
+    for b in range(FCOLS):
 
         @pl.when(step == b)
         def _():
             for a in range(na):
-                for p in range(2):
-                    start = (2 * a + p) * kb
-                    out_refs[a * width + b][0, p] = w[start : start + kb]
+                out_ref, start = out_refs[a * FCOLS + b], a * 2 * rb
+                if paired:
+                    count = kb // 2
+                    out_ref[0, :count] = w[start : start + count].astype(bf16)
+                    out_ref[0, count : 2 * count] = w[start + rb : start + rb + count].astype(bf16)
+                    re, im = start + count, start + rb + count
+                    tile = (TILE, w.shape[1])
+                    spot = lane(tile, 0)
+                    extra = jnp.where(spot == 1, jnp.broadcast_to(w[im : im + 1], tile), 0.0)
+                    extra = jnp.where(spot == 0, jnp.broadcast_to(w[re : re + 1], tile), extra)
+                    out_ref[0, 2 * count :] = extra.astype(bf16)
+                else:
+                    out_ref[0] = w[start : start + 2 * rb].astype(bf16)
 
 
 def pixels_kernel(nf, scale, *refs):
     blocks, table_ref, residual_ref, out_ref = refs[:nf], refs[nf], refs[nf + 1], refs[-1]
-    w = jnp.concatenate([blocks[j][0, p] for p in range(2) for j in range(nf)], axis=0)
+    w = jnp.concatenate([block[0] for block in blocks], axis=0)
     conv = jnp.dot(table_ref[...], w, preferred_element_type=f32)
     out_ref[0, 0] = residual_ref[0, 0] - conv * scale
 
 
-def chunks_of(nch):
-    sizes, left = [], nch
+def chunks_of(nch, npair):
+    sizes, left = [], nch - npair
     while left:
-        sizes.append(2 if len(sizes) >= 2 and left > 3 else 1)
+        sizes.append(2 if len(sizes) >= 2 and left >= 2 else 1)
         left -= sizes[-1]
-    return [(sum(sizes[:i]), n, [(0, FCOLS)]) for i, n in enumerate(sizes)]
-
-
-def send_order(members):
-    return sorted((j for j in members if j), key=lambda j: (-bin(j >> 1).count("1"), j))
+    paired = [False] * len(sizes)
+    while npair:
+        sizes.append(min(2, npair))
+        npair -= sizes[-1]
+        paired.append(True)
+    return [(sum(sizes[:i]), n, paired[i]) for i, n in enumerate(sizes)]
+
+
+def pairs_of(nch, nf, kb, frame):
+    return NPAIR if nch >= NPAIR + 4 and frame == nf * kb and kb % (2 * TILE) == 0 else 0
+
+
+def send_order(nf):
+    return sorted(range(1, nf), key=lambda j: (-bin(j >> 1).count("1"), j))
+
+
+NPAIR = 2
+TILE = 16
 
 
 VMEM = pl.BlockSpec(memory_space=pltpu.VMEM)
@@ -242,6 +287,7 @@
 
 
 def shards(nf, nz, residual, components, chan_weight, tile_pos, facet_psf, psf_spectra):
+    whole_psf = psf_spectra
     residual, psf_spectra = in_hbm(residual), in_hbm(psf_spectra)
     ntile, nch, rows, ts = components.shape
     npsf, _, _, kb, frame = psf_spectra.shape
@@ -249,7 +295,12 @@
     pad, half = (frame - fs) // 2, frame // 2
     total = nch * nz
     na = nf // FCOLS
-
+    npair, far = pairs_of(nch, nf, kb, frame), None
+
+    if npair:
+        far = lax.ppermute(
+            whole_psf[:, nch - npair :, :, kb // 2 :], "facet", [(s, nf - 1 - s) for s in range(nf)]
+        )
     sums = pl.pallas_call(
         functools.partial(moments_kernel, total),
         out_shape=jax.ShapeDtypeStruct((3 * ntile + 1, rows, ts), f32),
@@ -268,7 +319,7 @@
         out_specs=[VMEM] * 3,
         compiler_params=pltpu.CompilerParams(vmem_limit_bytes=SMALL_LIMIT),
         name="rowphases",
-    )(tile_pos)
+    )(tile_pos.T)
     col_table = pl.pallas_call(
         functools.partial(column_phases_kernel, frame, fs),
         out_shape=jax.ShapeDtypeStruct((FCOLS * ntile, ts, frame), bf16),
@@ -277,7 +328,7 @@
         scratch_shapes=[pltpu.VMEM((ts, frame), f32)] * 2,
         compiler_params=pltpu.CompilerParams(vmem_limit_bytes=SMALL_LIMIT),
         name="colphases",
-    )(tile_pos)
+    )(tile_pos.T)
     row_table, inv_table, flip = in_hbm(row_table), in_hbm(inv_table), in_hbm(flip)
     col_table = col_table.reshape(FCOLS, ntile * ts, frame)
     other = jnp.zeros_like(sums)
@@ -294,69 +345,78 @@
     )(facet_psf, sums, other)
     fit = lax.all_gather(fit, "facet", axis=0)
     psf_of = fit[:, 3 * ntile, 0, 0].astype(i32)
-    pix_table = pl.pallas_call(
-        functools.partial(pixel_phases_kernel, frame, pad, nf),
-        out_shape=jax.ShapeDtypeStruct((fs, 2 * frame), bf16),
-        out_specs=VMEM,
-        name="pixphases",
-    )()
+    rb_pair, block_pair = kb // 2 + TILE, kb + TILE
+    tables = {}
+    for paired in (False, True)[: 1 + bool(npair)]:
+        tables[paired] = pl.pallas_call(
+            functools.partial(pixel_phases_kernel, frame, pad, nf, kb),
+            out_shape=jax.ShapeDtypeStruct((fs, nf * (block_pair if paired else 2 * kb)), bf16),
+            out_specs=VMEM,
+            name="pixphases",
+        )()
 
     pieces = []
-    for chan0, count, groups in chunks_of(nch):
-        got = [None] * nf
-        for b0, width in groups:
-            members = [a * FCOLS + b0 + b for a in range(na) for b in range(width)]
-            w = pl.pallas_call(
-                functools.partial(rows_kernel, total, nch, chan0, b0),
-                grid_spec=pltpu.PrefetchScalarGridSpec(
-                    num_scalar_prefetch=1,
-                    grid=(count, width),
-                    in_specs=[
-                        pl.BlockSpec((nf, 3 * ntile + 1, rows, ts), lambda c, b, s: (0, 0, 0, 0)),
-                        pl.BlockSpec((na, ntile, 2 * kb, ts), lambda c, b, s: (0, 0, 0, 0)),
-                        pl.BlockSpec((1, ntile * ts, frame), lambda c, b, s, b0=b0: (b0 + b, 0, 0)),
-                        pl.BlockSpec((frame, fs), lambda c, b, s: (0, 0)),
-                        pl.BlockSpec((half, half), lambda c, b, s: (0, 0)),
-                        pl.BlockSpec((npsf, 1, 2, kb, frame), lambda c, b, s, c0=chan0: (0, c0 + c, 0, 0, 0)),
-                    ],
-                    out_specs=[pl.BlockSpec((1, 2, kb, fs), lambda c, b, s: (c, 0, 0, 0))] * (na * width),
-                    scratch_shapes=[
-                        pltpu.VMEM((na * 2 * kb, ntile * ts), bf16),
-                        pltpu.VMEM((npsf, 2, kb, half), bf16),
-                        pltpu.VMEM((na * 2 * kb, frame), bf16),
-                    ],
-                ),
-                out_shape=[jax.ShapeDtypeStruct((count, 2, kb, fs), bf16)] * (na * width),
-                cost_estimate=pl.CostEstimate(
-                    flops=count * na * width * 4 * kb * frame * (ntile * ts + fs),
-                    bytes_accessed=count * (npsf * 4 * kb * frame + na * width * 4 * kb * fs)
-                    + 2 * width * ntile * ts * frame,
-                    transcendentals=0,
-                ),
-                compiler_params=pltpu.CompilerParams(vmem_limit_bytes=VMEM_LIMIT),
-                name="rows",
-            )(psf_of, fit, row_table, col_table, inv_table, flip, psf_spectra)
-            for i, j in enumerate(members):
-                got[j] = w[i]
-            for j in send_order(members):
-                got[j] = lax.ppermute(got[j], "facet", [(s, s ^ j) for s in range(nf)])
-        pieces.append((chan0, count, got))
+    for chan0, count, paired in chunks_of(nch, npair):
+        rb, block = (rb_pair, block_pair) if paired else (kb, 2 * kb)
+        psf_type = f32 if paired else bf16
+        fixed = lambda *shape: pl.BlockSpec(shape, lambda c, b, s: (0,) * len(shape))
+        w = pl.pallas_call(
+            functools.partial(rows_kernel, total, nch, chan0, paired),
+            grid_spec=pltpu.PrefetchScalarGridSpec(
+                num_scalar_prefetch=1,
+                grid=(count, FCOLS),
+                in_specs=[
+                    fixed(nf, 3 * ntile + 1, rows, ts),
+                    fixed(na, ntile, 2 * kb, ts),
+                    pl.BlockSpec((1, ntile * ts, frame), lambda c, b, s: (b, 0, 0)),
+                    fixed(frame, fs),
+                    fixed(half, half),
+                    pl.BlockSpec((npsf, 1, 2, kb, frame), lambda c, b, s, c0=chan0: (0, c0 + c, 0, 0, 0)),
+                ]
+                + [
+                    pl.BlockSpec(
+                        (npsf, 1, 2, kb // 2, frame),
+                        lambda c, b, s, c0=chan0 - (nch - npair): (0, c0 + c, 0, 0, 0),
+                    )
+                ]
+                * paired,
+                out_specs=[pl.BlockSpec((1, block, fs), lambda c, b, s: (c, 0, 0))] * nf,
+                scratch_shapes=[
+                    pltpu.VMEM((na * 2 * rb, ntile * ts), bf16),
+                    pltpu.VMEM((npsf, 2, rb, half), psf_type),
+                    pltpu.VMEM((npsf, 2, rb, half), psf_type),
+                    pltpu.VMEM((na * 2 * rb, frame), bf16),
+                ],
+            ),
+            out_shape=[jax.ShapeDtypeStruct((count, block, fs), bf16)] * nf,
+            cost_estimate=pl.CostEstimate(
+                flops=count * nf * 4 * rb * frame * (ntile * ts + fs),
+                bytes_accessed=count * (npsf * 4 * kb * frame + nf * 2 * block * fs) + 8 * ntile * ts * frame,
+                transcendentals=0,
+            ),
+            compiler_params=pltpu.CompilerParams(vmem_limit_bytes=VMEM_LIMIT),
+            name="rows",
+        )(psf_of, fit, row_table, col_table, inv_table, flip, psf_spectra, *([far] * paired))
+        got = list(w)
+        for j in send_order(nf):
+            got[j] = lax.ppermute(w[j], "facet", [(s, s ^ j) for s in range(nf)])
+        pieces.append((chan0, count, block, tables[paired], got))
     result = None
-    for chan0, count, got in pieces:
+    for chan0, count, block, pix_table, got in pieces:
         image = pl.BlockSpec((1, 1, fs, fs), lambda c, c0=chan0: (c0 + c, 0, 0, 0))
         before = [] if result is None else [result]
         result = pl.pallas_call(
             functools.partial(pixels_kernel, nf, 1.0 / (frame * frame)),
             grid=(count,),
-            in_specs=[pl.BlockSpec((1, 2, kb, fs), lambda c: (c, 0, 0, 0))] * nf
-            + [pl.BlockSpec((fs, 2 * frame), lambda c: (0, 0)), image]
+            in_specs=[pl.BlockSpec((1, block, fs), lambda c: (c, 0, 0))] * nf
+            + [pl.BlockSpec((fs, nf * block), lambda c: (0, 0)), image]
             + [pl.BlockSpec(memory_space=pl.ANY)] * len(before),
             out_specs=image,
             out_shape=jax.ShapeDtypeStruct(residual.shape, f32),
             input_output_aliases={nf + 2: 0} if before else {},
             cost_estimate=pl.CostEstimate(
-                flops=count * 4 * fs * frame * fs,
-                bytes_accessed=count * (nf * 4 * kb * fs + 8 * fs * fs),
+                flops=count * 2 * fs * nf * block * fs,
+                bytes_accessed=count * (nf * 2 * block * fs + 8 * fs * fs),
                 transcendentals=0,
             ),
             compiler_params=pltpu.CompilerParams(vmem_limit_bytes=VMEM_LIMIT),

time: 221 us -> 258 us (1.17)
  waiting for transfers between devices: 44.9 us -> 88.4 us
  starting transfers between devices: 45.5 us -> 39.3 us
    ppermute x42 -> x36, waiting for transfers between devices: 41.7 us -> 85.2 us  [the longest x35 85.2 us: shards(): got[j] = lax.ppermute(w[j], 'facet', [(s, s ^ j) for s in range(nf)])]
    ppermute x42 -> x36, starting transfers between devices: 39.6 us -> 33.5 us  [the longest x35 31.8 us: shards(): got[j] = lax.ppermute(w[j], 'facet', [(s, s ^ j) for s in range(nf)])]
    pallas_call x6 -> x5, Pallas kernels: 21.8 us -> 19.2 us  [shards(): pl.pallas_call(functools.partial(pixels_kernel, nf, 1.0 / (frame * frame)...]
    unnamed x167 -> x154, local copies, waits for them, and re-layouts: 25.4 us -> 24.1 us
  transfers between devices with their start and end apart: 44 -> 38, of which waited for: 8 -> 8; matrix products, arithmetic and copies ran while one was open for 0% -> 1% of each run, Pallas kernels for 35% -> 30%
where the time goes in v2:
time: 258 us; the launch traced here: 257 us
  Pallas kernels  91.3 us (35%)
  waiting for transfers between devices  88.4 us (34%)
  starting transfers between devices  39.3 us (15%)
  local copies, waits for them, and re-layouts  25.5 us (10%)
  blocking collectives  9.97 us (4%)
    ppermute x35, waiting for transfers between devices, shards(): got[j] = lax.ppermute(w[j], 'facet', [(s, s ^ j) for s in range(nf)])  85.2 us
    pallas_call x5, Pallas kernels, shards(): pl.pallas_call(functools.partial(rows_kernel, total, nch, chan0, paired),...  57 us
    ppermute x35, starting transfers between devices, shards(): got[j] = lax.ppermute(w[j], 'facet', [(s, s ^ j) for s in range(nf)])  31.8 us
    unnamed x154, local copies, waits for them, and re-layouts  24.1 us
    pallas_call x5, Pallas kernels, shards(): pl.pallas_call(functools.partial(pixels_kernel, nf, 1.0 / (frame * frame)...  19.2 us
    all_gather x1, blocking collectives, shards(): fit = lax.all_gather(fit, 'facet', axis=0)  9.97 us
    pallas_call x2, Pallas kernels, shards(): pl.pallas_call(functools.partial(pixel_phases_kernel, frame, pad, nf, kb)...  6.52 us
    ppermute x2, starting transfers between devices, shards(): other = lax.ppermute(sums, 'freq', [(s, s ^ 1 << i) for s in range(nz)])  5.87 us
  transfers between devices with their start and end apart: 38, of which 8 were waited for; matrix products, arithmetic and copies ran while one was open for 1% of the time, Pallas kernels for 30%

profile of v2, /device:TPU:0, one launch (start us, length us, event | category | flops | bytes accessed | tf_op | source)
XLA Modules:
  0.0 256.9 jit_solution(2460652303557955764)
XLA Ops:
  0.0 1.6 moments.1
  1.6 3.1 %collective-permute-start = (f32[13,16,128]{2,1,0:T(8,128)}, f32[13,16,128]{2,1,0:T(8,128)S(1)}, u32[]{:S(2)}, u32[]{:S(2)}) collective-permute-start(f32[13,16,128]{2,1,0:T(8,128)} %moments.1), channel_id=1, source_target_pairs={{0,1},{1,0},{2,3},{3,2},{4,5},{5,4},{6,7},{7,6},{8,9},{9,8},{10,11... | collective-permute-start | bytes 319496 | tf_op jit(solution)/shard_map/ppermute | solution.py:338
  4.7 3.2 %collective-permute-done = f32[13,16,128]{2,1,0:T(8,128)S(1)} collective-permute-done((f32[13,16,128]{2,1,0:T(8,128)}, f32[13,16,128]{2,1,0:T(8,128)S(1)}, u32[]{:S(2)}, u32[]{:S(2)}) %collective-permute-start) | collective-permute-done | bytes 106528 | tf_op jit(solution)/shard_map/ppermute | solution.py:338
  8.8 2.8 %collective-permute-start.1 = (f32[13,16,128]{2,1,0:T(8,128)S(1)}, f32[13,16,128]{2,1,0:T(8,128)S(1)}, u32[]{:S(2)}, u32[]{:S(2)}) collective-permute-start(f32[13,16,128]{2,1,0:T(8,128)S(1)} %add.3.one_ref), channel_id=1, source_target_pairs={{0,2},{1,3},{2,0},{3,1},{4,6},{5,7},{6,4},{7,5},{8,10},{9,11},{10,... | collective-permute-start | bytes 319496 | tf_op jit(solution)/shard_map/ppermute | solution.py:338
  12.3 2.7 %rowphases.1 = (bf16[2,4,192,128]{3,2,1,0:T(8,128)(2,1)S(1)}, bf16[768,512]{1,0:T(8,128)(2,1)S(1)}, bf16[384,384]{1,0:T(8,128)(2,1)S(1)}) custom-call(s32[2,4]{1,0:T(2,128)S(1)} %bitcast.14), custom_call_target="tpu_custom_call" | custom-call | tf_op jit(solution)/shard_map/rowphases/pallas_call | solution.py:311
  17.3 2.7 %colphases.1 = bf16[16,128,768]{2,1,0:T(8,128)(2,1)S(1)} custom-call(s32[2,4]{1,0:T(2,128)S(1)} %bitcast.15), custom_call_target="tpu_custom_call" | custom-call | tf_op jit(solution)/shard_map/colphases/pallas_call | solution.py:323
  21.3 1.6 solve.1
  22.9 10.0 %all-gather = bf16[104,16,128]{2,1,0:T(8,128)(2,1)S(1)} all-gather(bf16[13,16,128]{2,1,0:T(8,128)(2,1)} %solve.1), channel_id=2, replica_groups=mesh['facet'=8,'freq'=4] {'facet'}, dimensions={0}, use_global_device_ids=true | all-gather | bytes 479232 | tf_op jit(solution)/shard_map/all_gather | solution.py:346
  33.1 7.8 %rows.9 = (bf16[1,192,512]{2,1,0:T(8,128)(2,1)S(1)}, bf16[1,192,512]{2,1,0:T(8,128)(2,1)S(1)}, bf16[1,192,512]{2,1,0:T(8,128)(2,1)S(1)}, bf16[1,192,512]{2,1,0:T...) custom-call(s32[8]{0:T(128)S(1)} %fusion.psf_of_ref, ...), custom_call_target="tpu_custom_call" | custom-call | flops 2415919104 | bytes 5898240 | tf_op jit(solution)/shard_map/rows/pallas_call | solution.py:363
  44.1 7.6 %rows.8 = (bf16[1,192,512]{2,1,0:T(8,128)(2,1)S(1)}, bf16[1,192,512]{2,1,0:T(8,128)(2,1)S(1)}, bf16[1,192,512]{2,1,0:T(8,128)(2,1)S(1)}, bf16[1,192,512]{2,1,0:T...) custom-call(s32[8]{0:T(128)S(1)} %fusion.psf_of_ref, ...), custom_call_target="tpu_custom_call" | custom-call | flops 2415919104 | bytes 5898240 | tf_op jit(solution)/shard_map/rows/pallas_call | solution.py:363
  56.8 10.0 %collective-permute-done.35.refs_5_ = bf16[1,192,512]{2,1,0:T(8,128)(2,1)S(1)} collective-permute-done((bf16[1,192,512]{2,1,0:T(8,128)(2,1)S(1)}, bf16[1,192,512]{2,1,0:T(8,128)(2,1)S(1)}, u32[]{:S(2)}, u32[]{:S(2)}) %collective-permute-start.35) | collective-permute-done | bytes 196640 | tf_op jit(solution)/shard_map/ppermute | solution.py:402
  69.2 1.5 collective-permute-start.29
  70.7 13.0 %rows.7 = (bf16[2,192,512]{2,1,0:T(8,128)(2,1)S(1)}, bf16[2,192,512]{2,1,0:T(8,128)(2,1)S(1)}, bf16[2,192,512]{2,1,0:T(8,128)(2,1)S(1)}, bf16[2,192,512]{2,1,0:T...) custom-call(s32[8]{0:T(128)S(1)} %fusion.psf_of_ref, ...), custom_call_target="tpu_custom_call" | custom-call | flops 4831838208 | bytes 8650752 | tf_op jit(solution)/shard_map/rows/pallas_call | solution.py:363
  87.9 1.7 collective-permute-start.2
  91.3 42.0 %collective-permute-done.30.refs_7_ = bf16[1,192,512]{2,1,0:T(8,128)(2,1)S(1)} collective-permute-done((bf16[1,192,512]{2,1,0:T(8,128)(2,1)S(1)}, bf16[1,192,512]{2,1,0:T(8,128)(2,1)S(1)}, u32[]{:S(2)}, u32[]{:S(2)}) %collective-permute-start.30) | collective-permute-done | bytes 196640 | tf_op jit(solution)/shard_map/ppermute | solution.py:402
  137.5 1.5 collective-permute-start.22
  140.6 14.0 %rows.6 = (bf16[2,192,512]{2,1,0:T(8,128)(2,1)S(1)}, bf16[2,192,512]{2,1,0:T(8,128)(2,1)S(1)}, bf16[2,192,512]{2,1,0:T(8,128)(2,1)S(1)}, bf16[2,192,512]{2,1,0:T...) custom-call(s32[8]{0:T(128)S(1)} %fusion.psf_of_ref, ...), custom_call_target="tpu_custom_call" | custom-call | flops 4831838208 | bytes 8650752 | tf_op jit(solution)/shard_map/rows/pallas_call | solution.py:363
  154.6 8.2 %collective-permute-done.20.refs_4_ = bf16[2,192,512]{2,1,0:T(8,128)(2,1)S(1)} collective-permute-done((bf16[2,192,512]{2,1,0:T(8,128)(2,1)S(1)}, bf16[2,192,512]{2,1,0:T(8,128)(2,1)S(1)}, u32[]{:S(2)}, u32[]{:S(2)}) %collective-permute-start.20) | collective-permute-done | bytes 393248 | tf_op jit(solution)/shard_map/ppermute | solution.py:402
  162.8 7.9 %collective-permute-done.21.refs_5_ = bf16[2,192,512]{2,1,0:T(8,128)(2,1)S(1)} collective-permute-done((bf16[2,192,512]{2,1,0:T(8,128)(2,1)S(1)}, bf16[2,192,512]{2,1,0:T(8,128)(2,1)S(1)}, u32[]{:S(2)}, u32[]{:S(2)}) %collective-permute-start.21) | collective-permute-done | bytes 393248 | tf_op jit(solution)/shard_map/ppermute | solution.py:402
  174.9 7.7 %collective-permute-done.11.refs_2_ = bf16[2,192,512]{2,1,0:T(8,128)(2,1)S(1)} collective-permute-done((bf16[2,192,512]{2,1,0:T(8,128)(2,1)S(1)}, bf16[2,192,512]{2,1,0:T(8,128)(2,1)S(1)}, u32[]{:S(2)}, u32[]{:S(2)}) %collective-permute-start.11) | collective-permute-done | bytes 393248 | tf_op jit(solution)/shard_map/ppermute | solution.py:402
  184.9 14.6 %rows.5 = (bf16[2,112,512]{2,1,0:T(8,128)(2,1)S(1)}, bf16[2,112,512]{2,1,0:T(8,128)(2,1)}, bf16[2,112,512]{2,1,0:T(8,128)(2,1)}, bf16[2,112,512]{2,1,0:T(8,128)(...) custom-call(s32[8]{0:T(128)S(1)} %fusion.psf_of_ref, ...), custom_call_target="tpu_custom_call" | custom-call | flops 3221225472 | bytes 7340032 | tf_op jit(solution)/shard_map/rows/pallas_call | solution.py:363
  204.4 1.6 collective-permute-start.3
  207.5 4.0 %pixphases.3.refs_8_ = bf16[512,1536]{1,0:T(8,128)(2,1)} custom-call(), custom_call_target="tpu_custom_call" | custom-call | tf_op jit(solution)/shard_map/pixphases/pallas_call | solution.py:351
  211.5 2.5 pixphases.2.refs_8_
  222.9 3.3 %pixels.5.refs_10_ = f32[8,1,512,512]{3,2,1,0:T(8,128)} custom-call(bf16[1,192,512]{2,1,0:T(8,128)(2,1)S(1)} %copy-done.33, bf16[1,192,512]{2,1,0:T(8,128)(2,1)S(1)} %copy-done.35, bf16[1,192,512]{2,1,0:T(8,128)(2,1)S(1)} %copy-done.37, bf16[1,192,512]{2,1,0:T(8,128)(2,1)S(1)} %copy-done.39, bf16[1,192,512]{2,1,0:T(8,128)(2,1)S(1)} %copy-done.41, ...), custom_call_target="tpu_custom_call" | custom-call | flops 805306368 | bytes 3670016 | tf_op jit(solution)/shard_map/pixels/pallas_call | solution.py:408
  226.4 3.4 %pixels.6.refs_10_ = f32[8,1,512,512]{3,2,1,0:T(8,128)} custom-call(bf16[1,192,512]{2,1,0:T(8,128)(2,1)S(1)} %copy-done.43, bf16[1,192,512]{2,1,0:T(8,128)(2,1)S(1)} %copy-done.51, bf16[1,192,512]{2,1,0:T(8,128)(2,1)S(1)} %copy-done.53, bf16[1,192,512]{2,1,0:T(8,128)(2,1)S(1)} %copy-done.55, ...), custom_call_target="tpu_custom_call", output_to_operand_aliasing={{}: (10, {})} | custom-call | flops 805306368 | bytes 3670016 | tf_op jit(solution)/shard_map/pixels/pallas_call | solution.py:408
  232.5 1.5 collective-permute-start.8
  234.9 4.3 %pixels.7.refs_10_ = f32[8,1,512,512]{3,2,1,0:T(8,128)} custom-call(bf16[2,192,512]{2,1,0:T(8,128)(2,1)S(1)} %get-tuple-element.67.refs_0_, bf16[2,192,512]{2,1,0:T(8,128)(2,1)S(1)} %copy-done.7, bf16[2,192,512]{2,1,0:T(8,128)(2,1)S(1)} %copy-done.9, bf16[2,192,512]{2,1,0:T(8,128)(2,1)S(1)} %copy-done.11, ...), custom_call_target="tpu_custom_call", output_to_operand_aliasing={{}: (10, {})} | custom-call | flops 1610612736 | bytes 7340032 | tf_op jit(solution)/shard_map/pixels/pallas_call | solution.py:408
  239.3 4.6 %pixels.8.refs_10_ = f32[8,1,512,512]{3,2,1,0:T(8,128)} custom-call(bf16[2,192,512]{2,1,0:T(8,128)(2,1)S(1)} %copy-done.21, bf16[2,192,512]{2,1,0:T(8,128)(2,1)S(1)} %copy-done.23, bf16[2,192,512]{2,1,0:T(8,128)(2,1)S(1)} %copy-done.25, bf16[2,192,512]{2,1,0:T(8,128)(2,1)S(1)} %copy-done.27, ...), custom_call_target="tpu_custom_call", output_to_operand_aliasing={{}: (10, {})} | custom-call | flops 1610612736 | bytes 7340032 | tf_op jit(solution)/shard_map/pixels/pallas_call | solution.py:408
  243.9 4.8 %collective-permute-done.6.refs_4_ = bf16[2,112,512]{2,1,0:T(8,128)(2,1)S(1)} collective-permute-done((bf16[2,112,512]{2,1,0:T(8,128)(2,1)S(1)}, bf16[2,112,512]{2,1,0:T(8,128)(2,1)S(1)}, u32[]{:S(2)}, u32[]{:S(2)}) %collective-permute-start.6) | collective-permute-done | bytes 229408 | tf_op jit(solution)/shard_map/ppermute | solution.py:402
  248.7 4.5 %collective-permute-done.7.refs_5_ = bf16[2,112,512]{2,1,0:T(8,128)(2,1)S(1)} collective-permute-done((bf16[2,112,512]{2,1,0:T(8,128)(2,1)S(1)}, bf16[2,112,512]{2,1,0:T(8,128)(2,1)S(1)}, u32[]{:S(2)}, u32[]{:S(2)}) %collective-permute-start.7) | collective-permute-done | bytes 229408 | tf_op jit(solution)/shard_map/ppermute | solution.py:402
  253.2 3.7 %pixels.9 = f32[8,1,512,512]{3,2,1,0:T(8,128)} custom-call(bf16[2,112,512]{2,1,0:T(8,128)(2,1)S(1)} %copy-done.31, bf16[2,112,512]{2,1,0:T(8,128)(2,1)S(1)} %collective-permute-done.3.refs_1_, bf16[2,112,512]{2,1,0:T(8,128)(2,1)S(1)} %collective-permute-done.4.refs_2_, ...), custom_call_target="tpu_custom_call", output_to_operand_aliasing={{}: (10, {})} | custom-call | flops 939524096 | bytes 6029312 | tf_op jit(solution)/shard_map/pixels/pallas_call | solution.py:408
  (218 shorter events, 52.4 us)
Async XLA Ops:
  41.3 12.6 %collective-permute-start.32 = (bf16[1,192,512]{2,1,0:T(8,128)(2,1)S(1)}, bf16[1,192,512]{2,1,0:T(8,128)(2,1)S(1)}, u32[]{:S(2)}, u32[]{:S(2)}) collective-permute-start(bf16[1,192,512]{2,1,0:T(8,128)(2,1)S(1)} %get-tuple-element.85), channel_id=1, source_target_pairs={{0,8},{4,12},{8,0},{12,4},{16,24},{20,28},{24,16},{28,20},{1,9},{5... | collective-permute-start | bytes 589832 | tf_op jit(solution)/shard_map/ppermute | solution.py:402
  42.9 12.7 %collective-permute-start.34 = (bf16[1,192,512]{2,1,0:T(8,128)(2,1)S(1)}, bf16[1,192,512]{2,1,0:T(8,128)(2,1)S(1)}, u32[]{:S(2)}, u32[]{:S(2)}) collective-permute-start(bf16[1,192,512]{2,1,0:T(8,128)(2,1)S(1)} %get-tuple-element.87), channel_id=1, source_target_pairs={{0,16},{4,20},{8,24},{12,28},{16,0},{20,4},{24,8},{28,12},{1,17},{... | collective-permute-start | bytes 589832 | tf_op jit(solution)/shard_map/ppermute | solution.py:402
  51.7 15.2 %collective-permute-start.35 = (bf16[1,192,512]{2,1,0:T(8,128)(2,1)S(1)}, bf16[1,192,512]{2,1,0:T(8,128)(2,1)S(1)}, u32[]{:S(2)}, u32[]{:S(2)}) collective-permute-start(bf16[1,192,512]{2,1,0:T(8,128)(2,1)S(1)} %get-tuple-element.88), channel_id=1, source_target_pairs={{0,20},{4,16},{8,28},{12,24},{16,4},{20,0},{24,12},{28,8},{1,21},{... | collective-permute-start | bytes 589832 | tf_op jit(solution)/shard_map/ppermute | solution.py:402
  52.5 15.3 %collective-permute-start.36 = (bf16[1,192,512]{2,1,0:T(8,128)(2,1)S(1)}, bf16[1,192,512]{2,1,0:T(8,128)(2,1)S(1)}, u32[]{:S(2)}, u32[]{:S(2)}) collective-permute-start(bf16[1,192,512]{2,1,0:T(8,128)(2,1)S(1)} %get-tuple-element.89), channel_id=1, source_target_pairs={{0,24},{4,28},{8,16},{12,20},{16,8},{20,12},{24,0},{28,4},{1,25},{... | collective-permute-start | bytes 589832 | tf_op jit(solution)/shard_map/ppermute | solution.py:402
  53.9 15.2 %collective-permute-start.37 = (bf16[1,192,512]{2,1,0:T(8,128)(2,1)S(1)}, bf16[1,192,512]{2,1,0:T(8,128)(2,1)S(1)}, u32[]{:S(2)}, u32[]{:S(2)}) collective-permute-start(bf16[1,192,512]{2,1,0:T(8,128)(2,1)S(1)} %get-tuple-element.90), channel_id=1, source_target_pairs={{0,28},{4,24},{8,20},{12,16},{16,12},{20,8},{24,4},{28,0},{1,29},{... | collective-permute-start | bytes 589832 | tf_op jit(solution)/shard_map/ppermute | solution.py:402
  54.9 14.2 %collective-permute-start.24 = (bf16[1,192,512]{2,1,0:T(8,128)(2,1)S(1)}, bf16[1,192,512]{2,1,0:T(8,128)(2,1)S(1)}, u32[]{:S(2)}, u32[]{:S(2)}) collective-permute-start(bf16[1,192,512]{2,1,0:T(8,128)(2,1)S(1)} %get-tuple-element.76), channel_id=1, source_target_pairs={{0,4},{4,0},{8,12},{12,8},{16,20},{20,16},{24,28},{28,24},{1,5},{5... | collective-permute-start | bytes 589832 | tf_op jit(solution)/shard_map/ppermute | solution.py:402
  55.6 28.2 %collective-permute-start.25 = (bf16[1,192,512]{2,1,0:T(8,128)(2,1)S(1)}, bf16[1,192,512]{2,1,0:T(8,128)(2,1)S(1)}, u32[]{:S(2)}, u32[]{:S(2)}) collective-permute-start(bf16[1,192,512]{2,1,0:T(8,128)(2,1)S(1)} %get-tuple-element.77), channel_id=1, source_target_pairs={{0,8},{4,12},{8,0},{12,4},{16,24},{20,28},{24,16},{28,20},{1,9},{5... | collective-permute-start | bytes 589832 | tf_op jit(solution)/shard_map/ppermute | solution.py:402
  66.8 17.6 %collective-permute-start.26 = (bf16[1,192,512]{2,1,0:T(8,128)(2,1)S(1)}, bf16[1,192,512]{2,1,0:T(8,128)(2,1)S(1)}, u32[]{:S(2)}, u32[]{:S(2)}) collective-permute-start(bf16[1,192,512]{2,1,0:T(8,128)(2,1)S(1)} %get-tuple-element.78), channel_id=1, source_target_pairs={{0,12},{4,8},{8,4},{12,0},{16,28},{20,24},{24,20},{28,16},{1,13},{... | collective-permute-start | bytes 589832 | tf_op jit(solution)/shard_map/ppermute | solution.py:402
  67.9 17.8 %collective-permute-start.27 = (bf16[1,192,512]{2,1,0:T(8,128)(2,1)S(1)}, bf16[1,192,512]{2,1,0:T(8,128)(2,1)S(1)}, u32[]{:S(2)}, u32[]{:S(2)}) collective-permute-start(bf16[1,192,512]{2,1,0:T(8,128)(2,1)S(1)} %get-tuple-element.79), channel_id=1, source_target_pairs={{0,16},{4,20},{8,24},{12,28},{16,0},{20,4},{24,8},{28,12},{1,17},{... | collective-permute-start | bytes 589832 | tf_op jit(solution)/shard_map/ppermute | solution.py:402
  69.1 18.1 %collective-permute-start.28 = (bf16[1,192,512]{2,1,0:T(8,128)(2,1)S(1)}, bf16[1,192,512]{2,1,0:T(8,128)(2,1)S(1)}, u32[]{:S(2)}, u32[]{:S(2)}) collective-permute-start(bf16[1,192,512]{2,1,0:T(8,128)(2,1)S(1)} %get-tuple-element.80), channel_id=1, source_target_pairs={{0,20},{4,16},{8,28},{12,24},{16,4},{20,0},{24,12},{28,8},{1,21},{... | collective-permute-start | bytes 589832 | tf_op jit(solution)/shard_map/ppermute | solution.py:402
  69.2 20.5 %collective-permute-start.29 = (bf16[1,192,512]{2,1,0:T(8,128)(2,1)S(1)}, bf16[1,192,512]{2,1,0:T(8,128)(2,1)S(1)}, u32[]{:S(2)}, u32[]{:S(2)}) collective-permute-start(bf16[1,192,512]{2,1,0:T(8,128)(2,1)S(1)} %get-tuple-element.81), channel_id=1, source_target_pairs={{0,24},{4,28},{8,16},{12,20},{16,8},{20,12},{24,0},{28,4},{1,25},{... | collective-permute-start | bytes 589832 | tf_op jit(solution)/shard_map/ppermute | solution.py:402
  83.8 50.9 %collective-permute-start.17 = (bf16[2,192,512]{2,1,0:T(8,128)(2,1)S(1)}, bf16[2,192,512]{2,1,0:T(8,128)(2,1)S(1)}, u32[]{:S(2)}, u32[]{:S(2)}) collective-permute-start(bf16[2,192,512]{2,1,0:T(8,128)(2,1)S(1)} %get-tuple-element.68), channel_id=1, source_target_pairs={{0,4},{4,0},{8,12},{12,8},{16,20},{20,16},{24,28},{28,24},{1,5},{5... | collective-permute-start | bytes 1179656 | tf_op jit(solution)/shard_map/ppermute | solution.py:402
  84.5 52.3 %collective-permute-start.18 = (bf16[2,192,512]{2,1,0:T(8,128)(2,1)S(1)}, bf16[2,192,512]{2,1,0:T(8,128)(2,1)S(1)}, u32[]{:S(2)}, u32[]{:S(2)}) collective-permute-start(bf16[2,192,512]{2,1,0:T(8,128)(2,1)S(1)} %get-tuple-element.69), channel_id=1, source_target_pairs={{0,8},{4,12},{8,0},{12,4},{16,24},{20,28},{24,16},{28,20},{1,9},{5... | collective-permute-start | bytes 1179656 | tf_op jit(solution)/shard_map/ppermute | solution.py:402
  85.7 53.3 %collective-permute-start.19 = (bf16[2,192,512]{2,1,0:T(8,128)(2,1)S(1)}, bf16[2,192,512]{2,1,0:T(8,128)(2,1)S(1)}, u32[]{:S(2)}, u32[]{:S(2)}) collective-permute-start(bf16[2,192,512]{2,1,0:T(8,128)(2,1)S(1)} %get-tuple-element.70), channel_id=1, source_target_pairs={{0,12},{4,8},{8,4},{12,0},{16,28},{20,24},{24,20},{28,16},{1,13},{... | collective-permute-start | bytes 1179656 | tf_op jit(solution)/shard_map/ppermute | solution.py:402
  87.9 96.9 %collective-permute-start.2 = (bf16[4,2,2,48,768]{4,3,2,1,0:T(8,128)(2,1)S(1)}, bf16[4,2,2,48,768]{4,3,2,1,0:T(8,128)(2,1)S(1)}, u32[]{:S(2)}, u32[]{:S(2)}) collective-permute-start(bf16[4,2,2,48,768]{4,3,2,1,0:T(8,128)(2,1)S(1)} %slice.7), channel_id=1, source_target_pairs={{0,28},{4,24},{8,20},{12,16},{16,12},{20,8},{24,4},{28,0},{1,29},{... | collective-permute-start | bytes 3538952 | tf_op jit(solution)/shard_map/ppermute | solution.py:301
  90.3 42.9 %collective-permute-start.30 = (bf16[1,192,512]{2,1,0:T(8,128)(2,1)S(1)}, bf16[1,192,512]{2,1,0:T(8,128)(2,1)S(1)}, u32[]{:S(2)}, u32[]{:S(2)}) collective-permute-start(bf16[1,192,512]{2,1,0:T(8,128)(2,1)S(1)} %get-tuple-element.82), channel_id=1, source_target_pairs={{0,28},{4,24},{8,20},{12,16},{16,12},{20,8},{24,4},{28,0},{1,29},{... | collective-permute-start | bytes 589832 | tf_op jit(solution)/shard_map/ppermute | solution.py:402
  133.9 28.8 %collective-permute-start.20 = (bf16[2,192,512]{2,1,0:T(8,128)(2,1)S(1)}, bf16[2,192,512]{2,1,0:T(8,128)(2,1)S(1)}, u32[]{:S(2)}, u32[]{:S(2)}) collective-permute-start(bf16[2,192,512]{2,1,0:T(8,128)(2,1)S(1)} %get-tuple-element.71), channel_id=1, source_target_pairs={{0,16},{4,20},{8,24},{12,28},{16,0},{20,4},{24,8},{28,12},{1,17},{... | collective-permute-start | bytes 1179656 | tf_op jit(solution)/shard_map/ppermute | solution.py:402
  135.5 35.1 %collective-permute-start.21 = (bf16[2,192,512]{2,1,0:T(8,128)(2,1)S(1)}, bf16[2,192,512]{2,1,0:T(8,128)(2,1)S(1)}, u32[]{:S(2)}, u32[]{:S(2)}) collective-permute-start(bf16[2,192,512]{2,1,0:T(8,128)(2,1)S(1)} %get-tuple-element.72), channel_id=1, source_target_pairs={{0,20},{4,16},{8,28},{12,24},{16,4},{20,0},{24,12},{28,8},{1,21},{... | collective-permute-start | bytes 1179656 | tf_op jit(solution)/shard_map/ppermute | solution.py:402
  137.5 33.9 %collective-permute-start.22 = (bf16[2,192,512]{2,1,0:T(8,128)(2,1)S(1)}, bf16[2,192,512]{2,1,0:T(8,128)(2,1)S(1)}, u32[]{:S(2)}, u32[]{:S(2)}) collective-permute-start(bf16[2,192,512]{2,1,0:T(8,128)(2,1)S(1)} %get-tuple-element.73), channel_id=1, source_target_pairs={{0,24},{4,28},{8,16},{12,20},{16,8},{20,12},{24,0},{28,4},{1,25},{... | collective-permute-start | bytes 1179656 | tf_op jit(solution)/shard_map/ppermute | solution.py:402
  139.7 32.4 %collective-permute-start.23 = (bf16[2,192,512]{2,1,0:T(8,128)(2,1)S(1)}, bf16[2,192,512]{2,1,0:T(8,128)(2,1)S(1)}, u32[]{:S(2)}, u32[]{:S(2)}) collective-permute-start(bf16[2,192,512]{2,1,0:T(8,128)(2,1)S(1)} %get-tuple-element.74), channel_id=1, source_target_pairs={{0,28},{4,24},{8,20},{12,16},{16,12},{20,8},{24,4},{28,0},{1,29},{... | collective-permute-start | bytes 1179656 | tf_op jit(solution)/shard_map/ppermute | solution.py:402
  171.4 32.2 %collective-permute-start.12 = (bf16[2,192,512]{2,1,0:T(8,128)(2,1)S(1)}, bf16[2,192,512]{2,1,0:T(8,128)(2,1)S(1)}, u32[]{:S(2)}, u32[]{:S(2)}) collective-permute-start(bf16[2,192,512]{2,1,0:T(8,128)(2,1)S(1)} %get-tuple-element.62), channel_id=1, source_target_pairs={{0,12},{4,8},{8,4},{12,0},{16,28},{20,24},{24,20},{28,16},{1,13},{... | collective-permute-start | bytes 1179656 | tf_op jit(solution)/shard_map/ppermute | solution.py:402
  172.1 33.9 %collective-permute-start.13 = (bf16[2,192,512]{2,1,0:T(8,128)(2,1)S(1)}, bf16[2,192,512]{2,1,0:T(8,128)(2,1)S(1)}, u32[]{:S(2)}, u32[]{:S(2)}) collective-permute-start(bf16[2,192,512]{2,1,0:T(8,128)(2,1)S(1)} %get-tuple-element.63), channel_id=1, source_target_pairs={{0,16},{4,20},{8,24},{12,28},{16,0},{20,4},{24,8},{28,12},{1,17},{... | collective-permute-start | bytes 1179656 | tf_op jit(solution)/shard_map/ppermute | solution.py:402
  173.7 56.1 %collective-permute-start.14 = (bf16[2,192,512]{2,1,0:T(8,128)(2,1)}, bf16[2,192,512]{2,1,0:T(8,128)(2,1)}, u32[]{:S(2)}, u32[]{:S(2)}) collective-permute-start(bf16[2,192,512]{2,1,0:T(8,128)(2,1)} %get-tuple-element.64), channel_id=1, source_target_pairs={{0,20},{4,16},{8,28},{12,24},{16,4},{20,0},{24,12},{28,8},{1,21},{... | collective-permute-start | bytes 1179656 | tf_op jit(solution)/shard_map/ppermute | solution.py:402
  183.4 47.0 %collective-permute-start.15 = (bf16[2,192,512]{2,1,0:T(8,128)(2,1)}, bf16[2,192,512]{2,1,0:T(8,128)(2,1)}, u32[]{:S(2)}, u32[]{:S(2)}) collective-permute-start(bf16[2,192,512]{2,1,0:T(8,128)(2,1)} %get-tuple-element.65), channel_id=1, source_target_pairs={{0,24},{4,28},{8,16},{12,20},{16,8},{20,12},{24,0},{28,4},{1,25},{... | collective-permute-start | bytes 1179656 | tf_op jit(solution)/shard_map/ppermute | solution.py:402
  184.9 46.3 %collective-permute-start.16 = (bf16[2,192,512]{2,1,0:T(8,128)(2,1)}, bf16[2,192,512]{2,1,0:T(8,128)(2,1)}, u32[]{:S(2)}, u32[]{:S(2)}) collective-permute-start(bf16[2,192,512]{2,1,0:T(8,128)(2,1)} %get-tuple-element.66), channel_id=1, source_target_pairs={{0,28},{4,24},{8,20},{12,16},{16,12},{20,8},{24,4},{28,0},{1,29},{... | collective-permute-start | bytes 1179656 | tf_op jit(solution)/shard_map/ppermute | solution.py:402
  204.4 28.1 %collective-permute-start.3 = (bf16[2,112,512]{2,1,0:T(8,128)(2,1)}, bf16[2,112,512]{2,1,0:T(8,128)(2,1)S(1)}, u32[]{:S(2)}, u32[]{:S(2)}) collective-permute-start(bf16[2,112,512]{2,1,0:T(8,128)(2,1)} %get-tuple-element.52), channel_id=1, source_target_pairs={{0,4},{4,0},{8,12},{12,8},{16,20},{20,16},{24,28},{28,24},{1,5},{5... | collective-permute-start | bytes 688136 | tf_op jit(solution)/shard_map/ppermute | solution.py:402
  206.8 27.2 %collective-permute-start.4 = (bf16[2,112,512]{2,1,0:T(8,128)(2,1)}, bf16[2,112,512]{2,1,0:T(8,128)(2,1)S(1)}, u32[]{:S(2)}, u32[]{:S(2)}) collective-permute-start(bf16[2,112,512]{2,1,0:T(8,128)(2,1)} %get-tuple-element.53), channel_id=1, source_target_pairs={{0,8},{4,12},{8,0},{12,4},{16,24},{20,28},{24,16},{28,20},{1,9},{5... | collective-permute-start | bytes 688136 | tf_op jit(solution)/shard_map/ppermute | solution.py:402
  229.8 14.1 %collective-permute-start.5 = (bf16[2,112,512]{2,1,0:T(8,128)(2,1)S(1)}, bf16[2,112,512]{2,1,0:T(8,128)(2,1)S(1)}, u32[]{:S(2)}, u32[]{:S(2)}) collective-permute-start(bf16[2,112,512]{2,1,0:T(8,128)(2,1)S(1)} %copy-done.74), channel_id=1, source_target_pairs={{0,12},{4,8},{8,4},{12,0},{16,28},{20,24},{24,20},{28,16},{1,13},{... | collective-permute-start | bytes 688136 | tf_op jit(solution)/shard_map/ppermute | solution.py:402
  230.4 18.3 %collective-permute-start.6 = (bf16[2,112,512]{2,1,0:T(8,128)(2,1)S(1)}, bf16[2,112,512]{2,1,0:T(8,128)(2,1)S(1)}, u32[]{:S(2)}, u32[]{:S(2)}) collective-permute-start(bf16[2,112,512]{2,1,0:T(8,128)(2,1)S(1)} %copy-done.72), channel_id=1, source_target_pairs={{0,16},{4,20},{8,24},{12,28},{16,0},{20,4},{24,8},{28,12},{1,17},{... | collective-permute-start | bytes 688136 | tf_op jit(solution)/shard_map/ppermute | solution.py:402
  231.2 22.0 %collective-permute-start.7 = (bf16[2,112,512]{2,1,0:T(8,128)(2,1)S(1)}, bf16[2,112,512]{2,1,0:T(8,128)(2,1)S(1)}, u32[]{:S(2)}, u32[]{:S(2)}) collective-permute-start(bf16[2,112,512]{2,1,0:T(8,128)(2,1)S(1)} %copy-done.70), channel_id=1, source_target_pairs={{0,20},{4,16},{8,28},{12,24},{16,4},{20,0},{24,12},{28,8},{1,21},{... | collective-permute-start | bytes 688136 | tf_op jit(solution)/shard_map/ppermute | solution.py:402
  232.5 20.7 %collective-permute-start.8 = (bf16[2,112,512]{2,1,0:T(8,128)(2,1)S(1)}, bf16[2,112,512]{2,1,0:T(8,128)(2,1)S(1)}, u32[]{:S(2)}, u32[]{:S(2)}) collective-permute-start(bf16[2,112,512]{2,1,0:T(8,128)(2,1)S(1)} %copy-done.68), channel_id=1, source_target_pairs={{0,24},{4,28},{8,16},{12,20},{16,8},{20,12},{24,0},{28,4},{1,25},{... | collective-permute-start | bytes 688136 | tf_op jit(solution)/shard_map/ppermute | solution.py:402
  234.0 19.2 %collective-permute-start.9 = (bf16[2,112,512]{2,1,0:T(8,128)(2,1)S(1)}, bf16[2,112,512]{2,1,0:T(8,128)(2,1)S(1)}, u32[]{:S(2)}, u32[]{:S(2)}) collective-permute-start(bf16[2,112,512]{2,1,0:T(8,128)(2,1)S(1)} %copy-done.66), channel_id=1, source_target_pairs={{0,28},{4,24},{8,20},{12,16},{16,12},{20,8},{24,4},{28,0},{1,29},{... | collective-permute-start | bytes 688136 | tf_op jit(solution)/shard_map/ppermute | solution.py:402
  (83 other events, 866.7 us)

commit v3 on v2

--- a/solution.py
+++ b/solution.py
@@ -134,7 +134,7 @@
     lax.fori_loop(0, FCOLS * ntile, columns, 0)
 
 
-def pixel_phases_kernel(frame, pad, nf, kb, out_ref):
+def pixel_phases_kernel(frame, pad, nf, kb, out_ref, cos_ref, sin_ref):
     me = lax.axis_index("facet")
     width = out_ref.shape[1]
     rows = width // nf
@@ -151,10 +151,14 @@
     shift = jnp.where(minus_sin, frame // 4, 0).astype(f32)
     k = (base + k).astype(f32)
     block = 64
+    grain = lane((block, 1), 0).astype(f32) * k
+    cos_ref[...] = cos_turn(grain, frame)
+    sin_ref[...] = cos_turn(grain - frame // 4, frame)
 
     def some(i, carry):
-        place = (pad + i * block + lane((block, 1), 0)).astype(f32)
-        out_ref[pl.ds(i * block, block)] = cos_turn(place * k + shift, frame).astype(bf16)
+        coarse = (pad + i * block).astype(f32) * k + shift
+        cos_i, sin_i = cos_turn(coarse, frame), cos_turn(coarse - frame // 4, frame)
+        out_ref[pl.ds(i * block, block)] = (cos_i * cos_ref[...] - sin_i * sin_ref[...]).astype(bf16)
         return carry
 
     lax.fori_loop(0, out_ref.shape[0] // block, some, 0)
@@ -183,29 +187,33 @@
                 for j in range(3)
             )
             model = (a0 + a1 * x + a2 * (x * x)).astype(bf16)
-            for a in range(na):
-                y = jnp.dot(row_ref[a, t], model, preferred_element_type=f32).astype(bf16)
-                start, cols = a * 2 * rb, slice(t * ts, (t + 1) * ts)
-                lhs_ref[start : start + rb, cols] = y[:rb]
-                lhs_ref[start + rb : start + 2 * rb, cols] = y[kb : kb + rb]
+            table = row_ref[:, t].reshape(na * 2 * kb, ts)
+            y = jnp.dot(table, model, preferred_element_type=f32).astype(bf16)
+            for part in range(2 * na):
+                lhs_ref[part * rb : (part + 1) * rb, t * ts : (t + 1) * ts] = y[part * kb : part * kb + rb]
         if paired:
             count = kb // 2
             i, m = lane((rb, count), 0), lane((rb, count), 1)
             mirror = jnp.where((i >= 1) & (i < count) & (m == count - i), 1.0, 0.0).astype(bf16)
-        for p in range(npsf):
-            for part in range(2):
-                psf = psf_ref[p, 0, part, :rb]
-                up, dn = psf[:, :half], turned(psf)
-                if paired:
-                    far = jnp.dot(mirror, far_ref[p, 0, part], preferred_element_type=f32).astype(bf16)
-                    far_up, far_dn = far[:, :half].astype(f32), turned(far)
-                    sign = 1.0 - 2.0 * part
-                    up = up.astype(f32) + sign * jnp.where(first, far_up, far_dn)
-                    dn = dn + sign * jnp.where(first, far_dn, far_up)
-                psf_up_ref[p, part] = up.astype(psf_up_ref.dtype)
-                psf_dn_ref[p, part] = dn.astype(psf_dn_ref.dtype)
-
-    both = jnp.dot(lhs_ref[...], col_ref[0], preferred_element_type=f32)
+        parts = 2 * npsf
+        psf = psf_ref[:, 0, :, :rb].reshape(parts * rb, frame)
+        up, dn = psf[:, :half], turned(psf)
+        if paired:
+            far = [
+                jnp.dot(mirror, far_ref[i // 2, 0, i % 2], preferred_element_type=f32).astype(bf16)
+                for i in range(parts)
+            ]
+            far = jnp.concatenate(far, axis=0)
+            far_up, far_dn = far[:, :half].astype(f32), turned(far)
+            for i in range(parts):
+                rows, sign = slice(i * rb, (i + 1) * rb), 1.0 - 2.0 * (i % 2)
+                psf_up_ref[i // 2, i % 2] = up[rows].astype(f32) + sign * jnp.where(first, far_up[rows], far_dn[rows])
+                psf_dn_ref[i // 2, i % 2] = dn[rows] + sign * jnp.where(first, far_dn[rows], far_up[rows])
+        else:
+            psf_up_ref[...] = up.reshape(psf_up_ref.shape)
+            psf_dn_ref[...] = dn.astype(bf16).reshape(psf_dn_ref.shape)
+
+    both = jnp.dot(lhs_ref[...], col_ref[step], preferred_element_type=f32)
     me = lax.axis_index("facet")
     zero = jnp.zeros((rb, half), f32)
     for a in range(na):
@@ -260,7 +268,7 @@
         left -= sizes[-1]
     paired = [False] * len(sizes)
     while npair:
-        sizes.append(min(2, npair))
+        sizes.append(1)
         npair -= sizes[-1]
         paired.append(True)
     return [(sum(sizes[:i]), n, paired[i]) for i, n in enumerate(sizes)]
@@ -295,12 +303,13 @@
     pad, half = (frame - fs) // 2, frame // 2
     total = nch * nz
     na = nf // FCOLS
-    npair, far = pairs_of(nch, nf, kb, frame), None
-
-    if npair:
-        far = lax.ppermute(
-            whole_psf[:, nch - npair :, :, kb // 2 :], "facet", [(s, nf - 1 - s) for s in range(nf)]
-        )
+    npair = pairs_of(nch, nf, kb, frame)
+
+    far = {}
+    for i in range(npair):
+        chan = nch - npair + i
+        mirror = [(s, nf - 1 - s) for s in range(nf)]
+        far[chan] = lax.ppermute(whole_psf[:, chan : chan + 1, :, kb // 2 :], "facet", mirror)
     sums = pl.pallas_call(
         functools.partial(moments_kernel, total),
         out_shape=jax.ShapeDtypeStruct((3 * ntile + 1, rows, ts), f32),
@@ -312,14 +321,19 @@
         functools.partial(row_phases_kernel, frame, fs),
         out_shape=[
             jax.ShapeDtypeStruct((na, ntile, 2 * kb, ts), bf16),
-            jax.ShapeDtypeStruct((frame, fs), bf16),
-            jax.ShapeDtypeStruct((half, half), bf16),
+            pltpu.HBM((frame, fs), bf16),
+            pltpu.HBM((half, half), bf16),
         ],
+        grid=(1,),
         in_specs=[SMEM],
-        out_specs=[VMEM] * 3,
+        out_specs=[
+            VMEM,
+            pl.BlockSpec((frame, fs), lambda i: (0, 0)),
+            pl.BlockSpec((half, half), lambda i: (0, 0)),
+        ],
         compiler_params=pltpu.CompilerParams(vmem_limit_bytes=SMALL_LIMIT),
         name="rowphases",
-    )(tile_pos.T)
+    )(in_hbm(tile_pos.T))
     col_table = pl.pallas_call(
         functools.partial(column_phases_kernel, frame, fs),
         out_shape=jax.ShapeDtypeStruct((FCOLS * ntile, ts, frame), bf16),
@@ -328,8 +342,7 @@
         scratch_shapes=[pltpu.VMEM((ts, frame), f32)] * 2,
         compiler_params=pltpu.CompilerParams(vmem_limit_bytes=SMALL_LIMIT),
         name="colphases",
-    )(tile_pos.T)
-    row_table, inv_table, flip = in_hbm(row_table), in_hbm(inv_table), in_hbm(flip)
+    )(in_hbm(tile_pos.T))
     col_table = col_table.reshape(FCOLS, ntile * ts, frame)
     other = jnp.zeros_like(sums)
     for i in range(nz.bit_length() - 1):
@@ -352,6 +365,7 @@
             functools.partial(pixel_phases_kernel, frame, pad, nf, kb),
             out_shape=jax.ShapeDtypeStruct((fs, nf * (block_pair if paired else 2 * kb)), bf16),
             out_specs=VMEM,
+            scratch_shapes=[pltpu.VMEM((64, nf * (block_pair if paired else 2 * kb)), f32)] * 2,
             name="pixphases",
         )()
 
@@ -359,24 +373,23 @@
     for chan0, count, paired in chunks_of(nch, npair):
         rb, block = (rb_pair, block_pair) if paired else (kb, 2 * kb)
         psf_type = f32 if paired else bf16
-        fixed = lambda *shape: pl.BlockSpec(shape, lambda c, b, s: (0,) * len(shape))
         w = pl.pallas_call(
             functools.partial(rows_kernel, total, nch, chan0, paired),
             grid_spec=pltpu.PrefetchScalarGridSpec(
                 num_scalar_prefetch=1,
                 grid=(count, FCOLS),
                 in_specs=[
-                    fixed(nf, 3 * ntile + 1, rows, ts),
-                    fixed(na, ntile, 2 * kb, ts),
-                    pl.BlockSpec((1, ntile * ts, frame), lambda c, b, s: (b, 0, 0)),
-                    fixed(frame, fs),
-                    fixed(half, half),
+                    VMEM,
+                    VMEM,
+                    VMEM,
+                    pl.BlockSpec((frame, fs), lambda c, b, s: (0, 0)),
+                    pl.BlockSpec((half, half), lambda c, b, s: (0, 0)),
                     pl.BlockSpec((npsf, 1, 2, kb, frame), lambda c, b, s, c0=chan0: (0, c0 + c, 0, 0, 0)),
                 ]
                 + [
                     pl.BlockSpec(
                         (npsf, 1, 2, kb // 2, frame),
-                        lambda c, b, s, c0=chan0 - (nch - npair): (0, c0 + c, 0, 0, 0),
+                        lambda c, b, s: (0, c, 0, 0, 0),
                     )
                 ]
                 * paired,
@@ -388,7 +401,7 @@
                     pltpu.VMEM((na * 2 * rb, frame), bf16),
                 ],
             ),
-            out_shape=[jax.ShapeDtypeStruct((count, block, fs), bf16)] * nf,
+            out_shape=[pltpu.HBM((count, block, fs), bf16)] * nf,
             cost_estimate=pl.CostEstimate(
                 flops=count * nf * 4 * rb * frame * (ntile * ts + fs),
                 bytes_accessed=count * (npsf * 4 * kb * frame + nf * 2 * block * fs) + 8 * ntile * ts * frame,
@@ -396,20 +409,20 @@
             ),
             compiler_params=pltpu.CompilerParams(vmem_limit_bytes=VMEM_LIMIT),
             name="rows",
-        )(psf_of, fit, row_table, col_table, inv_table, flip, psf_spectra, *([far] * paired))
+        )(psf_of, fit, row_table, col_table, in_hbm(inv_table), in_hbm(flip), psf_spectra, *([in_hbm(far[chan0])] if paired else []))
         got = list(w)
         for j in send_order(nf):
             got[j] = lax.ppermute(w[j], "facet", [(s, s ^ j) for s in range(nf)])
         pieces.append((chan0, count, block, tables[paired], got))
     result = None
-    for chan0, count, block, pix_table, got in pieces:
+    for n, (chan0, count, block, pix_table, got) in enumerate(pieces):
         image = pl.BlockSpec((1, 1, fs, fs), lambda c, c0=chan0: (c0 + c, 0, 0, 0))
         before = [] if result is None else [result]
         result = pl.pallas_call(
             functools.partial(pixels_kernel, nf, 1.0 / (frame * frame)),
             grid=(count,),
             in_specs=[pl.BlockSpec((1, block, fs), lambda c: (c, 0, 0))] * nf
-            + [pl.BlockSpec((fs, nf * block), lambda c: (0, 0)), image]
+            + [VMEM, image]
             + [pl.BlockSpec(memory_space=pl.ANY)] * len(before),
             out_specs=image,
             out_shape=jax.ShapeDtypeStruct(residual.shape, f32),
@@ -421,7 +434,7 @@
             ),
             compiler_params=pltpu.CompilerParams(vmem_limit_bytes=VMEM_LIMIT),
             name="pixels",
-        )(*got, pix_table, residual, *before)
+        )(*(got if n >= len(pieces) - 2 else map(in_hbm, got)), pix_table, residual, *before)
     return result
 
 

time: 258 us -> 227 us (0.88)
  waiting for transfers between devices: 88.4 us -> 58.9 us
  local copies, waits for them, and re-layouts: 25.5 us -> 4.21 us
  starting transfers between devices: 39.3 us -> 52.7 us
  Pallas kernels: 91.3 us -> 98.7 us
    ppermute x35 -> x42, waiting for transfers between devices: 85.2 us -> 55.7 us  [shards(): got[j] = lax.ppermute(w[j], 'facet', [(s, s ^ j) for s in range(nf)])]
    unnamed x154 -> x66, local copies, waits for them, and re-layouts: 24.1 us -> 2.88 us
    ppermute x35 -> x42, starting transfers between devices: 31.8 us -> 44.1 us  [shards(): got[j] = lax.ppermute(w[j], 'facet', [(s, s ^ j) for s in range(nf)])]
    pallas_call x5 -> x6, Pallas kernels: 57 us -> 61.1 us  [shards(): pl.pallas_call(functools.partial(rows_kernel, total, nch, chan0, paired),...]
    pallas_call x5 -> x6, Pallas kernels: 19.2 us -> 23.2 us  [shards(): pl.pallas_call(functools.partial(pixels_kernel, nf, 1.0 / (frame * frame)...]
  transfers between devices with their start and end apart: 38 -> 46, of which waited for: 8 -> 9; matrix products, arithmetic and copies ran while one was open for 1% -> 1% of each run, Pallas kernels for 30% -> 37%
where the time goes in v3:
time: 227 us
  Pallas kernels  98.7 us (43%)
  waiting for transfers between devices  58.9 us (26%)
  starting transfers between devices  52.7 us (23%)
  blocking collectives  9.97 us (4%)
  local copies, waits for them, and re-layouts  4.21 us (2%)
    pallas_call x6, Pallas kernels, shards(): pl.pallas_call(functools.partial(rows_kernel, total, nch, chan0, paired),...  61.1 us
    ppermute x42, waiting for transfers between devices, shards(): got[j] = lax.ppermute(w[j], 'facet', [(s, s ^ j) for s in range(nf)])  55.7 us
    ppermute x42, starting transfers between devices, shards(): got[j] = lax.ppermute(w[j], 'facet', [(s, s ^ j) for s in range(nf)])  44.1 us
    pallas_call x6, Pallas kernels, shards(): pl.pallas_call(functools.partial(pixels_kernel, nf, 1.0 / (frame * frame)...  23.2 us
    all_gather x1, blocking collectives, shards(): fit = lax.all_gather(fit, 'facet', axis=0)  9.97 us
    ppermute x2, starting transfers between devices, shards(): other = lax.ppermute(sums, 'freq', [(s, s ^ 1 << i) for s in range(nz)])  5.87 us
    pallas_call x2, Pallas kernels, shards(): pl.pallas_call(functools.partial(pixel_phases_kernel, frame, pad, nf, kb)...  4.67 us
  transfers between devices with their start and end apart: 46, of which 9 were waited for; matrix products, arithmetic and copies ran while one was open for 1% of the time, Pallas kernels for 37%

profile of v3, /device:TPU:0, one launch (start us, length us, event | category | flops | bytes accessed | tf_op | source)
XLA Modules:
  0.0 226.5 jit_solution(2936591093810122738)
XLA Ops:
  0.0 1.6 moments.1
  1.6 3.1 %collective-permute-start = (f32[13,16,128]{2,1,0:T(8,128)}, f32[13,16,128]{2,1,0:T(8,128)S(1)}, u32[]{:S(2)}, u32[]{:S(2)}) collective-permute-start(f32[13,16,128]{2,1,0:T(8,128)} %moments.1), channel_id=1, source_target_pairs={{0,1},{1,0},{2,3},{3,2},{4,5},{5,4},{6,7},{7,6},{8,9},{9,8},{10,11... | collective-permute-start | bytes 319496 | tf_op jit(solution)/shard_map/ppermute | solution.py:351
  4.7 3.2 %collective-permute-done = f32[13,16,128]{2,1,0:T(8,128)S(1)} collective-permute-done((f32[13,16,128]{2,1,0:T(8,128)}, f32[13,16,128]{2,1,0:T(8,128)S(1)}, u32[]{:S(2)}, u32[]{:S(2)}) %collective-permute-start) | collective-permute-done | bytes 106528 | tf_op jit(solution)/shard_map/ppermute | solution.py:351
  8.8 2.8 %collective-permute-start.1 = (f32[13,16,128]{2,1,0:T(8,128)S(1)}, f32[13,16,128]{2,1,0:T(8,128)}, u32[]{:S(2)}, u32[]{:S(2)}) collective-permute-start(f32[13,16,128]{2,1,0:T(8,128)S(1)} %add.3.one_ref), channel_id=1, source_target_pairs={{0,2},{1,3},{2,0},{3,1},{4,6},{5,7},{6,4},{7,5},{8,10},{9,11},{10,... | collective-permute-start | bytes 319496 | tf_op jit(solution)/shard_map/ppermute | solution.py:351
  11.6 3.7 %rowphases.1 = (bf16[2,4,192,128]{3,2,1,0:T(8,128)(2,1)S(1)}, bf16[768,512]{1,0:T(8,128)(2,1)}, bf16[384,384]{1,0:T(8,128)(2,1)}) custom-call(s32[2,4]{1,0:T(2,128)} %bitcast.16), custom_call_target="tpu_custom_call" | custom-call | tf_op jit(solution)/shard_map/rowphases/pallas_call | solution.py:320
  15.3 2.8 %colphases.1 = bf16[16,128,768]{2,1,0:T(8,128)(2,1)S(1)} custom-call(s32[2,4]{1,0:T(2,128)} %bitcast.17), custom_call_target="tpu_custom_call" | custom-call | tf_op jit(solution)/shard_map/colphases/pallas_call | solution.py:337
  18.8 1.6 solve.1
  20.4 10.0 %all-gather = bf16[104,16,128]{2,1,0:T(8,128)(2,1)S(1)} all-gather(bf16[13,16,128]{2,1,0:T(8,128)(2,1)} %solve.1), channel_id=2, replica_groups=mesh['facet'=8,'freq'=4] {'facet'}, dimensions={0}, use_global_device_ids=true | all-gather | bytes 479232 | tf_op jit(solution)/shard_map/all_gather | solution.py:359
  30.6 8.7 %rows.11 = (bf16[1,192,512]{2,1,0:T(8,128)(2,1)}, bf16[1,192,512]{2,1,0:T(8,128)(2,1)}, bf16[1,192,512]{2,1,0:T(8,128)(2,1)}, bf16[1,192,512]{2,1,0:T(8,128)(2,1...) custom-call(s32[8]{0:T(128)S(1)} %fusion.psf_of_ref, ...), custom_call_target="tpu_custom_call" | custom-call | flops 2415919104 | bytes 5898240 | tf_op jit(solution)/shard_map/rows/pallas_call | solution.py:376
  44.6 8.5 %rows.10 = (bf16[1,192,512]{2,1,0:T(8,128)(2,1)}, bf16[1,192,512]{2,1,0:T(8,128)(2,1)}, bf16[1,192,512]{2,1,0:T(8,128)(2,1)}, bf16[1,192,512]{2,1,0:T(8,128)(2,1...) custom-call(s32[8]{0:T(128)S(1)} %fusion.psf_of_ref, ...), custom_call_target="tpu_custom_call" | custom-call | flops 2415919104 | bytes 5898240 | tf_op jit(solution)/shard_map/rows/pallas_call | solution.py:376
  57.0 5.5 %collective-permute-start.34 = (bf16[1,192,512]{2,1,0:T(8,128)(2,1)}, bf16[1,192,512]{2,1,0:T(8,128)(2,1)}, u32[]{:S(2)}, u32[]{:S(2)}) collective-permute-start(bf16[1,192,512]{2,1,0:T(8,128)(2,1)} %get-tuple-element.94), channel_id=1, source_target_pairs={{0,12},{4,8},{8,4},{12,0},{16,28},{20,24},{24,20},{28,16},{1,13},{... | collective-permute-start | bytes 589832 | tf_op jit(solution)/shard_map/ppermute | solution.py:415
  69.6 1.5 collective-permute-start.37
  72.3 14.0 %rows.9 = (bf16[2,192,512]{2,1,0:T(8,128)(2,1)}, bf16[2,192,512]{2,1,0:T(8,128)(2,1)}, bf16[2,192,512]{2,1,0:T(8,128)(2,1)}, bf16[2,192,512]{2,1,0:T(8,128)(2,1)...) custom-call(s32[8]{0:T(128)S(1)} %fusion.psf_of_ref, ...), custom_call_target="tpu_custom_call" | custom-call | flops 4831838208 | bytes 8650752 | tf_op jit(solution)/shard_map/rows/pallas_call | solution.py:376
  86.3 21.3 %collective-permute-done.36.refs_5_ = bf16[1,192,512]{2,1,0:T(8,128)(2,1)S(1)} collective-permute-done((bf16[1,192,512]{2,1,0:T(8,128)(2,1)}, bf16[1,192,512]{2,1,0:T(8,128)(2,1)S(1)}, u32[]{:S(2)}, u32[]{:S(2)}) %collective-permute-start.36) | collective-permute-done | bytes 196640 | tf_op jit(solution)/shard_map/ppermute | solution.py:415
  110.9 14.0 %rows.8 = (bf16[2,192,512]{2,1,0:T(8,128)(2,1)}, bf16[2,192,512]{2,1,0:T(8,128)(2,1)}, bf16[2,192,512]{2,1,0:T(8,128)(2,1)}, bf16[2,192,512]{2,1,0:T(8,128)(2,1)...) custom-call(s32[8]{0:T(128)S(1)} %fusion.psf_of_ref, ...), custom_call_target="tpu_custom_call" | custom-call | flops 4831838208 | bytes 8650752 | tf_op jit(solution)/shard_map/rows/pallas_call | solution.py:376
  125.5 1.5 collective-permute-start.30
  129.9 23.3 %collective-permute-done.29.refs_5_ = bf16[2,192,512]{2,1,0:T(8,128)(2,1)} collective-permute-done((bf16[2,192,512]{2,1,0:T(8,128)(2,1)S(1)}, bf16[2,192,512]{2,1,0:T(8,128)(2,1)}, u32[]{:S(2)}, u32[]{:S(2)}) %collective-permute-start.29) | collective-permute-done | bytes 393248 | tf_op jit(solution)/shard_map/ppermute | solution.py:415
  156.8 2.8 %pixphases.3.refs_8_ = bf16[512,1536]{1,0:T(8,128)(2,1)} custom-call(), custom_call_target="tpu_custom_call" | custom-call | tf_op jit(solution)/shard_map/pixphases/pallas_call | solution.py:364
  159.6 1.9 pixphases.2.refs_8_
  161.5 1.6 collective-permute-start.24
  164.5 3.8 %pixels.6.refs_10_ = f32[8,1,512,512]{3,2,1,0:T(8,128)} custom-call(bf16[1,192,512]{2,1,0:T(8,128)(2,1)} %get-tuple-element.99.refs_0_, bf16[1,192,512]{2,1,0:T(8,128)(2,1)} %collective-permute-done.39.refs_1_, bf16[1,192,512]{2,1,0:T(8,128)(2,1)} %copy-done.10, bf16[1,192,512]{2,1,0:T(8,128)(2,1)} %copy-done.11, bf16[1,192,512]{2,1,0:T(8,128)(2,1)} %copy-done.12, ...), custom_call_target="tpu_custom_call" | custom-call | flops 805306368 | bytes 3670016 | tf_op jit(solution)/shard_map/pixels/pallas_call | solution.py:421
  168.2 3.8 %pixels.7.refs_10_ = f32[8,1,512,512]{3,2,1,0:T(8,128)} custom-call(bf16[1,192,512]{2,1,0:T(8,128)(2,1)} %get-tuple-element.91.refs_0_, bf16[1,192,512]{2,1,0:T(8,128)(2,1)} %copy-done.16, bf16[1,192,512]{2,1,0:T(8,128)(2,1)} %copy-done.17, bf16[1,192,512]{2,1,0:T(8,128)(2,1)} %collective-permute-done.34.refs_3_, ...), custom_call_target="tpu_custom_call", output_to_operand_aliasing={{}: (10, {})} | custom-call | flops 805306368 | bytes 3670016 | tf_op jit(solution)/shard_map/pixels/pallas_call | solution.py:421
  172.1 8.0 %rows.7 = (bf16[1,112,512]{2,1,0:T(8,128)(2,1)}, bf16[1,112,512]{2,1,0:T(8,128)(2,1)}, bf16[1,112,512]{2,1,0:T(8,128)(2,1)}, bf16[1,112,512]{2,1,0:T(8,128)(2,1)...) custom-call(s32[8]{0:T(128)S(1)} %fusion.psf_of_ref, ...), custom_call_target="tpu_custom_call" | custom-call | flops 1610612736 | bytes 5242880 | tf_op jit(solution)/shard_map/rows/pallas_call | solution.py:376
  180.3 2.8 %collective-permute-done.21.refs_4_ = bf16[2,192,512]{2,1,0:T(8,128)(2,1)} collective-permute-done((bf16[2,192,512]{2,1,0:T(8,128)(2,1)}, bf16[2,192,512]{2,1,0:T(8,128)(2,1)}, u32[]{:S(2)}, u32[]{:S(2)}) %collective-permute-start.21) | collective-permute-done | bytes 393248 | tf_op jit(solution)/shard_map/ppermute | solution.py:415
  184.4 5.5 %collective-permute-done.22.refs_5_ = bf16[2,192,512]{2,1,0:T(8,128)(2,1)} collective-permute-done((bf16[2,192,512]{2,1,0:T(8,128)(2,1)}, bf16[2,192,512]{2,1,0:T(8,128)(2,1)}, u32[]{:S(2)}, u32[]{:S(2)}) %collective-permute-start.22) | collective-permute-done | bytes 393248 | tf_op jit(solution)/shard_map/ppermute | solution.py:415
  189.9 1.5 collective-permute-start.13
  192.1 7.8 %rows.6 = (bf16[1,112,512]{2,1,0:T(8,128)(2,1)}, bf16[1,112,512]{2,1,0:T(8,128)(2,1)}, bf16[1,112,512]{2,1,0:T(8,128)(2,1)}, bf16[1,112,512]{2,1,0:T(8,128)(2,1)...) custom-call(s32[8]{0:T(128)S(1)} %fusion.psf_of_ref, ...), custom_call_target="tpu_custom_call" | custom-call | flops 1610612736 | bytes 5242880 | tf_op jit(solution)/shard_map/rows/pallas_call | solution.py:376
  201.9 1.7 collective-permute-start.17
  204.6 4.9 %pixels.8.refs_10_ = f32[8,1,512,512]{3,2,1,0:T(8,128)} custom-call(bf16[2,192,512]{2,1,0:T(8,128)(2,1)} %get-tuple-element.83.refs_0_, bf16[2,192,512]{2,1,0:T(8,128)(2,1)} %collective-permute-done.25.refs_1_, bf16[2,192,512]{2,1,0:T(8,128)(2,1)} %collective-permute-done.26.refs_2_, ...), custom_call_target="tpu_custom_call", output_to_operand_aliasing={{}: (10, {})} | custom-call | flops 1610612736 | bytes 7340032 | tf_op jit(solution)/shard_map/pixels/pallas_call | solution.py:421
  215.2 4.9 %pixels.9.refs_10_ = f32[8,1,512,512]{3,2,1,0:T(8,128)} custom-call(bf16[2,192,512]{2,1,0:T(8,128)(2,1)} %get-tuple-element.75.refs_0_, bf16[2,192,512]{2,1,0:T(8,128)(2,1)} %collective-permute-done.18.refs_1_, bf16[2,192,512]{2,1,0:T(8,128)(2,1)} %collective-permute-done.19.refs_2_, ...), custom_call_target="tpu_custom_call", output_to_operand_aliasing={{}: (10, {})} | custom-call | flops 1610612736 | bytes 7340032 | tf_op jit(solution)/shard_map/pixels/pallas_call | solution.py:421
  220.1 2.9 %pixels.10.refs_10_ = f32[8,1,512,512]{3,2,1,0:T(8,128)} custom-call(bf16[1,112,512]{2,1,0:T(8,128)(2,1)S(1)} %copy-done.5, bf16[1,112,512]{2,1,0:T(8,128)(2,1)S(1)} %collective-permute-done.11.refs_1_, bf16[1,112,512]{2,1,0:T(8,128)(2,1)S(1)} %collective-permute-done.12.refs_2_, ...), custom_call_target="tpu_custom_call", output_to_operand_aliasing={{}: (10, {})} | custom-call | flops 469762048 | bytes 3014656 | tf_op jit(solution)/shard_map/pixels/pallas_call | solution.py:421
  223.6 2.9 %pixels.11 = f32[8,1,512,512]{3,2,1,0:T(8,128)} custom-call(bf16[1,112,512]{2,1,0:T(8,128)(2,1)S(1)} %copy-done.6, bf16[1,112,512]{2,1,0:T(8,128)(2,1)S(1)} %collective-permute-done.3.refs_1_, bf16[1,112,512]{2,1,0:T(8,128)(2,1)S(1)} %collective-permute-done.4.refs_2_, ...), custom_call_target="tpu_custom_call", output_to_operand_aliasing={{}: (10, {})} | custom-call | flops 469762048 | bytes 3014656 | tf_op jit(solution)/shard_map/pixels/pallas_call | solution.py:421
  (148 shorter events, 41.6 us)
Async XLA Ops:
  39.7 13.4 %collective-permute-start.40 = (bf16[1,192,512]{2,1,0:T(8,128)(2,1)}, bf16[1,192,512]{2,1,0:T(8,128)(2,1)S(1)}, u32[]{:S(2)}, u32[]{:S(2)}) collective-permute-start(bf16[1,192,512]{2,1,0:T(8,128)(2,1)} %get-tuple-element.101), channel_id=1, source_target_pairs={{0,8},{4,12},{8,0},{12,4},{16,24},{20,28},{24,16},{28,20},{1,9},{5... | collective-permute-start | bytes 589832 | tf_op jit(solution)/shard_map/ppermute | solution.py:415
  40.9 13.3 %collective-permute-start.41 = (bf16[1,192,512]{2,1,0:T(8,128)(2,1)}, bf16[1,192,512]{2,1,0:T(8,128)(2,1)S(1)}, u32[]{:S(2)}, u32[]{:S(2)}) collective-permute-start(bf16[1,192,512]{2,1,0:T(8,128)(2,1)} %get-tuple-element.102), channel_id=1, source_target_pairs={{0,12},{4,8},{8,4},{12,0},{16,28},{20,24},{24,20},{28,16},{1,13},{... | collective-permute-start | bytes 589832 | tf_op jit(solution)/shard_map/ppermute | solution.py:415
  41.2 13.6 %collective-permute-start.42 = (bf16[1,192,512]{2,1,0:T(8,128)(2,1)}, bf16[1,192,512]{2,1,0:T(8,128)(2,1)S(1)}, u32[]{:S(2)}, u32[]{:S(2)}) collective-permute-start(bf16[1,192,512]{2,1,0:T(8,128)(2,1)} %get-tuple-element.103), channel_id=1, source_target_pairs={{0,16},{4,20},{8,24},{12,28},{16,0},{20,4},{24,8},{28,12},{1,17},{... | collective-permute-start | bytes 589832 | tf_op jit(solution)/shard_map/ppermute | solution.py:415
  42.4 14.5 %collective-permute-start.43 = (bf16[1,192,512]{2,1,0:T(8,128)(2,1)}, bf16[1,192,512]{2,1,0:T(8,128)(2,1)S(1)}, u32[]{:S(2)}, u32[]{:S(2)}) collective-permute-start(bf16[1,192,512]{2,1,0:T(8,128)(2,1)} %get-tuple-element.104), channel_id=1, source_target_pairs={{0,20},{4,16},{8,28},{12,24},{16,4},{20,0},{24,12},{28,8},{1,21},{... | collective-permute-start | bytes 589832 | tf_op jit(solution)/shard_map/ppermute | solution.py:415
  43.2 19.3 %collective-permute-start.44 = (bf16[1,192,512]{2,1,0:T(8,128)(2,1)}, bf16[1,192,512]{2,1,0:T(8,128)(2,1)S(1)}, u32[]{:S(2)}, u32[]{:S(2)}) collective-permute-start(bf16[1,192,512]{2,1,0:T(8,128)(2,1)} %get-tuple-element.105), channel_id=1, source_target_pairs={{0,24},{4,28},{8,16},{12,20},{16,8},{20,12},{24,0},{28,4},{1,25},{... | collective-permute-start | bytes 589832 | tf_op jit(solution)/shard_map/ppermute | solution.py:415
  54.9 12.4 %collective-permute-start.33 = (bf16[1,192,512]{2,1,0:T(8,128)(2,1)}, bf16[1,192,512]{2,1,0:T(8,128)(2,1)S(1)}, u32[]{:S(2)}, u32[]{:S(2)}) collective-permute-start(bf16[1,192,512]{2,1,0:T(8,128)(2,1)} %get-tuple-element.93), channel_id=1, source_target_pairs={{0,8},{4,12},{8,0},{12,4},{16,24},{20,28},{24,16},{28,20},{1,9},{5... | collective-permute-start | bytes 589832 | tf_op jit(solution)/shard_map/ppermute | solution.py:415
  57.0 12.7 %collective-permute-start.34 = (bf16[1,192,512]{2,1,0:T(8,128)(2,1)}, bf16[1,192,512]{2,1,0:T(8,128)(2,1)}, u32[]{:S(2)}, u32[]{:S(2)}) collective-permute-start(bf16[1,192,512]{2,1,0:T(8,128)(2,1)} %get-tuple-element.94), channel_id=1, source_target_pairs={{0,12},{4,8},{8,4},{12,0},{16,28},{20,24},{24,20},{28,16},{1,13},{... | collective-permute-start | bytes 589832 | tf_op jit(solution)/shard_map/ppermute | solution.py:415
  64.6 44.9 %collective-permute-start.10 = (bf16[4,1,2,48,768]{4,3,2,1,0:T(8,128)(2,1)S(1)}, bf16[4,1,2,48,768]{4,3,2,1,0:T(8,128)(2,1)S(1)}, u32[]{:S(2)}, u32[]{:S(2)}) collective-permute-start(bf16[4,1,2,48,768]{4,3,2,1,0:T(8,128)(2,1)S(1)} %get-tuple-element.107), channel_id=1, source_target_pairs={{0,28},{4,24},{8,20},{12,16},{16,12},{20,8},{24,4},{28,0},{1,29},{... | collective-permute-start | bytes 1769480 | tf_op jit(solution)/shard_map/ppermute | solution.py:312
  65.8 59.2 %collective-permute-start.2 = (bf16[4,1,2,48,768]{4,3,2,1,0:T(8,128)(2,1)S(1)}, bf16[4,1,2,48,768]{4,3,2,1,0:T(8,128)(2,1)}, u32[]{:S(2)}, u32[]{:S(2)}) collective-permute-start(bf16[4,1,2,48,768]{4,3,2,1,0:T(8,128)(2,1)S(1)} %get-tuple-element.108), channel_id=1, source_target_pairs={{0,28},{4,24},{8,20},{12,16},{16,12},{20,8},{24,4},{28,0},{1,29},{... | collective-permute-start | bytes 1769480 | tf_op jit(solution)/shard_map/ppermute | solution.py:312
  67.9 39.7 %collective-permute-start.36 = (bf16[1,192,512]{2,1,0:T(8,128)(2,1)}, bf16[1,192,512]{2,1,0:T(8,128)(2,1)S(1)}, u32[]{:S(2)}, u32[]{:S(2)}) collective-permute-start(bf16[1,192,512]{2,1,0:T(8,128)(2,1)} %get-tuple-element.96), channel_id=1, source_target_pairs={{0,20},{4,16},{8,28},{12,24},{16,4},{20,0},{24,12},{28,8},{1,21},{... | collective-permute-start | bytes 589832 | tf_op jit(solution)/shard_map/ppermute | solution.py:415
  69.6 38.2 %collective-permute-start.37 = (bf16[1,192,512]{2,1,0:T(8,128)(2,1)}, bf16[1,192,512]{2,1,0:T(8,128)(2,1)S(1)}, u32[]{:S(2)}, u32[]{:S(2)}) collective-permute-start(bf16[1,192,512]{2,1,0:T(8,128)(2,1)} %get-tuple-element.97), channel_id=1, source_target_pairs={{0,24},{4,28},{8,16},{12,20},{16,8},{20,12},{24,0},{28,4},{1,25},{... | collective-permute-start | bytes 589832 | tf_op jit(solution)/shard_map/ppermute | solution.py:415
  71.1 38.0 %collective-permute-start.38 = (bf16[1,192,512]{2,1,0:T(8,128)(2,1)}, bf16[1,192,512]{2,1,0:T(8,128)(2,1)S(1)}, u32[]{:S(2)}, u32[]{:S(2)}) collective-permute-start(bf16[1,192,512]{2,1,0:T(8,128)(2,1)} %get-tuple-element.98), channel_id=1, source_target_pairs={{0,28},{4,24},{8,20},{12,16},{16,12},{20,8},{24,4},{28,0},{1,29},{... | collective-permute-start | bytes 589832 | tf_op jit(solution)/shard_map/ppermute | solution.py:415
  107.7 17.8 %collective-permute-start.25 = (bf16[2,192,512]{2,1,0:T(8,128)(2,1)}, bf16[2,192,512]{2,1,0:T(8,128)(2,1)}, u32[]{:S(2)}, u32[]{:S(2)}) collective-permute-start(bf16[2,192,512]{2,1,0:T(8,128)(2,1)} %get-tuple-element.84), channel_id=1, source_target_pairs={{0,4},{4,0},{8,12},{12,8},{16,20},{20,16},{24,28},{28,24},{1,5},{5... | collective-permute-start | bytes 1179656 | tf_op jit(solution)/shard_map/ppermute | solution.py:415
  107.8 19.3 %collective-permute-start.26 = (bf16[2,192,512]{2,1,0:T(8,128)(2,1)}, bf16[2,192,512]{2,1,0:T(8,128)(2,1)}, u32[]{:S(2)}, u32[]{:S(2)}) collective-permute-start(bf16[2,192,512]{2,1,0:T(8,128)(2,1)} %get-tuple-element.85), channel_id=1, source_target_pairs={{0,8},{4,12},{8,0},{12,4},{16,24},{20,28},{24,16},{28,20},{1,9},{5... | collective-permute-start | bytes 1179656 | tf_op jit(solution)/shard_map/ppermute | solution.py:415
  109.1 19.1 %collective-permute-start.27 = (bf16[2,192,512]{2,1,0:T(8,128)(2,1)}, bf16[2,192,512]{2,1,0:T(8,128)(2,1)}, u32[]{:S(2)}, u32[]{:S(2)}) collective-permute-start(bf16[2,192,512]{2,1,0:T(8,128)(2,1)} %get-tuple-element.86), channel_id=1, source_target_pairs={{0,12},{4,8},{8,4},{12,0},{16,28},{20,24},{24,20},{28,16},{1,13},{... | collective-permute-start | bytes 1179656 | tf_op jit(solution)/shard_map/ppermute | solution.py:415
  109.6 19.0 %collective-permute-start.28 = (bf16[2,192,512]{2,1,0:T(8,128)(2,1)}, bf16[2,192,512]{2,1,0:T(8,128)(2,1)}, u32[]{:S(2)}, u32[]{:S(2)}) collective-permute-start(bf16[2,192,512]{2,1,0:T(8,128)(2,1)} %get-tuple-element.87), channel_id=1, source_target_pairs={{0,16},{4,20},{8,24},{12,28},{16,0},{20,4},{24,8},{28,12},{1,17},{... | collective-permute-start | bytes 1179656 | tf_op jit(solution)/shard_map/ppermute | solution.py:415
  125.0 28.2 %collective-permute-start.29 = (bf16[2,192,512]{2,1,0:T(8,128)(2,1)S(1)}, bf16[2,192,512]{2,1,0:T(8,128)(2,1)}, u32[]{:S(2)}, u32[]{:S(2)}) collective-permute-start(bf16[2,192,512]{2,1,0:T(8,128)(2,1)S(1)} %copy-done.23), channel_id=1, source_target_pairs={{0,20},{4,16},{8,28},{12,24},{16,4},{20,0},{24,12},{28,8},{1,21},{... | collective-permute-start | bytes 1179656 | tf_op jit(solution)/shard_map/ppermute | solution.py:415
  125.5 28.5 %collective-permute-start.30 = (bf16[2,192,512]{2,1,0:T(8,128)(2,1)S(1)}, bf16[2,192,512]{2,1,0:T(8,128)(2,1)}, u32[]{:S(2)}, u32[]{:S(2)}) collective-permute-start(bf16[2,192,512]{2,1,0:T(8,128)(2,1)S(1)} %copy-done.22), channel_id=1, source_target_pairs={{0,24},{4,28},{8,16},{12,20},{16,8},{20,12},{24,0},{28,4},{1,25},{... | collective-permute-start | bytes 1179656 | tf_op jit(solution)/shard_map/ppermute | solution.py:415
  127.1 28.2 %collective-permute-start.31 = (bf16[2,192,512]{2,1,0:T(8,128)(2,1)S(1)}, bf16[2,192,512]{2,1,0:T(8,128)(2,1)}, u32[]{:S(2)}, u32[]{:S(2)}) collective-permute-start(bf16[2,192,512]{2,1,0:T(8,128)(2,1)S(1)} %copy-done.21), channel_id=1, source_target_pairs={{0,28},{4,24},{8,20},{12,16},{16,12},{20,8},{24,4},{28,0},{1,29},{... | collective-permute-start | bytes 1179656 | tf_op jit(solution)/shard_map/ppermute | solution.py:415
  128.2 27.3 %collective-permute-start.18 = (bf16[2,192,512]{2,1,0:T(8,128)(2,1)}, bf16[2,192,512]{2,1,0:T(8,128)(2,1)}, u32[]{:S(2)}, u32[]{:S(2)}) collective-permute-start(bf16[2,192,512]{2,1,0:T(8,128)(2,1)} %get-tuple-element.76), channel_id=1, source_target_pairs={{0,4},{4,0},{8,12},{12,8},{16,20},{20,16},{24,28},{28,24},{1,5},{5... | collective-permute-start | bytes 1179656 | tf_op jit(solution)/shard_map/ppermute | solution.py:415
  128.6 32.9 %collective-permute-start.19 = (bf16[2,192,512]{2,1,0:T(8,128)(2,1)}, bf16[2,192,512]{2,1,0:T(8,128)(2,1)}, u32[]{:S(2)}, u32[]{:S(2)}) collective-permute-start(bf16[2,192,512]{2,1,0:T(8,128)(2,1)} %get-tuple-element.77), channel_id=1, source_target_pairs={{0,8},{4,12},{8,0},{12,4},{16,24},{20,28},{24,16},{28,20},{1,9},{5... | collective-permute-start | bytes 1179656 | tf_op jit(solution)/shard_map/ppermute | solution.py:415
  153.2 26.9 %collective-permute-start.20 = (bf16[2,192,512]{2,1,0:T(8,128)(2,1)}, bf16[2,192,512]{2,1,0:T(8,128)(2,1)}, u32[]{:S(2)}, u32[]{:S(2)}) collective-permute-start(bf16[2,192,512]{2,1,0:T(8,128)(2,1)} %get-tuple-element.78), channel_id=1, source_target_pairs={{0,12},{4,8},{8,4},{12,0},{16,28},{20,24},{24,20},{28,16},{1,13},{... | collective-permute-start | bytes 1179656 | tf_op jit(solution)/shard_map/ppermute | solution.py:415
  154.0 29.2 %collective-permute-start.21 = (bf16[2,192,512]{2,1,0:T(8,128)(2,1)}, bf16[2,192,512]{2,1,0:T(8,128)(2,1)}, u32[]{:S(2)}, u32[]{:S(2)}) collective-permute-start(bf16[2,192,512]{2,1,0:T(8,128)(2,1)} %get-tuple-element.79), channel_id=1, source_target_pairs={{0,16},{4,20},{8,24},{12,28},{16,0},{20,4},{24,8},{28,12},{1,17},{... | collective-permute-start | bytes 1179656 | tf_op jit(solution)/shard_map/ppermute | solution.py:415
  155.2 34.7 %collective-permute-start.22 = (bf16[2,192,512]{2,1,0:T(8,128)(2,1)}, bf16[2,192,512]{2,1,0:T(8,128)(2,1)}, u32[]{:S(2)}, u32[]{:S(2)}) collective-permute-start(bf16[2,192,512]{2,1,0:T(8,128)(2,1)} %get-tuple-element.80), channel_id=1, source_target_pairs={{0,20},{4,16},{8,28},{12,24},{16,4},{20,0},{24,12},{28,8},{1,21},{... | collective-permute-start | bytes 1179656 | tf_op jit(solution)/shard_map/ppermute | solution.py:415
  155.5 35.9 %collective-permute-start.23 = (bf16[2,192,512]{2,1,0:T(8,128)(2,1)}, bf16[2,192,512]{2,1,0:T(8,128)(2,1)}, u32[]{:S(2)}, u32[]{:S(2)}) collective-permute-start(bf16[2,192,512]{2,1,0:T(8,128)(2,1)} %get-tuple-element.81), channel_id=1, source_target_pairs={{0,24},{4,28},{8,16},{12,20},{16,8},{20,12},{24,0},{28,4},{1,25},{... | collective-permute-start | bytes 1179656 | tf_op jit(solution)/shard_map/ppermute | solution.py:415
  161.5 38.4 %collective-permute-start.24 = (bf16[2,192,512]{2,1,0:T(8,128)(2,1)}, bf16[2,192,512]{2,1,0:T(8,128)(2,1)S(1)}, u32[]{:S(2)}, u32[]{:S(2)}) collective-permute-start(bf16[2,192,512]{2,1,0:T(8,128)(2,1)} %get-tuple-element.82), channel_id=1, source_target_pairs={{0,28},{4,24},{8,20},{12,16},{16,12},{20,8},{24,4},{28,0},{1,29},{... | collective-permute-start | bytes 1179656 | tf_op jit(solution)/shard_map/ppermute | solution.py:415
  180.1 20.3 %collective-permute-start.11 = (bf16[1,112,512]{2,1,0:T(8,128)(2,1)}, bf16[1,112,512]{2,1,0:T(8,128)(2,1)S(1)}, u32[]{:S(2)}, u32[]{:S(2)}) collective-permute-start(bf16[1,112,512]{2,1,0:T(8,128)(2,1)} %get-tuple-element.68), channel_id=1, source_target_pairs={{0,4},{4,0},{8,12},{12,8},{16,20},{20,16},{24,28},{28,24},{1,5},{5... | collective-permute-start | bytes 344072 | tf_op jit(solution)/shard_map/ppermute | solution.py:415
  183.1 18.8 %collective-permute-start.12 = (bf16[1,112,512]{2,1,0:T(8,128)(2,1)}, bf16[1,112,512]{2,1,0:T(8,128)(2,1)S(1)}, u32[]{:S(2)}, u32[]{:S(2)}) collective-permute-start(bf16[1,112,512]{2,1,0:T(8,128)(2,1)} %get-tuple-element.69), channel_id=1, source_target_pairs={{0,8},{4,12},{8,0},{12,4},{16,24},{20,28},{24,16},{28,20},{1,9},{5... | collective-permute-start | bytes 344072 | tf_op jit(solution)/shard_map/ppermute | solution.py:415
  189.9 13.8 %collective-permute-start.13 = (bf16[1,112,512]{2,1,0:T(8,128)(2,1)}, bf16[1,112,512]{2,1,0:T(8,128)(2,1)S(1)}, u32[]{:S(2)}, u32[]{:S(2)}) collective-permute-start(bf16[1,112,512]{2,1,0:T(8,128)(2,1)} %get-tuple-element.70), channel_id=1, source_target_pairs={{0,12},{4,8},{8,4},{12,0},{16,28},{20,24},{24,20},{28,16},{1,13},{... | collective-permute-start | bytes 344072 | tf_op jit(solution)/shard_map/ppermute | solution.py:415
  191.4 12.3 %collective-permute-start.14 = (bf16[1,112,512]{2,1,0:T(8,128)(2,1)}, bf16[1,112,512]{2,1,0:T(8,128)(2,1)S(1)}, u32[]{:S(2)}, u32[]{:S(2)}) collective-permute-start(bf16[1,112,512]{2,1,0:T(8,128)(2,1)} %get-tuple-element.71), channel_id=1, source_target_pairs={{0,16},{4,20},{8,24},{12,28},{16,0},{20,4},{24,8},{28,12},{1,17},{... | collective-permute-start | bytes 344072 | tf_op jit(solution)/shard_map/ppermute | solution.py:415
  210.2 12.9 %collective-permute-start.5 = (bf16[1,112,512]{2,1,0:T(8,128)(2,1)S(1)}, bf16[1,112,512]{2,1,0:T(8,128)(2,1)S(1)}, u32[]{:S(2)}, u32[]{:S(2)}) collective-permute-start(bf16[1,112,512]{2,1,0:T(8,128)(2,1)S(1)} %copy-done.29), channel_id=1, source_target_pairs={{0,12},{4,8},{8,4},{12,0},{16,28},{20,24},{24,20},{28,16},{1,13},{... | collective-permute-start | bytes 344072 | tf_op jit(solution)/shard_map/ppermute | solution.py:415
  210.8 12.3 %collective-permute-start.6 = (bf16[1,112,512]{2,1,0:T(8,128)(2,1)S(1)}, bf16[1,112,512]{2,1,0:T(8,128)(2,1)S(1)}, u32[]{:S(2)}, u32[]{:S(2)}) collective-permute-start(bf16[1,112,512]{2,1,0:T(8,128)(2,1)S(1)} %copy-done.28), channel_id=1, source_target_pairs={{0,16},{4,20},{8,24},{12,28},{16,0},{20,4},{24,8},{28,12},{1,17},{... | collective-permute-start | bytes 344072 | tf_op jit(solution)/shard_map/ppermute | solution.py:415
  (47 other events, 533.4 us)

commit v4 on v3

--- a/solution.py
+++ b/solution.py
@@ -134,17 +134,16 @@
     lax.fori_loop(0, FCOLS * ntile, columns, 0)
 
 
-def pixel_phases_kernel(frame, pad, nf, kb, out_ref, cos_ref, sin_ref):
+def pixel_phases_kernel(frame, pad, nf, kb, count, extra, out_ref, cos_ref, sin_ref):
     me = lax.axis_index("facet")
     width = out_ref.shape[1]
-    rows = width // nf
     column = lane((1, width), 1)
     inner, base = column, jnp.zeros((1, width), i32)
     for j in range(nf):
-        here = (column >= j * rows) & (column < (j + 1) * rows)
-        inner = jnp.where(here, column - j * rows, inner)
-        base = jnp.where(here, jnp.bitwise_xor(me, j) * kb, base)
-    count = kb if rows == 2 * kb else kb // 2
+        for start, rows, skip in ((j * 2 * count, 2 * count, 0), (nf * 2 * count + j * extra, extra, 2 * count)):
+            here = (column >= start) & (column < start + rows)
+            inner = jnp.where(here, column - start + skip, inner)
+            base = jnp.where(here, jnp.bitwise_xor(me, j) * kb, base)
     k = jnp.where(inner < count, inner, inner - count)
     k = jnp.where(inner < 2 * count, k, count)
     minus_sin = ((inner >= count) & (inner < 2 * count)) | (inner == 2 * count + 1)
@@ -245,7 +244,7 @@
                     out_ref[0, :count] = w[start : start + count].astype(bf16)
                     out_ref[0, count : 2 * count] = w[start + rb : start + rb + count].astype(bf16)
                     re, im = start + count, start + rb + count
-                    tile = (TILE, w.shape[1])
+                    tile = (EXTRA, w.shape[1])
                     spot = lane(tile, 0)
                     extra = jnp.where(spot == 1, jnp.broadcast_to(w[im : im + 1], tile), 0.0)
                     extra = jnp.where(spot == 0, jnp.broadcast_to(w[re : re + 1], tile), extra)
@@ -254,9 +253,13 @@
                     out_ref[0] = w[start : start + 2 * rb].astype(bf16)
 
 
-def pixels_kernel(nf, scale, *refs):
+def pixels_kernel(nf, scale, extra, *refs):
     blocks, table_ref, residual_ref, out_ref = refs[:nf], refs[nf], refs[nf + 1], refs[-1]
-    w = jnp.concatenate([block[0] for block in blocks], axis=0)
+    rows = blocks[0].shape[1] - extra
+    w = jnp.concatenate([block[0, :rows] for block in blocks], axis=0)
+    if extra:
+        more = jnp.concatenate([block[0, rows:].astype(f32) for block in blocks], axis=0)
+        w = jnp.concatenate([w, more.astype(bf16)], axis=0)
     conv = jnp.dot(table_ref[...], w, preferred_element_type=f32)
     out_ref[0, 0] = residual_ref[0, 0] - conv * scale
 
@@ -284,6 +287,7 @@
 
 NPAIR = 2
 TILE = 16
+EXTRA = 8
 
 
 VMEM = pl.BlockSpec(memory_space=pltpu.VMEM)
@@ -358,11 +362,13 @@
     )(facet_psf, sums, other)
     fit = lax.all_gather(fit, "facet", axis=0)
     psf_of = fit[:, 3 * ntile, 0, 0].astype(i32)
-    rb_pair, block_pair = kb // 2 + TILE, kb + TILE
+    rb_pair, block_pair = kb // 2 + TILE, kb + EXTRA
     tables = {}
     for paired in (False, True)[: 1 + bool(npair)]:
         tables[paired] = pl.pallas_call(
-            functools.partial(pixel_phases_kernel, frame, pad, nf, kb),
+            functools.partial(
+                pixel_phases_kernel, frame, pad, nf, kb, kb // 2 if paired else kb, EXTRA * paired
+            ),
             out_shape=jax.ShapeDtypeStruct((fs, nf * (block_pair if paired else 2 * kb)), bf16),
             out_specs=VMEM,
             scratch_shapes=[pltpu.VMEM((64, nf * (block_pair if paired else 2 * kb)), f32)] * 2,
@@ -419,7 +425,9 @@
         image = pl.BlockSpec((1, 1, fs, fs), lambda c, c0=chan0: (c0 + c, 0, 0, 0))
         before = [] if result is None else [result]
         result = pl.pallas_call(
-            functools.partial(pixels_kernel, nf, 1.0 / (frame * frame)),
+            functools.partial(
+                pixels_kernel, nf, 1.0 / (frame * frame), EXTRA if block == block_pair else 0
+            ),
             grid=(count,),
             in_specs=[pl.BlockSpec((1, block, fs), lambda c: (c, 0, 0))] * nf
             + [VMEM, image]

time: 227 us -> 226 us (level)
  transfers between devices with their start and end apart: 46 -> 46, of which waited for: 9 -> 8; matrix products, arithmetic and copies ran while one was open for 1% -> 1% of each run, Pallas kernels for 37% -> 37%
where the time goes in v4:
time: 226 us
  Pallas kernels  98.7 us (44%)
  waiting for transfers between devices  57.9 us (26%)
  starting transfers between devices  52.8 us (23%)
  blocking collectives  9.97 us (4%)
  local copies, waits for them, and re-layouts  4.21 us (2%)
    pallas_call x6, Pallas kernels, shards(): pl.pallas_call(functools.partial(rows_kernel, total, nch, chan0, paired),...  61 us
    ppermute x42, waiting for transfers between devices, shards(): got[j] = lax.ppermute(w[j], 'facet', [(s, s ^ j) for s in range(nf)])  54.7 us
    ppermute x42, starting transfers between devices, shards(): got[j] = lax.ppermute(w[j], 'facet', [(s, s ^ j) for s in range(nf)])  44.3 us
    pallas_call x6, Pallas kernels, shards(): pl.pallas_call(functools.partial(pixels_kernel, nf, 1.0 / (frame * frame)...  23.2 us
    all_gather x1, blocking collectives, shards(): fit = lax.all_gather(fit, 'facet', axis=0)  9.97 us
    ppermute x2, starting transfers between devices, shards(): other = lax.ppermute(sums, 'freq', [(s, s ^ 1 << i) for s in range(nz)])  5.87 us
    pallas_call x2, Pallas kernels, shards(): pl.pallas_call(functools.partial(pixel_phases_kernel, frame, pad, nf, kb,...  4.68 us
  transfers between devices with their start and end apart: 46, of which 8 were waited for; matrix products, arithmetic and copies ran while one was open for 1% of the time, Pallas kernels for 37%

profile of v4, /device:TPU:0, one launch (start us, length us, event | category | flops | bytes accessed | tf_op | source)
XLA Modules:
  0.0 225.7 jit_solution(11452189194356751173)
XLA Ops:
  0.0 1.6 moments.1
  1.6 3.1 %collective-permute-start = (f32[13,16,128]{2,1,0:T(8,128)}, f32[13,16,128]{2,1,0:T(8,128)S(1)}, u32[]{:S(2)}, u32[]{:S(2)}) collective-permute-start(f32[13,16,128]{2,1,0:T(8,128)} %moments.1), channel_id=1, source_target_pairs={{0,1},{1,0},{2,3},{3,2},{4,5},{5,4},{6,7},{7,6},{8,9},{9,8},{10,11... | collective-permute-start | bytes 319496 | tf_op jit(solution)/shard_map/ppermute | solution.py:355
  4.7 3.2 %collective-permute-done = f32[13,16,128]{2,1,0:T(8,128)S(1)} collective-permute-done((f32[13,16,128]{2,1,0:T(8,128)}, f32[13,16,128]{2,1,0:T(8,128)S(1)}, u32[]{:S(2)}, u32[]{:S(2)}) %collective-permute-start) | collective-permute-done | bytes 106528 | tf_op jit(solution)/shard_map/ppermute | solution.py:355
  8.8 2.8 %collective-permute-start.1 = (f32[13,16,128]{2,1,0:T(8,128)S(1)}, f32[13,16,128]{2,1,0:T(8,128)}, u32[]{:S(2)}, u32[]{:S(2)}) collective-permute-start(f32[13,16,128]{2,1,0:T(8,128)S(1)} %add.3.one_ref), channel_id=1, source_target_pairs={{0,2},{1,3},{2,0},{3,1},{4,6},{5,7},{6,4},{7,5},{8,10},{9,11},{10,... | collective-permute-start | bytes 319496 | tf_op jit(solution)/shard_map/ppermute | solution.py:355
  11.6 3.7 %rowphases.1 = (bf16[2,4,192,128]{3,2,1,0:T(8,128)(2,1)S(1)}, bf16[768,512]{1,0:T(8,128)(2,1)}, bf16[384,384]{1,0:T(8,128)(2,1)}) custom-call(s32[2,4]{1,0:T(2,128)} %bitcast.16), custom_call_target="tpu_custom_call" | custom-call | tf_op jit(solution)/shard_map/rowphases/pallas_call | solution.py:324
  15.3 2.8 %colphases.1 = bf16[16,128,768]{2,1,0:T(8,128)(2,1)S(1)} custom-call(s32[2,4]{1,0:T(2,128)} %bitcast.17), custom_call_target="tpu_custom_call" | custom-call | tf_op jit(solution)/shard_map/colphases/pallas_call | solution.py:341
  18.8 1.6 solve.1
  20.4 10.0 %all-gather = bf16[104,16,128]{2,1,0:T(8,128)(2,1)S(1)} all-gather(bf16[13,16,128]{2,1,0:T(8,128)(2,1)} %solve.1), channel_id=2, replica_groups=mesh['facet'=8,'freq'=4] {'facet'}, dimensions={0}, use_global_device_ids=true | all-gather | bytes 479232 | tf_op jit(solution)/shard_map/all_gather | solution.py:363
  30.6 8.7 %rows.11 = (bf16[1,192,512]{2,1,0:T(8,128)(2,1)}, bf16[1,192,512]{2,1,0:T(8,128)(2,1)}, bf16[1,192,512]{2,1,0:T(8,128)(2,1)}, bf16[1,192,512]{2,1,0:T(8,128)(2,1...) custom-call(s32[8]{0:T(128)S(1)} %fusion.psf_of_ref, ...), custom_call_target="tpu_custom_call" | custom-call | flops 2415919104 | bytes 5898240 | tf_op jit(solution)/shard_map/rows/pallas_call | solution.py:382
  44.6 8.5 %rows.10 = (bf16[1,192,512]{2,1,0:T(8,128)(2,1)}, bf16[1,192,512]{2,1,0:T(8,128)(2,1)}, bf16[1,192,512]{2,1,0:T(8,128)(2,1)}, bf16[1,192,512]{2,1,0:T(8,128)(2,1...) custom-call(s32[8]{0:T(128)S(1)} %fusion.psf_of_ref, ...), custom_call_target="tpu_custom_call" | custom-call | flops 2415919104 | bytes 5898240 | tf_op jit(solution)/shard_map/rows/pallas_call | solution.py:382
  57.0 5.5 %collective-permute-start.34 = (bf16[1,192,512]{2,1,0:T(8,128)(2,1)}, bf16[1,192,512]{2,1,0:T(8,128)(2,1)}, u32[]{:S(2)}, u32[]{:S(2)}) collective-permute-start(bf16[1,192,512]{2,1,0:T(8,128)(2,1)} %get-tuple-element.94), channel_id=1, source_target_pairs={{0,12},{4,8},{8,4},{12,0},{16,28},{20,24},{24,20},{28,16},{1,13},{... | collective-permute-start | bytes 589832 | tf_op jit(solution)/shard_map/ppermute | solution.py:421
  69.6 1.5 collective-permute-start.37
  72.3 14.0 %rows.9 = (bf16[2,192,512]{2,1,0:T(8,128)(2,1)}, bf16[2,192,512]{2,1,0:T(8,128)(2,1)}, bf16[2,192,512]{2,1,0:T(8,128)(2,1)}, bf16[2,192,512]{2,1,0:T(8,128)(2,1)...) custom-call(s32[8]{0:T(128)S(1)} %fusion.psf_of_ref, ...), custom_call_target="tpu_custom_call" | custom-call | flops 4831838208 | bytes 8650752 | tf_op jit(solution)/shard_map/rows/pallas_call | solution.py:382
  86.3 21.3 %collective-permute-done.36.refs_5_ = bf16[1,192,512]{2,1,0:T(8,128)(2,1)S(1)} collective-permute-done((bf16[1,192,512]{2,1,0:T(8,128)(2,1)}, bf16[1,192,512]{2,1,0:T(8,128)(2,1)S(1)}, u32[]{:S(2)}, u32[]{:S(2)}) %collective-permute-start.36) | collective-permute-done | bytes 196640 | tf_op jit(solution)/shard_map/ppermute | solution.py:421
  110.9 14.0 %rows.8 = (bf16[2,192,512]{2,1,0:T(8,128)(2,1)}, bf16[2,192,512]{2,1,0:T(8,128)(2,1)}, bf16[2,192,512]{2,1,0:T(8,128)(2,1)}, bf16[2,192,512]{2,1,0:T(8,128)(2,1)...) custom-call(s32[8]{0:T(128)S(1)} %fusion.psf_of_ref, ...), custom_call_target="tpu_custom_call" | custom-call | flops 4831838208 | bytes 8650752 | tf_op jit(solution)/shard_map/rows/pallas_call | solution.py:382
  125.5 1.5 collective-permute-start.30
  129.9 23.3 %collective-permute-done.29.refs_5_ = bf16[2,192,512]{2,1,0:T(8,128)(2,1)} collective-permute-done((bf16[2,192,512]{2,1,0:T(8,128)(2,1)S(1)}, bf16[2,192,512]{2,1,0:T(8,128)(2,1)}, u32[]{:S(2)}, u32[]{:S(2)}) %collective-permute-start.29) | collective-permute-done | bytes 393248 | tf_op jit(solution)/shard_map/ppermute | solution.py:421
  156.8 2.8 %pixphases.3.refs_8_ = bf16[512,1536]{1,0:T(8,128)(2,1)} custom-call(), custom_call_target="tpu_custom_call" | custom-call | tf_op jit(solution)/shard_map/pixphases/pallas_call | solution.py:368
  159.6 1.9 pixphases.2.refs_8_
  161.5 1.6 collective-permute-start.24
  164.5 3.8 %pixels.6.refs_10_ = f32[8,1,512,512]{3,2,1,0:T(8,128)} custom-call(bf16[1,192,512]{2,1,0:T(8,128)(2,1)} %get-tuple-element.99.refs_0_, bf16[1,192,512]{2,1,0:T(8,128)(2,1)} %collective-permute-done.39.refs_1_, bf16[1,192,512]{2,1,0:T(8,128)(2,1)} %copy-done.10, bf16[1,192,512]{2,1,0:T(8,128)(2,1)} %copy-done.11, bf16[1,192,512]{2,1,0:T(8,128)(2,1)} %copy-done.12, ...), custom_call_target="tpu_custom_call" | custom-call | flops 805306368 | bytes 3670016 | tf_op jit(solution)/shard_map/pixels/pallas_call | solution.py:427
  168.3 3.8 %pixels.7.refs_10_ = f32[8,1,512,512]{3,2,1,0:T(8,128)} custom-call(bf16[1,192,512]{2,1,0:T(8,128)(2,1)} %get-tuple-element.91.refs_0_, bf16[1,192,512]{2,1,0:T(8,128)(2,1)} %copy-done.16, bf16[1,192,512]{2,1,0:T(8,128)(2,1)} %copy-done.17, bf16[1,192,512]{2,1,0:T(8,128)(2,1)} %collective-permute-done.34.refs_3_, ...), custom_call_target="tpu_custom_call", output_to_operand_aliasing={{}: (10, {})} | custom-call | flops 805306368 | bytes 3670016 | tf_op jit(solution)/shard_map/pixels/pallas_call | solution.py:427
  172.1 8.0 %rows.7 = (bf16[1,104,512]{2,1,0:T(8,128)(2,1)}, bf16[1,104,512]{2,1,0:T(8,128)(2,1)}, bf16[1,104,512]{2,1,0:T(8,128)(2,1)}, bf16[1,104,512]{2,1,0:T(8,128)(2,1)...) custom-call(s32[8]{0:T(128)S(1)} %fusion.psf_of_ref, ...), custom_call_target="tpu_custom_call" | custom-call | flops 1610612736 | bytes 5177344 | tf_op jit(solution)/shard_map/rows/pallas_call | solution.py:382
  180.3 2.9 %collective-permute-done.21.refs_4_ = bf16[2,192,512]{2,1,0:T(8,128)(2,1)} collective-permute-done((bf16[2,192,512]{2,1,0:T(8,128)(2,1)}, bf16[2,192,512]{2,1,0:T(8,128)(2,1)}, u32[]{:S(2)}, u32[]{:S(2)}) %collective-permute-start.21) | collective-permute-done | bytes 393248 | tf_op jit(solution)/shard_map/ppermute | solution.py:421
  184.4 5.5 %collective-permute-done.22.refs_5_ = bf16[2,192,512]{2,1,0:T(8,128)(2,1)} collective-permute-done((bf16[2,192,512]{2,1,0:T(8,128)(2,1)}, bf16[2,192,512]{2,1,0:T(8,128)(2,1)}, u32[]{:S(2)}, u32[]{:S(2)}) %collective-permute-start.22) | collective-permute-done | bytes 393248 | tf_op jit(solution)/shard_map/ppermute | solution.py:421
  189.9 1.5 collective-permute-start.13
  192.1 7.8 %rows.6 = (bf16[1,104,512]{2,1,0:T(8,128)(2,1)}, bf16[1,104,512]{2,1,0:T(8,128)(2,1)}, bf16[1,104,512]{2,1,0:T(8,128)(2,1)}, bf16[1,104,512]{2,1,0:T(8,128)(2,1)...) custom-call(s32[8]{0:T(128)S(1)} %fusion.psf_of_ref, ...), custom_call_target="tpu_custom_call" | custom-call | flops 1610612736 | bytes 5177344 | tf_op jit(solution)/shard_map/rows/pallas_call | solution.py:382
  201.9 1.7 collective-permute-start.17
  204.5 4.9 %pixels.8.refs_10_ = f32[8,1,512,512]{3,2,1,0:T(8,128)} custom-call(bf16[2,192,512]{2,1,0:T(8,128)(2,1)} %get-tuple-element.83.refs_0_, bf16[2,192,512]{2,1,0:T(8,128)(2,1)} %collective-permute-done.25.refs_1_, bf16[2,192,512]{2,1,0:T(8,128)(2,1)} %collective-permute-done.26.refs_2_, ...), custom_call_target="tpu_custom_call", output_to_operand_aliasing={{}: (10, {})} | custom-call | flops 1610612736 | bytes 7340032 | tf_op jit(solution)/shard_map/pixels/pallas_call | solution.py:427
  214.9 4.9 %pixels.9.refs_10_ = f32[8,1,512,512]{3,2,1,0:T(8,128)} custom-call(bf16[2,192,512]{2,1,0:T(8,128)(2,1)} %get-tuple-element.75.refs_0_, bf16[2,192,512]{2,1,0:T(8,128)(2,1)} %collective-permute-done.18.refs_1_, bf16[2,192,512]{2,1,0:T(8,128)(2,1)} %collective-permute-done.19.refs_2_, ...), custom_call_target="tpu_custom_call", output_to_operand_aliasing={{}: (10, {})} | custom-call | flops 1610612736 | bytes 7340032 | tf_op jit(solution)/shard_map/pixels/pallas_call | solution.py:427
  219.8 2.9 %pixels.10.refs_10_ = f32[8,1,512,512]{3,2,1,0:T(8,128)} custom-call(bf16[1,104,512]{2,1,0:T(8,128)(2,1)S(1)} %copy-done.5, bf16[1,104,512]{2,1,0:T(8,128)(2,1)S(1)} %collective-permute-done.11.refs_1_, bf16[1,104,512]{2,1,0:T(8,128)(2,1)S(1)} %collective-permute-done.12.refs_2_, ...), custom_call_target="tpu_custom_call", output_to_operand_aliasing={{}: (10, {})} | custom-call | flops 436207616 | bytes 2949120 | tf_op jit(solution)/shard_map/pixels/pallas_call | solution.py:427
  222.8 2.9 %pixels.11 = f32[8,1,512,512]{3,2,1,0:T(8,128)} custom-call(bf16[1,104,512]{2,1,0:T(8,128)(2,1)S(1)} %copy-done.6, bf16[1,104,512]{2,1,0:T(8,128)(2,1)S(1)} %collective-permute-done.3.refs_1_, bf16[1,104,512]{2,1,0:T(8,128)(2,1)S(1)} %collective-permute-done.4.refs_2_, ...), custom_call_target="tpu_custom_call", output_to_operand_aliasing={{}: (10, {})} | custom-call | flops 436207616 | bytes 2949120 | tf_op jit(solution)/shard_map/pixels/pallas_call | solution.py:427
  (148 shorter events, 40.7 us)
Async XLA Ops:
  39.7 13.4 %collective-permute-start.40 = (bf16[1,192,512]{2,1,0:T(8,128)(2,1)}, bf16[1,192,512]{2,1,0:T(8,128)(2,1)S(1)}, u32[]{:S(2)}, u32[]{:S(2)}) collective-permute-start(bf16[1,192,512]{2,1,0:T(8,128)(2,1)} %get-tuple-element.101), channel_id=1, source_target_pairs={{0,8},{4,12},{8,0},{12,4},{16,24},{20,28},{24,16},{28,20},{1,9},{5... | collective-permute-start | bytes 589832 | tf_op jit(solution)/shard_map/ppermute | solution.py:421
  40.9 13.3 %collective-permute-start.41 = (bf16[1,192,512]{2,1,0:T(8,128)(2,1)}, bf16[1,192,512]{2,1,0:T(8,128)(2,1)S(1)}, u32[]{:S(2)}, u32[]{:S(2)}) collective-permute-start(bf16[1,192,512]{2,1,0:T(8,128)(2,1)} %get-tuple-element.102), channel_id=1, source_target_pairs={{0,12},{4,8},{8,4},{12,0},{16,28},{20,24},{24,20},{28,16},{1,13},{... | collective-permute-start | bytes 589832 | tf_op jit(solution)/shard_map/ppermute | solution.py:421
  41.2 13.6 %collective-permute-start.42 = (bf16[1,192,512]{2,1,0:T(8,128)(2,1)}, bf16[1,192,512]{2,1,0:T(8,128)(2,1)S(1)}, u32[]{:S(2)}, u32[]{:S(2)}) collective-permute-start(bf16[1,192,512]{2,1,0:T(8,128)(2,1)} %get-tuple-element.103), channel_id=1, source_target_pairs={{0,16},{4,20},{8,24},{12,28},{16,0},{20,4},{24,8},{28,12},{1,17},{... | collective-permute-start | bytes 589832 | tf_op jit(solution)/shard_map/ppermute | solution.py:421
  42.4 14.5 %collective-permute-start.43 = (bf16[1,192,512]{2,1,0:T(8,128)(2,1)}, bf16[1,192,512]{2,1,0:T(8,128)(2,1)S(1)}, u32[]{:S(2)}, u32[]{:S(2)}) collective-permute-start(bf16[1,192,512]{2,1,0:T(8,128)(2,1)} %get-tuple-element.104), channel_id=1, source_target_pairs={{0,20},{4,16},{8,28},{12,24},{16,4},{20,0},{24,12},{28,8},{1,21},{... | collective-permute-start | bytes 589832 | tf_op jit(solution)/shard_map/ppermute | solution.py:421
  43.2 19.3 %collective-permute-start.44 = (bf16[1,192,512]{2,1,0:T(8,128)(2,1)}, bf16[1,192,512]{2,1,0:T(8,128)(2,1)S(1)}, u32[]{:S(2)}, u32[]{:S(2)}) collective-permute-start(bf16[1,192,512]{2,1,0:T(8,128)(2,1)} %get-tuple-element.105), channel_id=1, source_target_pairs={{0,24},{4,28},{8,16},{12,20},{16,8},{20,12},{24,0},{28,4},{1,25},{... | collective-permute-start | bytes 589832 | tf_op jit(solution)/shard_map/ppermute | solution.py:421
  54.9 12.4 %collective-permute-start.33 = (bf16[1,192,512]{2,1,0:T(8,128)(2,1)}, bf16[1,192,512]{2,1,0:T(8,128)(2,1)S(1)}, u32[]{:S(2)}, u32[]{:S(2)}) collective-permute-start(bf16[1,192,512]{2,1,0:T(8,128)(2,1)} %get-tuple-element.93), channel_id=1, source_target_pairs={{0,8},{4,12},{8,0},{12,4},{16,24},{20,28},{24,16},{28,20},{1,9},{5... | collective-permute-start | bytes 589832 | tf_op jit(solution)/shard_map/ppermute | solution.py:421
  57.0 12.7 %collective-permute-start.34 = (bf16[1,192,512]{2,1,0:T(8,128)(2,1)}, bf16[1,192,512]{2,1,0:T(8,128)(2,1)}, u32[]{:S(2)}, u32[]{:S(2)}) collective-permute-start(bf16[1,192,512]{2,1,0:T(8,128)(2,1)} %get-tuple-element.94), channel_id=1, source_target_pairs={{0,12},{4,8},{8,4},{12,0},{16,28},{20,24},{24,20},{28,16},{1,13},{... | collective-permute-start | bytes 589832 | tf_op jit(solution)/shard_map/ppermute | solution.py:421
  64.6 44.9 %collective-permute-start.10 = (bf16[4,1,2,48,768]{4,3,2,1,0:T(8,128)(2,1)S(1)}, bf16[4,1,2,48,768]{4,3,2,1,0:T(8,128)(2,1)S(1)}, u32[]{:S(2)}, u32[]{:S(2)}) collective-permute-start(bf16[4,1,2,48,768]{4,3,2,1,0:T(8,128)(2,1)S(1)} %get-tuple-element.107), channel_id=1, source_target_pairs={{0,28},{4,24},{8,20},{12,16},{16,12},{20,8},{24,4},{28,0},{1,29},{... | collective-permute-start | bytes 1769480 | tf_op jit(solution)/shard_map/ppermute | solution.py:316
  65.8 59.2 %collective-permute-start.2 = (bf16[4,1,2,48,768]{4,3,2,1,0:T(8,128)(2,1)S(1)}, bf16[4,1,2,48,768]{4,3,2,1,0:T(8,128)(2,1)}, u32[]{:S(2)}, u32[]{:S(2)}) collective-permute-start(bf16[4,1,2,48,768]{4,3,2,1,0:T(8,128)(2,1)S(1)} %get-tuple-element.108), channel_id=1, source_target_pairs={{0,28},{4,24},{8,20},{12,16},{16,12},{20,8},{24,4},{28,0},{1,29},{... | collective-permute-start | bytes 1769480 | tf_op jit(solution)/shard_map/ppermute | solution.py:316
  67.9 39.7 %collective-permute-start.36 = (bf16[1,192,512]{2,1,0:T(8,128)(2,1)}, bf16[1,192,512]{2,1,0:T(8,128)(2,1)S(1)}, u32[]{:S(2)}, u32[]{:S(2)}) collective-permute-start(bf16[1,192,512]{2,1,0:T(8,128)(2,1)} %get-tuple-element.96), channel_id=1, source_target_pairs={{0,20},{4,16},{8,28},{12,24},{16,4},{20,0},{24,12},{28,8},{1,21},{... | collective-permute-start | bytes 589832 | tf_op jit(solution)/shard_map/ppermute | solution.py:421
  69.6 38.2 %collective-permute-start.37 = (bf16[1,192,512]{2,1,0:T(8,128)(2,1)}, bf16[1,192,512]{2,1,0:T(8,128)(2,1)S(1)}, u32[]{:S(2)}, u32[]{:S(2)}) collective-permute-start(bf16[1,192,512]{2,1,0:T(8,128)(2,1)} %get-tuple-element.97), channel_id=1, source_target_pairs={{0,24},{4,28},{8,16},{12,20},{16,8},{20,12},{24,0},{28,4},{1,25},{... | collective-permute-start | bytes 589832 | tf_op jit(solution)/shard_map/ppermute | solution.py:421
  71.1 38.0 %collective-permute-start.38 = (bf16[1,192,512]{2,1,0:T(8,128)(2,1)}, bf16[1,192,512]{2,1,0:T(8,128)(2,1)S(1)}, u32[]{:S(2)}, u32[]{:S(2)}) collective-permute-start(bf16[1,192,512]{2,1,0:T(8,128)(2,1)} %get-tuple-element.98), channel_id=1, source_target_pairs={{0,28},{4,24},{8,20},{12,16},{16,12},{20,8},{24,4},{28,0},{1,29},{... | collective-permute-start | bytes 589832 | tf_op jit(solution)/shard_map/ppermute | solution.py:421
  107.7 17.8 %collective-permute-start.25 = (bf16[2,192,512]{2,1,0:T(8,128)(2,1)}, bf16[2,192,512]{2,1,0:T(8,128)(2,1)}, u32[]{:S(2)}, u32[]{:S(2)}) collective-permute-start(bf16[2,192,512]{2,1,0:T(8,128)(2,1)} %get-tuple-element.84), channel_id=1, source_target_pairs={{0,4},{4,0},{8,12},{12,8},{16,20},{20,16},{24,28},{28,24},{1,5},{5... | collective-permute-start | bytes 1179656 | tf_op jit(solution)/shard_map/ppermute | solution.py:421
  107.8 19.3 %collective-permute-start.26 = (bf16[2,192,512]{2,1,0:T(8,128)(2,1)}, bf16[2,192,512]{2,1,0:T(8,128)(2,1)}, u32[]{:S(2)}, u32[]{:S(2)}) collective-permute-start(bf16[2,192,512]{2,1,0:T(8,128)(2,1)} %get-tuple-element.85), channel_id=1, source_target_pairs={{0,8},{4,12},{8,0},{12,4},{16,24},{20,28},{24,16},{28,20},{1,9},{5... | collective-permute-start | bytes 1179656 | tf_op jit(solution)/shard_map/ppermute | solution.py:421
  109.1 19.1 %collective-permute-start.27 = (bf16[2,192,512]{2,1,0:T(8,128)(2,1)}, bf16[2,192,512]{2,1,0:T(8,128)(2,1)}, u32[]{:S(2)}, u32[]{:S(2)}) collective-permute-start(bf16[2,192,512]{2,1,0:T(8,128)(2,1)} %get-tuple-element.86), channel_id=1, source_target_pairs={{0,12},{4,8},{8,4},{12,0},{16,28},{20,24},{24,20},{28,16},{1,13},{... | collective-permute-start | bytes 1179656 | tf_op jit(solution)/shard_map/ppermute | solution.py:421
  109.6 19.0 %collective-permute-start.28 = (bf16[2,192,512]{2,1,0:T(8,128)(2,1)}, bf16[2,192,512]{2,1,0:T(8,128)(2,1)}, u32[]{:S(2)}, u32[]{:S(2)}) collective-permute-start(bf16[2,192,512]{2,1,0:T(8,128)(2,1)} %get-tuple-element.87), channel_id=1, source_target_pairs={{0,16},{4,20},{8,24},{12,28},{16,0},{20,4},{24,8},{28,12},{1,17},{... | collective-permute-start | bytes 1179656 | tf_op jit(solution)/shard_map/ppermute | solution.py:421
  125.0 28.2 %collective-permute-start.29 = (bf16[2,192,512]{2,1,0:T(8,128)(2,1)S(1)}, bf16[2,192,512]{2,1,0:T(8,128)(2,1)}, u32[]{:S(2)}, u32[]{:S(2)}) collective-permute-start(bf16[2,192,512]{2,1,0:T(8,128)(2,1)S(1)} %copy-done.23), channel_id=1, source_target_pairs={{0,20},{4,16},{8,28},{12,24},{16,4},{20,0},{24,12},{28,8},{1,21},{... | collective-permute-start | bytes 1179656 | tf_op jit(solution)/shard_map/ppermute | solution.py:421
  125.5 28.5 %collective-permute-start.30 = (bf16[2,192,512]{2,1,0:T(8,128)(2,1)S(1)}, bf16[2,192,512]{2,1,0:T(8,128)(2,1)}, u32[]{:S(2)}, u32[]{:S(2)}) collective-permute-start(bf16[2,192,512]{2,1,0:T(8,128)(2,1)S(1)} %copy-done.22), channel_id=1, source_target_pairs={{0,24},{4,28},{8,16},{12,20},{16,8},{20,12},{24,0},{28,4},{1,25},{... | collective-permute-start | bytes 1179656 | tf_op jit(solution)/shard_map/ppermute | solution.py:421
  127.1 28.2 %collective-permute-start.31 = (bf16[2,192,512]{2,1,0:T(8,128)(2,1)S(1)}, bf16[2,192,512]{2,1,0:T(8,128)(2,1)}, u32[]{:S(2)}, u32[]{:S(2)}) collective-permute-start(bf16[2,192,512]{2,1,0:T(8,128)(2,1)S(1)} %copy-done.21), channel_id=1, source_target_pairs={{0,28},{4,24},{8,20},{12,16},{16,12},{20,8},{24,4},{28,0},{1,29},{... | collective-permute-start | bytes 1179656 | tf_op jit(solution)/shard_map/ppermute | solution.py:421
  128.2 27.3 %collective-permute-start.18 = (bf16[2,192,512]{2,1,0:T(8,128)(2,1)}, bf16[2,192,512]{2,1,0:T(8,128)(2,1)}, u32[]{:S(2)}, u32[]{:S(2)}) collective-permute-start(bf16[2,192,512]{2,1,0:T(8,128)(2,1)} %get-tuple-element.76), channel_id=1, source_target_pairs={{0,4},{4,0},{8,12},{12,8},{16,20},{20,16},{24,28},{28,24},{1,5},{5... | collective-permute-start | bytes 1179656 | tf_op jit(solution)/shard_map/ppermute | solution.py:421
  128.6 32.9 %collective-permute-start.19 = (bf16[2,192,512]{2,1,0:T(8,128)(2,1)}, bf16[2,192,512]{2,1,0:T(8,128)(2,1)}, u32[]{:S(2)}, u32[]{:S(2)}) collective-permute-start(bf16[2,192,512]{2,1,0:T(8,128)(2,1)} %get-tuple-element.77), channel_id=1, source_target_pairs={{0,8},{4,12},{8,0},{12,4},{16,24},{20,28},{24,16},{28,20},{1,9},{5... | collective-permute-start | bytes 1179656 | tf_op jit(solution)/shard_map/ppermute | solution.py:421
  153.2 26.9 %collective-permute-start.20 = (bf16[2,192,512]{2,1,0:T(8,128)(2,1)}, bf16[2,192,512]{2,1,0:T(8,128)(2,1)}, u32[]{:S(2)}, u32[]{:S(2)}) collective-permute-start(bf16[2,192,512]{2,1,0:T(8,128)(2,1)} %get-tuple-element.78), channel_id=1, source_target_pairs={{0,12},{4,8},{8,4},{12,0},{16,28},{20,24},{24,20},{28,16},{1,13},{... | collective-permute-start | bytes 1179656 | tf_op jit(solution)/shard_map/ppermute | solution.py:421
  154.0 29.2 %collective-permute-start.21 = (bf16[2,192,512]{2,1,0:T(8,128)(2,1)}, bf16[2,192,512]{2,1,0:T(8,128)(2,1)}, u32[]{:S(2)}, u32[]{:S(2)}) collective-permute-start(bf16[2,192,512]{2,1,0:T(8,128)(2,1)} %get-tuple-element.79), channel_id=1, source_target_pairs={{0,16},{4,20},{8,24},{12,28},{16,0},{20,4},{24,8},{28,12},{1,17},{... | collective-permute-start | bytes 1179656 | tf_op jit(solution)/shard_map/ppermute | solution.py:421
  155.2 34.7 %collective-permute-start.22 = (bf16[2,192,512]{2,1,0:T(8,128)(2,1)}, bf16[2,192,512]{2,1,0:T(8,128)(2,1)}, u32[]{:S(2)}, u32[]{:S(2)}) collective-permute-start(bf16[2,192,512]{2,1,0:T(8,128)(2,1)} %get-tuple-element.80), channel_id=1, source_target_pairs={{0,20},{4,16},{8,28},{12,24},{16,4},{20,0},{24,12},{28,8},{1,21},{... | collective-permute-start | bytes 1179656 | tf_op jit(solution)/shard_map/ppermute | solution.py:421
  155.5 35.9 %collective-permute-start.23 = (bf16[2,192,512]{2,1,0:T(8,128)(2,1)}, bf16[2,192,512]{2,1,0:T(8,128)(2,1)}, u32[]{:S(2)}, u32[]{:S(2)}) collective-permute-start(bf16[2,192,512]{2,1,0:T(8,128)(2,1)} %get-tuple-element.81), channel_id=1, source_target_pairs={{0,24},{4,28},{8,16},{12,20},{16,8},{20,12},{24,0},{28,4},{1,25},{... | collective-permute-start | bytes 1179656 | tf_op jit(solution)/shard_map/ppermute | solution.py:421
  161.5 38.3 %collective-permute-start.24 = (bf16[2,192,512]{2,1,0:T(8,128)(2,1)}, bf16[2,192,512]{2,1,0:T(8,128)(2,1)S(1)}, u32[]{:S(2)}, u32[]{:S(2)}) collective-permute-start(bf16[2,192,512]{2,1,0:T(8,128)(2,1)} %get-tuple-element.82), channel_id=1, source_target_pairs={{0,28},{4,24},{8,20},{12,16},{16,12},{20,8},{24,4},{28,0},{1,29},{... | collective-permute-start | bytes 1179656 | tf_op jit(solution)/shard_map/ppermute | solution.py:421
  180.1 20.3 %collective-permute-start.11 = (bf16[1,104,512]{2,1,0:T(8,128)(2,1)}, bf16[1,104,512]{2,1,0:T(8,128)(2,1)S(1)}, u32[]{:S(2)}, u32[]{:S(2)}) collective-permute-start(bf16[1,104,512]{2,1,0:T(8,128)(2,1)} %get-tuple-element.68), channel_id=1, source_target_pairs={{0,4},{4,0},{8,12},{12,8},{16,20},{20,16},{24,28},{28,24},{1,5},{5... | collective-permute-start | bytes 319496 | tf_op jit(solution)/shard_map/ppermute | solution.py:421
  183.1 18.7 %collective-permute-start.12 = (bf16[1,104,512]{2,1,0:T(8,128)(2,1)}, bf16[1,104,512]{2,1,0:T(8,128)(2,1)S(1)}, u32[]{:S(2)}, u32[]{:S(2)}) collective-permute-start(bf16[1,104,512]{2,1,0:T(8,128)(2,1)} %get-tuple-element.69), channel_id=1, source_target_pairs={{0,8},{4,12},{8,0},{12,4},{16,24},{20,28},{24,16},{28,20},{1,9},{5... | collective-permute-start | bytes 319496 | tf_op jit(solution)/shard_map/ppermute | solution.py:421
  189.9 13.7 %collective-permute-start.13 = (bf16[1,104,512]{2,1,0:T(8,128)(2,1)}, bf16[1,104,512]{2,1,0:T(8,128)(2,1)S(1)}, u32[]{:S(2)}, u32[]{:S(2)}) collective-permute-start(bf16[1,104,512]{2,1,0:T(8,128)(2,1)} %get-tuple-element.70), channel_id=1, source_target_pairs={{0,12},{4,8},{8,4},{12,0},{16,28},{20,24},{24,20},{28,16},{1,13},{... | collective-permute-start | bytes 319496 | tf_op jit(solution)/shard_map/ppermute | solution.py:421
  191.4 12.3 %collective-permute-start.14 = (bf16[1,104,512]{2,1,0:T(8,128)(2,1)}, bf16[1,104,512]{2,1,0:T(8,128)(2,1)S(1)}, u32[]{:S(2)}, u32[]{:S(2)}) collective-permute-start(bf16[1,104,512]{2,1,0:T(8,128)(2,1)} %get-tuple-element.71), channel_id=1, source_target_pairs={{0,16},{4,20},{8,24},{12,28},{16,0},{20,4},{24,8},{28,12},{1,17},{... | collective-permute-start | bytes 319496 | tf_op jit(solution)/shard_map/ppermute | solution.py:421
  209.6 13.1 %collective-permute-start.5 = (bf16[1,104,512]{2,1,0:T(8,128)(2,1)S(1)}, bf16[1,104,512]{2,1,0:T(8,128)(2,1)S(1)}, u32[]{:S(2)}, u32[]{:S(2)}) collective-permute-start(bf16[1,104,512]{2,1,0:T(8,128)(2,1)S(1)} %copy-done.29), channel_id=1, source_target_pairs={{0,12},{4,8},{8,4},{12,0},{16,28},{20,24},{24,20},{28,16},{1,13},{... | collective-permute-start | bytes 319496 | tf_op jit(solution)/shard_map/ppermute | solution.py:421
  210.5 12.3 %collective-permute-start.6 = (bf16[1,104,512]{2,1,0:T(8,128)(2,1)S(1)}, bf16[1,104,512]{2,1,0:T(8,128)(2,1)S(1)}, u32[]{:S(2)}, u32[]{:S(2)}) collective-permute-start(bf16[1,104,512]{2,1,0:T(8,128)(2,1)S(1)} %copy-done.28), channel_id=1, source_target_pairs={{0,16},{4,20},{8,24},{12,28},{16,0},{20,4},{24,8},{28,12},{1,17},{... | collective-permute-start | bytes 319496 | tf_op jit(solution)/shard_map/ppermute | solution.py:421
  (47 other events, 527.1 us)

commit v5 on v4

--- a/solution.py
+++ b/solution.py
@@ -48,9 +48,16 @@
     out_ref[3 * ntile, 5:] = jnp.zeros((rest, out_ref.shape[2]), f32)
 
 
-def solve_kernel(psf_ref, one_ref, two_ref, out_ref):
+def total_of(parts):
+    while len(parts) > 1:
+        parts = [a + b for a, b in zip(parts[::2], parts[1::2])]
+    return parts[0]
+
+
+def solve_kernel(psf_ref, *refs):
+    refs, out_ref = refs[:-1], refs[-1]
     ntile = (out_ref.shape[0] - 1) // 3
-    gram = one_ref[3 * ntile] + two_ref[3 * ntile]
+    gram = total_of([ref[3 * ntile] for ref in refs])
     g0, g1, g2, g3, g4 = (gram[j : j + 1] for j in range(5))
     c00 = g2 * g4 - g3 * g3
     c01 = g2 * g3 - g1 * g4
@@ -60,7 +67,7 @@
     c22 = g0 * g2 - g1 * g1
     det = g0 * c00 + g1 * c01 + g2 * c02
     for t in range(ntile):
-        m0, m1, m2 = (one_ref[j * ntile + t] + two_ref[j * ntile + t] for j in range(3))
+        m0, m1, m2 = (total_of([ref[j * ntile + t] for ref in refs]) for j in range(3))
         out_ref[t] = ((c00 * m0 + c01 * m1 + c02 * m2) / det).astype(bf16)
         out_ref[ntile + t] = ((c01 * m0 + c11 * m1 + c12 * m2) / det).astype(bf16)
         out_ref[2 * ntile + t] = ((c02 * m0 + c12 * m1 + c22 * m2) / det).astype(bf16)
@@ -279,6 +286,14 @@
 
 def pairs_of(nch, nf, kb, frame):
     return NPAIR if nch >= NPAIR + 4 and frame == nf * kb and kb % (2 * TILE) == 0 else 0
+
+
+def rounds_of(nz):
+    rounds, stride = [], 1
+    while stride < nz:
+        rounds.append((stride, min(4, nz // stride)))
+        stride *= rounds[-1][1]
+    return rounds
 
 
 def send_order(nf):
@@ -348,18 +363,19 @@
         name="colphases",
     )(in_hbm(tile_pos.T))
     col_table = col_table.reshape(FCOLS, ntile * ts, frame)
-    other = jnp.zeros_like(sums)
-    for i in range(nz.bit_length() - 1):
-        if i:
-            sums = sums + other
-        other = lax.ppermute(sums, "freq", [(s, s ^ (1 << i)) for s in range(nz)])
+    terms = [sums]
+    for stride, size in rounds_of(nz):
+        sums = total_of(terms)
+        terms = [sums] + [None] * (size - 1)
+        for h in range(size - 1, 0, -1):
+            terms[h] = lax.ppermute(sums, "freq", [(s, s ^ (stride * h)) for s in range(nz)])
     fit = pl.pallas_call(
         solve_kernel,
         out_shape=jax.ShapeDtypeStruct((3 * ntile + 1, rows, ts), bf16),
-        in_specs=[SMEM, VMEM, VMEM],
+        in_specs=[SMEM] + [VMEM] * len(terms),
         out_specs=VMEM,
         name="solve",
-    )(facet_psf, sums, other)
+    )(facet_psf, *terms)
     fit = lax.all_gather(fit, "facet", axis=0)
     psf_of = fit[:, 3 * ntile, 0, 0].astype(i32)
     rb_pair, block_pair = kb // 2 + TILE, kb + EXTRA

time: 226 us -> 242 us (1.071)
  waiting for transfers between devices: 57.9 us -> 79.7 us
  starting transfers between devices: 52.8 us -> 46.9 us
    ppermute x42, waiting for transfers between devices: 54.7 us -> 78.1 us  [shards(): got[j] = lax.ppermute(w[j], 'facet', [(s, s ^ j) for s in range(nf)])]
    ppermute x42, starting transfers between devices: 44.3 us -> 39.5 us  [shards(): got[j] = lax.ppermute(w[j], 'facet', [(s, s ^ j) for s in range(nf)])]
    ppermute x2 -> x3, starting transfers between devices: 5.87 us -> 5.64 us  [shards(): lax.ppermute(sums, 'freq', [(s, s ^ stride * h) for s in range(nz)])]
  transfers between devices with their start and end apart: 46 -> 47, of which waited for: 8 -> 11; matrix products, arithmetic and copies ran while one was open for 1% -> 1% of each run, Pallas kernels for 37% -> 35%
where the time goes in v5:
time: 242 us; the launch traced here: 241 us
  Pallas kernels  99.4 us (41%)
  waiting for transfers between devices  79.7 us (33%)
  starting transfers between devices  46.9 us (19%)
  blocking collectives  9.97 us (4%)
  local copies, waits for them, and re-layouts  3.87 us (2%)
    ppermute x42, waiting for transfers between devices, shards(): got[j] = lax.ppermute(w[j], 'facet', [(s, s ^ j) for s in range(nf)])  78.1 us
    pallas_call x6, Pallas kernels, shards(): pl.pallas_call(functools.partial(rows_kernel, total, nch, chan0, paired),...  61.6 us
    ppermute x42, starting transfers between devices, shards(): got[j] = lax.ppermute(w[j], 'facet', [(s, s ^ j) for s in range(nf)])  39.5 us
    pallas_call x6, Pallas kernels, shards(): pl.pallas_call(functools.partial(pixels_kernel, nf, 1.0 / (frame * frame)...  23.2 us
    all_gather x1, blocking collectives, shards(): fit = lax.all_gather(fit, 'facet', axis=0)  9.97 us
    ppermute x3, starting transfers between devices, shards(): lax.ppermute(sums, 'freq', [(s, s ^ stride * h) for s in range(nz)])  5.64 us
  transfers between devices with their start and end apart: 47, of which 11 were waited for; matrix products, arithmetic and copies ran while one was open for 1% of the time, Pallas kernels for 35%

profile of v5, /device:TPU:0, one launch (start us, length us, event | category | flops | bytes accessed | tf_op | source)
XLA Modules:
  0.0 241.1 jit_solution(10847290565696362700)
XLA Ops:
  1.6 3.1 %collective-permute-start = (f32[13,16,128]{2,1,0:T(8,128)}, f32[13,16,128]{2,1,0:T(8,128)}, u32[]{:S(2)}, u32[]{:S(2)}) collective-permute-start(f32[13,16,128]{2,1,0:T(8,128)} %moments.1.refs_0_), channel_id=1, source_target_pairs={{0,1},{1,0},{2,3},{3,2},{4,5},{5,4},{6,7},{7,6},{8,9},{9,8},{10,11... | collective-permute-start | bytes 319496 | tf_op jit(solution)/shard_map/ppermute | solution.py:371
  4.7 2.6 %collective-permute-start.1 = (f32[13,16,128]{2,1,0:T(8,128)}, f32[13,16,128]{2,1,0:T(8,128)}, u32[]{:S(2)}, u32[]{:S(2)}) collective-permute-start(f32[13,16,128]{2,1,0:T(8,128)} %moments.1.refs_0_), channel_id=1, source_target_pairs={{0,2},{1,3},{2,0},{3,1},{4,6},{5,7},{6,4},{7,5},{8,10},{9,11},{10,... | collective-permute-start | bytes 319496 | tf_op jit(solution)/shard_map/ppermute | solution.py:371
  7.3 3.7 %rowphases.1 = (bf16[2,4,192,128]{3,2,1,0:T(8,128)(2,1)S(1)}, bf16[768,512]{1,0:T(8,128)(2,1)}, bf16[384,384]{1,0:T(8,128)(2,1)}) custom-call(s32[2,4]{1,0:T(2,128)} %bitcast.16), custom_call_target="tpu_custom_call" | custom-call | tf_op jit(solution)/shard_map/rowphases/pallas_call | solution.py:339
  11.0 2.8 %colphases.1 = bf16[16,128,768]{2,1,0:T(8,128)(2,1)S(1)} custom-call(s32[2,4]{1,0:T(2,128)} %bitcast.17), custom_call_target="tpu_custom_call" | custom-call | tf_op jit(solution)/shard_map/colphases/pallas_call | solution.py:356
  17.7 10.0 %all-gather = bf16[104,16,128]{2,1,0:T(8,128)(2,1)S(1)} all-gather(bf16[13,16,128]{2,1,0:T(8,128)(2,1)} %solve.1), channel_id=2, replica_groups=mesh['facet'=8,'freq'=4] {'facet'}, dimensions={0}, use_global_device_ids=true | all-gather | bytes 479232 | tf_op jit(solution)/shard_map/all_gather | solution.py:379
  28.0 8.8 %rows.11 = (bf16[1,192,512]{2,1,0:T(8,128)(2,1)}, bf16[1,192,512]{2,1,0:T(8,128)(2,1)}, bf16[1,192,512]{2,1,0:T(8,128)(2,1)}, bf16[1,192,512]{2,1,0:T(8,128)(2,1...) custom-call(s32[8]{0:T(128)S(1)} %fusion.psf_of_ref, ...), custom_call_target="tpu_custom_call" | custom-call | flops 2415919104 | bytes 5898240 | tf_op jit(solution)/shard_map/rows/pallas_call | solution.py:398
  42.0 3.2 %collective-permute-done.41.refs_2_ = bf16[1,192,512]{2,1,0:T(8,128)(2,1)} collective-permute-done((bf16[1,192,512]{2,1,0:T(8,128)(2,1)}, bf16[1,192,512]{2,1,0:T(8,128)(2,1)}, u32[]{:S(2)}, u32[]{:S(2)}) %collective-permute-start.41) | collective-permute-done | bytes 196640 | tf_op jit(solution)/shard_map/ppermute | solution.py:437
  45.2 8.6 %rows.10 = (bf16[1,192,512]{2,1,0:T(8,128)(2,1)}, bf16[1,192,512]{2,1,0:T(8,128)(2,1)}, bf16[1,192,512]{2,1,0:T(8,128)(2,1)}, bf16[1,192,512]{2,1,0:T(8,128)(2,1...) custom-call(s32[8]{0:T(128)S(1)} %fusion.psf_of_ref, ...), custom_call_target="tpu_custom_call" | custom-call | flops 2415919104 | bytes 5898240 | tf_op jit(solution)/shard_map/rows/pallas_call | solution.py:398
  56.6 1.9 collective-permute-done.44.refs_5_
  61.3 14.2 %rows.9 = (bf16[2,192,512]{2,1,0:T(8,128)(2,1)}, bf16[2,192,512]{2,1,0:T(8,128)(2,1)}, bf16[2,192,512]{2,1,0:T(8,128)(2,1)}, bf16[2,192,512]{2,1,0:T(8,128)(2,1)...) custom-call(s32[8]{0:T(128)S(1)} %fusion.psf_of_ref, ...), custom_call_target="tpu_custom_call" | custom-call | flops 4831838208 | bytes 8650752 | tf_op jit(solution)/shard_map/rows/pallas_call | solution.py:398
  80.6 2.4 fusion.1
  82.9 18.1 %collective-permute-done.38.refs_6_ = bf16[1,192,512]{2,1,0:T(8,128)(2,1)S(1)} collective-permute-done((bf16[1,192,512]{2,1,0:T(8,128)(2,1)S(1)}, bf16[1,192,512]{2,1,0:T(8,128)(2,1)S(1)}, u32[]{:S(2)}, u32[]{:S(2)}) %collective-permute-start.38) | collective-permute-done | bytes 196640 | tf_op jit(solution)/shard_map/ppermute | solution.py:437
  101.1 2.5 %collective-permute-done.39.refs_7_ = bf16[1,192,512]{2,1,0:T(8,128)(2,1)S(1)} collective-permute-done((bf16[1,192,512]{2,1,0:T(8,128)(2,1)S(1)}, bf16[1,192,512]{2,1,0:T(8,128)(2,1)S(1)}, u32[]{:S(2)}, u32[]{:S(2)}) %collective-permute-start.39) | collective-permute-done | bytes 196640 | tf_op jit(solution)/shard_map/ppermute | solution.py:437
  108.0 14.2 %rows.8 = (bf16[2,192,512]{2,1,0:T(8,128)(2,1)}, bf16[2,192,512]{2,1,0:T(8,128)(2,1)}, bf16[2,192,512]{2,1,0:T(8,128)(2,1)}, bf16[2,192,512]{2,1,0:T(8,128)(2,1)...) custom-call(s32[8]{0:T(128)S(1)} %fusion.psf_of_ref, ...), custom_call_target="tpu_custom_call" | custom-call | flops 4831838208 | bytes 8650752 | tf_op jit(solution)/shard_map/rows/pallas_call | solution.py:398
  122.2 20.2 %collective-permute-done.29.refs_4_ = bf16[2,192,512]{2,1,0:T(8,128)(2,1)} collective-permute-done((bf16[2,192,512]{2,1,0:T(8,128)(2,1)}, bf16[2,192,512]{2,1,0:T(8,128)(2,1)}, u32[]{:S(2)}, u32[]{:S(2)}) %collective-permute-start.29) | collective-permute-done | bytes 393248 | tf_op jit(solution)/shard_map/ppermute | solution.py:437
  142.5 8.3 %collective-permute-done.30.refs_5_ = bf16[2,192,512]{2,1,0:T(8,128)(2,1)} collective-permute-done((bf16[2,192,512]{2,1,0:T(8,128)(2,1)}, bf16[2,192,512]{2,1,0:T(8,128)(2,1)}, u32[]{:S(2)}, u32[]{:S(2)}) %collective-permute-start.30) | collective-permute-done | bytes 393248 | tf_op jit(solution)/shard_map/ppermute | solution.py:437
  152.3 1.8 collective-permute-start.3
  155.3 7.8 %collective-permute-done.20.refs_2_ = bf16[2,192,512]{2,1,0:T(8,128)(2,1)} collective-permute-done((bf16[2,192,512]{2,1,0:T(8,128)(2,1)}, bf16[2,192,512]{2,1,0:T(8,128)(2,1)}, u32[]{:S(2)}, u32[]{:S(2)}) %collective-permute-start.20) | collective-permute-done | bytes 393248 | tf_op jit(solution)/shard_map/ppermute | solution.py:437
  163.2 7.2 %collective-permute-done.21.refs_3_ = bf16[2,192,512]{2,1,0:T(8,128)(2,1)} collective-permute-done((bf16[2,192,512]{2,1,0:T(8,128)(2,1)}, bf16[2,192,512]{2,1,0:T(8,128)(2,1)}, u32[]{:S(2)}, u32[]{:S(2)}) %collective-permute-start.21) | collective-permute-done | bytes 393248 | tf_op jit(solution)/shard_map/ppermute | solution.py:437
  171.8 2.8 %pixphases.3.refs_8_ = bf16[512,1536]{1,0:T(8,128)(2,1)} custom-call(), custom_call_target="tpu_custom_call" | custom-call | tf_op jit(solution)/shard_map/pixphases/pallas_call | solution.py:384
  174.6 1.9 pixphases.2.refs_8_
  176.5 2.1 collective-permute-start.25
  180.1 3.8 %pixels.6.refs_10_ = f32[8,1,512,512]{3,2,1,0:T(8,128)} custom-call(bf16[1,192,512]{2,1,0:T(8,128)(2,1)} %get-tuple-element.99.refs_0_, bf16[1,192,512]{2,1,0:T(8,128)(2,1)} %collective-permute-done.40.refs_1_, bf16[1,192,512]{2,1,0:T(8,128)(2,1)} %collective-permute-done.41.refs_2_, bf16[1,192,512]{2,1,0:T(8,128)(2,1)} %copy-done.8, ...), custom_call_target="tpu_custom_call" | custom-call | flops 805306368 | bytes 3670016 | tf_op jit(solution)/shard_map/pixels/pallas_call | solution.py:443
  183.8 3.8 %pixels.7.refs_10_ = f32[8,1,512,512]{3,2,1,0:T(8,128)} custom-call(bf16[1,192,512]{2,1,0:T(8,128)(2,1)} %get-tuple-element.91.refs_0_, bf16[1,192,512]{2,1,0:T(8,128)(2,1)} %copy-done.13, bf16[1,192,512]{2,1,0:T(8,128)(2,1)} %copy-done.14, bf16[1,192,512]{2,1,0:T(8,128)(2,1)} %copy-done.15, ...), custom_call_target="tpu_custom_call", output_to_operand_aliasing={{}: (10, {})} | custom-call | flops 805306368 | bytes 3670016 | tf_op jit(solution)/shard_map/pixels/pallas_call | solution.py:443
  187.7 8.1 %rows.7 = (bf16[1,104,512]{2,1,0:T(8,128)(2,1)}, bf16[1,104,512]{2,1,0:T(8,128)(2,1)}, bf16[1,104,512]{2,1,0:T(8,128)(2,1)}, bf16[1,104,512]{2,1,0:T(8,128)(2,1)...) custom-call(s32[8]{0:T(128)S(1)} %fusion.psf_of_ref, ...), custom_call_target="tpu_custom_call" | custom-call | flops 1610612736 | bytes 5177344 | tf_op jit(solution)/shard_map/rows/pallas_call | solution.py:398
  195.8 8.4 %collective-permute-done.23.refs_5_ = bf16[2,192,512]{2,1,0:T(8,128)(2,1)} collective-permute-done((bf16[2,192,512]{2,1,0:T(8,128)(2,1)}, bf16[2,192,512]{2,1,0:T(8,128)(2,1)}, u32[]{:S(2)}, u32[]{:S(2)}) %collective-permute-start.23) | collective-permute-done | bytes 393248 | tf_op jit(solution)/shard_map/ppermute | solution.py:437
  206.3 7.9 %rows.6 = (bf16[1,104,512]{2,1,0:T(8,128)(2,1)}, bf16[1,104,512]{2,1,0:T(8,128)(2,1)}, bf16[1,104,512]{2,1,0:T(8,128)(2,1)}, bf16[1,104,512]{2,1,0:T(8,128)(2,1)...) custom-call(s32[8]{0:T(128)S(1)} %fusion.psf_of_ref, ...), custom_call_target="tpu_custom_call" | custom-call | flops 1610612736 | bytes 5177344 | tf_op jit(solution)/shard_map/rows/pallas_call | solution.py:398
  217.8 1.9 collective-permute-start.10
  219.8 4.9 %pixels.8.refs_10_ = f32[8,1,512,512]{3,2,1,0:T(8,128)} custom-call(bf16[2,192,512]{2,1,0:T(8,128)(2,1)} %get-tuple-element.83.refs_0_, bf16[2,192,512]{2,1,0:T(8,128)(2,1)} %collective-permute-done.26.refs_1_, bf16[2,192,512]{2,1,0:T(8,128)(2,1)} %collective-permute-done.27.refs_2_, ...), custom_call_target="tpu_custom_call", output_to_operand_aliasing={{}: (10, {})} | custom-call | flops 1610612736 | bytes 7340032 | tf_op jit(solution)/shard_map/pixels/pallas_call | solution.py:443
  230.3 4.9 %pixels.9.refs_10_ = f32[8,1,512,512]{3,2,1,0:T(8,128)} custom-call(bf16[2,192,512]{2,1,0:T(8,128)(2,1)} %get-tuple-element.75.refs_0_, bf16[2,192,512]{2,1,0:T(8,128)(2,1)} %collective-permute-done.19.refs_1_, bf16[2,192,512]{2,1,0:T(8,128)(2,1)} %collective-permute-done.20.refs_2_, ...), custom_call_target="tpu_custom_call", output_to_operand_aliasing={{}: (10, {})} | custom-call | flops 1610612736 | bytes 7340032 | tf_op jit(solution)/shard_map/pixels/pallas_call | solution.py:443
  235.2 2.9 %pixels.10.refs_10_ = f32[8,1,512,512]{3,2,1,0:T(8,128)} custom-call(bf16[1,104,512]{2,1,0:T(8,128)(2,1)S(1)} %copy-done.5, bf16[1,104,512]{2,1,0:T(8,128)(2,1)S(1)} %collective-permute-done.12.refs_1_, bf16[1,104,512]{2,1,0:T(8,128)(2,1)S(1)} %collective-permute-done.13.refs_2_, ...), custom_call_target="tpu_custom_call", output_to_operand_aliasing={{}: (10, {})} | custom-call | flops 436207616 | bytes 2949120 | tf_op jit(solution)/shard_map/pixels/pallas_call | solution.py:443
  238.2 2.9 %pixels.11 = f32[8,1,512,512]{3,2,1,0:T(8,128)} custom-call(bf16[1,104,512]{2,1,0:T(8,128)(2,1)S(1)} %copy-done.6, bf16[1,104,512]{2,1,0:T(8,128)(2,1)S(1)} %collective-permute-done.4.refs_1_, bf16[1,104,512]{2,1,0:T(8,128)(2,1)S(1)} %collective-permute-done.5.refs_2_, ...), custom_call_target="tpu_custom_call", output_to_operand_aliasing={{}: (10, {})} | custom-call | flops 436207616 | bytes 2949120 | tf_op jit(solution)/shard_map/pixels/pallas_call | solution.py:443
  (143 shorter events, 42.5 us)
Async XLA Ops:
  1.6 12.9 %collective-permute-start = (f32[13,16,128]{2,1,0:T(8,128)}, f32[13,16,128]{2,1,0:T(8,128)}, u32[]{:S(2)}, u32[]{:S(2)}) collective-permute-start(f32[13,16,128]{2,1,0:T(8,128)} %moments.1.refs_0_), channel_id=1, source_target_pairs={{0,1},{1,0},{2,3},{3,2},{4,5},{5,4},{6,7},{7,6},{8,9},{9,8},{10,11... | collective-permute-start | bytes 319496 | tf_op jit(solution)/shard_map/ppermute | solution.py:371
  38.3 15.4 %collective-permute-start.42 = (bf16[1,192,512]{2,1,0:T(8,128)(2,1)}, bf16[1,192,512]{2,1,0:T(8,128)(2,1)S(1)}, u32[]{:S(2)}, u32[]{:S(2)}) collective-permute-start(bf16[1,192,512]{2,1,0:T(8,128)(2,1)} %get-tuple-element.102), channel_id=1, source_target_pairs={{0,12},{4,8},{8,4},{12,0},{16,28},{20,24},{24,20},{28,16},{1,13},{... | collective-permute-start | bytes 589832 | tf_op jit(solution)/shard_map/ppermute | solution.py:437
  38.6 16.8 %collective-permute-start.43 = (bf16[1,192,512]{2,1,0:T(8,128)(2,1)}, bf16[1,192,512]{2,1,0:T(8,128)(2,1)S(1)}, u32[]{:S(2)}, u32[]{:S(2)}) collective-permute-start(bf16[1,192,512]{2,1,0:T(8,128)(2,1)} %get-tuple-element.103), channel_id=1, source_target_pairs={{0,16},{4,20},{8,24},{12,28},{16,0},{20,4},{24,8},{28,12},{1,17},{... | collective-permute-start | bytes 589832 | tf_op jit(solution)/shard_map/ppermute | solution.py:437
  39.8 18.7 %collective-permute-start.44 = (bf16[1,192,512]{2,1,0:T(8,128)(2,1)}, bf16[1,192,512]{2,1,0:T(8,128)(2,1)S(1)}, u32[]{:S(2)}, u32[]{:S(2)}) collective-permute-start(bf16[1,192,512]{2,1,0:T(8,128)(2,1)} %get-tuple-element.104), channel_id=1, source_target_pairs={{0,20},{4,16},{8,28},{12,24},{16,4},{20,0},{24,12},{28,8},{1,21},{... | collective-permute-start | bytes 589832 | tf_op jit(solution)/shard_map/ppermute | solution.py:437
  40.6 19.0 %collective-permute-start.45 = (bf16[1,192,512]{2,1,0:T(8,128)(2,1)}, bf16[1,192,512]{2,1,0:T(8,128)(2,1)S(1)}, u32[]{:S(2)}, u32[]{:S(2)}) collective-permute-start(bf16[1,192,512]{2,1,0:T(8,128)(2,1)} %get-tuple-element.105), channel_id=1, source_target_pairs={{0,24},{4,28},{8,16},{12,20},{16,8},{20,12},{24,0},{28,4},{1,25},{... | collective-permute-start | bytes 589832 | tf_op jit(solution)/shard_map/ppermute | solution.py:437
  45.2 15.1 %collective-permute-start.46 = (bf16[1,192,512]{2,1,0:T(8,128)(2,1)}, bf16[1,192,512]{2,1,0:T(8,128)(2,1)S(1)}, u32[]{:S(2)}, u32[]{:S(2)}) collective-permute-start(bf16[1,192,512]{2,1,0:T(8,128)(2,1)} %get-tuple-element.106), channel_id=1, source_target_pairs={{0,28},{4,24},{8,20},{12,16},{16,12},{20,8},{24,4},{28,0},{1,29},{... | collective-permute-start | bytes 589832 | tf_op jit(solution)/shard_map/ppermute | solution.py:437
  53.7 21.8 %collective-permute-start.33 = (bf16[1,192,512]{2,1,0:T(8,128)(2,1)}, bf16[1,192,512]{2,1,0:T(8,128)(2,1)S(1)}, u32[]{:S(2)}, u32[]{:S(2)}) collective-permute-start(bf16[1,192,512]{2,1,0:T(8,128)(2,1)} %get-tuple-element.92), channel_id=1, source_target_pairs={{0,4},{4,0},{8,12},{12,8},{16,20},{20,16},{24,28},{28,24},{1,5},{5... | collective-permute-start | bytes 589832 | tf_op jit(solution)/shard_map/ppermute | solution.py:437
  55.3 20.7 %collective-permute-start.34 = (bf16[1,192,512]{2,1,0:T(8,128)(2,1)}, bf16[1,192,512]{2,1,0:T(8,128)(2,1)S(1)}, u32[]{:S(2)}, u32[]{:S(2)}) collective-permute-start(bf16[1,192,512]{2,1,0:T(8,128)(2,1)} %get-tuple-element.93), channel_id=1, source_target_pairs={{0,8},{4,12},{8,0},{12,4},{16,24},{20,28},{24,16},{28,20},{1,9},{5... | collective-permute-start | bytes 589832 | tf_op jit(solution)/shard_map/ppermute | solution.py:437
  58.5 18.3 %collective-permute-start.35 = (bf16[1,192,512]{2,1,0:T(8,128)(2,1)}, bf16[1,192,512]{2,1,0:T(8,128)(2,1)S(1)}, u32[]{:S(2)}, u32[]{:S(2)}) collective-permute-start(bf16[1,192,512]{2,1,0:T(8,128)(2,1)} %get-tuple-element.94), channel_id=1, source_target_pairs={{0,12},{4,8},{8,4},{12,0},{16,28},{20,24},{24,20},{28,16},{1,13},{... | collective-permute-start | bytes 589832 | tf_op jit(solution)/shard_map/ppermute | solution.py:437
  59.5 18.0 %collective-permute-start.36 = (bf16[1,192,512]{2,1,0:T(8,128)(2,1)}, bf16[1,192,512]{2,1,0:T(8,128)(2,1)S(1)}, u32[]{:S(2)}, u32[]{:S(2)}) collective-permute-start(bf16[1,192,512]{2,1,0:T(8,128)(2,1)} %get-tuple-element.95), channel_id=1, source_target_pairs={{0,16},{4,20},{8,24},{12,28},{16,0},{20,4},{24,8},{28,12},{1,17},{... | collective-permute-start | bytes 589832 | tf_op jit(solution)/shard_map/ppermute | solution.py:437
  60.3 18.7 %collective-permute-start.37 = (bf16[1,192,512]{2,1,0:T(8,128)(2,1)}, bf16[1,192,512]{2,1,0:T(8,128)(2,1)S(1)}, u32[]{:S(2)}, u32[]{:S(2)}) collective-permute-start(bf16[1,192,512]{2,1,0:T(8,128)(2,1)} %get-tuple-element.96), channel_id=1, source_target_pairs={{0,20},{4,16},{8,28},{12,24},{16,4},{20,0},{24,12},{28,8},{1,21},{... | collective-permute-start | bytes 589832 | tf_op jit(solution)/shard_map/ppermute | solution.py:437
  75.5 29.3 %collective-permute-start.26 = (bf16[2,192,512]{2,1,0:T(8,128)(2,1)}, bf16[2,192,512]{2,1,0:T(8,128)(2,1)}, u32[]{:S(2)}, u32[]{:S(2)}) collective-permute-start(bf16[2,192,512]{2,1,0:T(8,128)(2,1)} %get-tuple-element.84), channel_id=1, source_target_pairs={{0,4},{4,0},{8,12},{12,8},{16,20},{20,16},{24,28},{28,24},{1,5},{5... | collective-permute-start | bytes 1179656 | tf_op jit(solution)/shard_map/ppermute | solution.py:437
  76.1 29.5 %collective-permute-start.27 = (bf16[2,192,512]{2,1,0:T(8,128)(2,1)}, bf16[2,192,512]{2,1,0:T(8,128)(2,1)}, u32[]{:S(2)}, u32[]{:S(2)}) collective-permute-start(bf16[2,192,512]{2,1,0:T(8,128)(2,1)} %get-tuple-element.85), channel_id=1, source_target_pairs={{0,8},{4,12},{8,0},{12,4},{16,24},{20,28},{24,16},{28,20},{1,9},{5... | collective-permute-start | bytes 1179656 | tf_op jit(solution)/shard_map/ppermute | solution.py:437
  76.9 30.3 %collective-permute-start.28 = (bf16[2,192,512]{2,1,0:T(8,128)(2,1)}, bf16[2,192,512]{2,1,0:T(8,128)(2,1)}, u32[]{:S(2)}, u32[]{:S(2)}) collective-permute-start(bf16[2,192,512]{2,1,0:T(8,128)(2,1)} %get-tuple-element.86), channel_id=1, source_target_pairs={{0,12},{4,8},{8,4},{12,0},{16,28},{20,24},{24,20},{28,16},{1,13},{... | collective-permute-start | bytes 1179656 | tf_op jit(solution)/shard_map/ppermute | solution.py:437
  77.5 23.6 %collective-permute-start.38 = (bf16[1,192,512]{2,1,0:T(8,128)(2,1)S(1)}, bf16[1,192,512]{2,1,0:T(8,128)(2,1)S(1)}, u32[]{:S(2)}, u32[]{:S(2)}) collective-permute-start(bf16[1,192,512]{2,1,0:T(8,128)(2,1)S(1)} %copy-done.21), channel_id=1, source_target_pairs={{0,24},{4,28},{8,16},{12,20},{16,8},{20,12},{24,0},{28,4},{1,25},{... | collective-permute-start | bytes 589832 | tf_op jit(solution)/shard_map/ppermute | solution.py:437
  79.0 24.5 %collective-permute-start.39 = (bf16[1,192,512]{2,1,0:T(8,128)(2,1)S(1)}, bf16[1,192,512]{2,1,0:T(8,128)(2,1)S(1)}, u32[]{:S(2)}, u32[]{:S(2)}) collective-permute-start(bf16[1,192,512]{2,1,0:T(8,128)(2,1)S(1)} %copy-done.20), channel_id=1, source_target_pairs={{0,28},{4,24},{8,20},{12,16},{16,12},{20,8},{24,4},{28,0},{1,29},{... | collective-permute-start | bytes 589832 | tf_op jit(solution)/shard_map/ppermute | solution.py:437
  101.1 75.5 %collective-permute-start.11 = (bf16[4,1,2,48,768]{4,3,2,1,0:T(8,128)(2,1)}, bf16[4,1,2,48,768]{4,3,2,1,0:T(8,128)(2,1)}, u32[]{:S(2)}, u32[]{:S(2)}) collective-permute-start(bf16[4,1,2,48,768]{4,3,2,1,0:T(8,128)(2,1)} %get-tuple-element.107), channel_id=1, source_target_pairs={{0,28},{4,24},{8,20},{12,16},{16,12},{20,8},{24,4},{28,0},{1,29},{... | collective-permute-start | bytes 1769480 | tf_op jit(solution)/shard_map/ppermute | solution.py:331
  103.5 38.9 %collective-permute-start.29 = (bf16[2,192,512]{2,1,0:T(8,128)(2,1)}, bf16[2,192,512]{2,1,0:T(8,128)(2,1)}, u32[]{:S(2)}, u32[]{:S(2)}) collective-permute-start(bf16[2,192,512]{2,1,0:T(8,128)(2,1)} %get-tuple-element.87), channel_id=1, source_target_pairs={{0,16},{4,20},{8,24},{12,28},{16,0},{20,4},{24,8},{28,12},{1,17},{... | collective-permute-start | bytes 1179656 | tf_op jit(solution)/shard_map/ppermute | solution.py:437
  104.8 46.0 %collective-permute-start.30 = (bf16[2,192,512]{2,1,0:T(8,128)(2,1)}, bf16[2,192,512]{2,1,0:T(8,128)(2,1)}, u32[]{:S(2)}, u32[]{:S(2)}) collective-permute-start(bf16[2,192,512]{2,1,0:T(8,128)(2,1)} %get-tuple-element.88), channel_id=1, source_target_pairs={{0,20},{4,16},{8,28},{12,24},{16,4},{20,0},{24,12},{28,8},{1,21},{... | collective-permute-start | bytes 1179656 | tf_op jit(solution)/shard_map/ppermute | solution.py:437
  105.6 46.5 %collective-permute-start.31 = (bf16[2,192,512]{2,1,0:T(8,128)(2,1)}, bf16[2,192,512]{2,1,0:T(8,128)(2,1)}, u32[]{:S(2)}, u32[]{:S(2)}) collective-permute-start(bf16[2,192,512]{2,1,0:T(8,128)(2,1)} %get-tuple-element.89), channel_id=1, source_target_pairs={{0,24},{4,28},{8,16},{12,20},{16,8},{20,12},{24,0},{28,4},{1,25},{... | collective-permute-start | bytes 1179656 | tf_op jit(solution)/shard_map/ppermute | solution.py:437
  107.1 45.2 %collective-permute-start.32 = (bf16[2,192,512]{2,1,0:T(8,128)(2,1)}, bf16[2,192,512]{2,1,0:T(8,128)(2,1)}, u32[]{:S(2)}, u32[]{:S(2)}) collective-permute-start(bf16[2,192,512]{2,1,0:T(8,128)(2,1)} %get-tuple-element.90), channel_id=1, source_target_pairs={{0,28},{4,24},{8,20},{12,16},{16,12},{20,8},{24,4},{28,0},{1,29},{... | collective-permute-start | bytes 1179656 | tf_op jit(solution)/shard_map/ppermute | solution.py:437
  152.1 18.2 %collective-permute-start.21 = (bf16[2,192,512]{2,1,0:T(8,128)(2,1)}, bf16[2,192,512]{2,1,0:T(8,128)(2,1)}, u32[]{:S(2)}, u32[]{:S(2)}) collective-permute-start(bf16[2,192,512]{2,1,0:T(8,128)(2,1)} %get-tuple-element.78), channel_id=1, source_target_pairs={{0,12},{4,8},{8,4},{12,0},{16,28},{20,24},{24,20},{28,16},{1,13},{... | collective-permute-start | bytes 1179656 | tf_op jit(solution)/shard_map/ppermute | solution.py:437
  152.3 53.2 %collective-permute-start.3 = (bf16[4,1,2,48,768]{4,3,2,1,0:T(8,128)(2,1)}, bf16[4,1,2,48,768]{4,3,2,1,0:T(8,128)(2,1)}, u32[]{:S(2)}, u32[]{:S(2)}) collective-permute-start(bf16[4,1,2,48,768]{4,3,2,1,0:T(8,128)(2,1)} %get-tuple-element.108), channel_id=1, source_target_pairs={{0,28},{4,24},{8,20},{12,16},{16,12},{20,8},{24,4},{28,0},{1,29},{... | collective-permute-start | bytes 1769480 | tf_op jit(solution)/shard_map/ppermute | solution.py:331
  154.1 41.6 %collective-permute-start.22 = (bf16[2,192,512]{2,1,0:T(8,128)(2,1)}, bf16[2,192,512]{2,1,0:T(8,128)(2,1)}, u32[]{:S(2)}, u32[]{:S(2)}) collective-permute-start(bf16[2,192,512]{2,1,0:T(8,128)(2,1)} %get-tuple-element.79), channel_id=1, source_target_pairs={{0,16},{4,20},{8,24},{12,28},{16,0},{20,4},{24,8},{28,12},{1,17},{... | collective-permute-start | bytes 1179656 | tf_op jit(solution)/shard_map/ppermute | solution.py:437
  163.2 41.0 %collective-permute-start.23 = (bf16[2,192,512]{2,1,0:T(8,128)(2,1)}, bf16[2,192,512]{2,1,0:T(8,128)(2,1)}, u32[]{:S(2)}, u32[]{:S(2)}) collective-permute-start(bf16[2,192,512]{2,1,0:T(8,128)(2,1)} %get-tuple-element.80), channel_id=1, source_target_pairs={{0,20},{4,16},{8,28},{12,24},{16,4},{20,0},{24,12},{28,8},{1,21},{... | collective-permute-start | bytes 1179656 | tf_op jit(solution)/shard_map/ppermute | solution.py:437
  170.4 34.6 %collective-permute-start.24 = (bf16[2,192,512]{2,1,0:T(8,128)(2,1)}, bf16[2,192,512]{2,1,0:T(8,128)(2,1)}, u32[]{:S(2)}, u32[]{:S(2)}) collective-permute-start(bf16[2,192,512]{2,1,0:T(8,128)(2,1)} %get-tuple-element.81), channel_id=1, source_target_pairs={{0,24},{4,28},{8,16},{12,20},{16,8},{20,12},{24,0},{28,4},{1,25},{... | collective-permute-start | bytes 1179656 | tf_op jit(solution)/shard_map/ppermute | solution.py:437
  176.5 37.6 %collective-permute-start.25 = (bf16[2,192,512]{2,1,0:T(8,128)(2,1)}, bf16[2,192,512]{2,1,0:T(8,128)(2,1)S(1)}, u32[]{:S(2)}, u32[]{:S(2)}) collective-permute-start(bf16[2,192,512]{2,1,0:T(8,128)(2,1)} %get-tuple-element.82), channel_id=1, source_target_pairs={{0,28},{4,24},{8,20},{12,16},{16,12},{20,8},{24,4},{28,0},{1,29},{... | collective-permute-start | bytes 1179656 | tf_op jit(solution)/shard_map/ppermute | solution.py:437
  195.8 19.9 %collective-permute-start.12 = (bf16[1,104,512]{2,1,0:T(8,128)(2,1)}, bf16[1,104,512]{2,1,0:T(8,128)(2,1)S(1)}, u32[]{:S(2)}, u32[]{:S(2)}) collective-permute-start(bf16[1,104,512]{2,1,0:T(8,128)(2,1)} %get-tuple-element.68), channel_id=1, source_target_pairs={{0,4},{4,0},{8,12},{12,8},{16,20},{20,16},{24,28},{28,24},{1,5},{5... | collective-permute-start | bytes 319496 | tf_op jit(solution)/shard_map/ppermute | solution.py:437
  204.2 12.9 %collective-permute-start.13 = (bf16[1,104,512]{2,1,0:T(8,128)(2,1)}, bf16[1,104,512]{2,1,0:T(8,128)(2,1)S(1)}, u32[]{:S(2)}, u32[]{:S(2)}) collective-permute-start(bf16[1,104,512]{2,1,0:T(8,128)(2,1)} %get-tuple-element.69), channel_id=1, source_target_pairs={{0,8},{4,12},{8,0},{12,4},{16,24},{20,28},{24,16},{28,20},{1,9},{5... | collective-permute-start | bytes 319496 | tf_op jit(solution)/shard_map/ppermute | solution.py:437
  205.0 12.8 %collective-permute-start.14 = (bf16[1,104,512]{2,1,0:T(8,128)(2,1)}, bf16[1,104,512]{2,1,0:T(8,128)(2,1)S(1)}, u32[]{:S(2)}, u32[]{:S(2)}) collective-permute-start(bf16[1,104,512]{2,1,0:T(8,128)(2,1)} %get-tuple-element.70), channel_id=1, source_target_pairs={{0,12},{4,8},{8,4},{12,0},{16,28},{20,24},{24,20},{28,16},{1,13},{... | collective-permute-start | bytes 319496 | tf_op jit(solution)/shard_map/ppermute | solution.py:437
  205.5 14.3 %collective-permute-start.15 = (bf16[1,104,512]{2,1,0:T(8,128)(2,1)}, bf16[1,104,512]{2,1,0:T(8,128)(2,1)S(1)}, u32[]{:S(2)}, u32[]{:S(2)}) collective-permute-start(bf16[1,104,512]{2,1,0:T(8,128)(2,1)} %get-tuple-element.71), channel_id=1, source_target_pairs={{0,16},{4,20},{8,24},{12,28},{16,0},{20,4},{24,8},{28,12},{1,17},{... | collective-permute-start | bytes 319496 | tf_op jit(solution)/shard_map/ppermute | solution.py:437
  225.1 13.0 %collective-permute-start.5 = (bf16[1,104,512]{2,1,0:T(8,128)(2,1)S(1)}, bf16[1,104,512]{2,1,0:T(8,128)(2,1)S(1)}, u32[]{:S(2)}, u32[]{:S(2)}) collective-permute-start(bf16[1,104,512]{2,1,0:T(8,128)(2,1)S(1)} %copy-done.26), channel_id=1, source_target_pairs={{0,8},{4,12},{8,0},{12,4},{16,24},{20,28},{24,16},{28,20},{1,9},{5... | collective-permute-start | bytes 319496 | tf_op jit(solution)/shard_map/ppermute | solution.py:437
  (45 other events, 770.7 us)

commit v6 on v4

--- a/solution.py
+++ b/solution.py
@@ -10,7 +10,7 @@
 
 FCOLS = 4
 VMEM_LIMIT = 20 * 1024 * 1024
-SMALL_LIMIT = 12 * 1024 * 1024
+SMALL_LIMIT = 10 * 1024 * 1024
 
 bf16, f32, i32 = jnp.bfloat16, jnp.float32, jnp.int32
 
@@ -319,8 +319,9 @@
         out_shape=jax.ShapeDtypeStruct((3 * ntile + 1, rows, ts), f32),
         in_specs=[SMEM, VMEM],
         out_specs=VMEM,
+        compiler_params=pltpu.CompilerParams(vmem_limit_bytes=SMALL_LIMIT),
         name="moments",
-    )(chan_weight, components)
+    )(in_hbm(chan_weight), in_hbm(components))
     row_table, inv_table, flip = pl.pallas_call(
         functools.partial(row_phases_kernel, frame, fs),
         out_shape=[
@@ -358,6 +359,7 @@
         out_shape=jax.ShapeDtypeStruct((3 * ntile + 1, rows, ts), bf16),
         in_specs=[SMEM, VMEM, VMEM],
         out_specs=VMEM,
+        compiler_params=pltpu.CompilerParams(vmem_limit_bytes=SMALL_LIMIT),
         name="solve",
     )(facet_psf, sums, other)
     fit = lax.all_gather(fit, "facet", axis=0)
@@ -372,6 +374,7 @@
             out_shape=jax.ShapeDtypeStruct((fs, nf * (block_pair if paired else 2 * kb)), bf16),
             out_specs=VMEM,
             scratch_shapes=[pltpu.VMEM((64, nf * (block_pair if paired else 2 * kb)), f32)] * 2,
+            compiler_params=pltpu.CompilerParams(vmem_limit_bytes=VMEM_LIMIT),
             name="pixphases",
         )()
 
@@ -415,13 +418,13 @@
             ),
             compiler_params=pltpu.CompilerParams(vmem_limit_bytes=VMEM_LIMIT),
             name="rows",
-        )(psf_of, fit, row_table, col_table, in_hbm(inv_table), in_hbm(flip), psf_spectra, *([in_hbm(far[chan0])] if paired else []))
+        )(psf_of, fit, row_table, col_table, in_hbm(inv_table), in_hbm(flip), psf_spectra, *([far[chan0]] if paired else []))
         got = list(w)
         for j in send_order(nf):
             got[j] = lax.ppermute(w[j], "facet", [(s, s ^ j) for s in range(nf)])
         pieces.append((chan0, count, block, tables[paired], got))
     result = None
-    for n, (chan0, count, block, pix_table, got) in enumerate(pieces):
+    for chan0, count, block, pix_table, got in pieces:
         image = pl.BlockSpec((1, 1, fs, fs), lambda c, c0=chan0: (c0 + c, 0, 0, 0))
         before = [] if result is None else [result]
         result = pl.pallas_call(
@@ -442,7 +445,7 @@
             ),
             compiler_params=pltpu.CompilerParams(vmem_limit_bytes=VMEM_LIMIT),
             name="pixels",
-        )(*(got if n >= len(pieces) - 2 else map(in_hbm, got)), pix_table, residual, *before)
+        )(*got, pix_table, residual, *before)
     return result
 
 

time: 226 us -> 222 us (0.982)
  Pallas kernels: 98.7 us -> 91.5 us
  waiting for transfers between devices: 57.9 us -> 64.9 us
  local copies, waits for them, and re-layouts: 4.21 us -> 1.39 us
    ppermute x42, waiting for transfers between devices: 54.7 us -> 61.9 us  [shards(): got[j] = lax.ppermute(w[j], 'facet', [(s, s ^ j) for s in range(nf)])]
    unnamed x66 -> x36, local copies, waits for them, and re-layouts: 2.88 us -> 0.07 us
    pallas_call x6, Pallas kernels: 23.2 us -> 20.7 us  [shards(): pl.pallas_call(functools.partial(pixels_kernel, nf, 1.0 / (frame * frame)...]
  transfers between devices with their start and end apart: 46 -> 46, of which waited for: 8 -> 9; matrix products, arithmetic and copies ran while one was open for 1% -> 1% of each run, Pallas kernels for 37% -> 36%
where the time goes in v6:
time: 222 us; the launch traced here: 221 us
  Pallas kernels  91.5 us (41%)
  waiting for transfers between devices  64.9 us (29%)
  starting transfers between devices  52.8 us (24%)
  blocking collectives  9.72 us (4%)
    ppermute x42, waiting for transfers between devices, shards(): got[j] = lax.ppermute(w[j], 'facet', [(s, s ^ j) for s in range(nf)])  61.9 us
    pallas_call x6, Pallas kernels, shards(): pl.pallas_call(functools.partial(rows_kernel, total, nch, chan0, paired),...  60.5 us
    ppermute x42, starting transfers between devices, shards(): got[j] = lax.ppermute(w[j], 'facet', [(s, s ^ j) for s in range(nf)])  44.2 us
    pallas_call x6, Pallas kernels, shards(): pl.pallas_call(functools.partial(pixels_kernel, nf, 1.0 / (frame * frame)...  20.7 us
    all_gather x1, blocking collectives, shards(): fit = lax.all_gather(fit, 'facet', axis=0)  9.72 us
    ppermute x2, starting transfers between devices, shards(): other = lax.ppermute(sums, 'freq', [(s, s ^ 1 << i) for s in range(nz)])  5.93 us
  transfers between devices with their start and end apart: 46, of which 9 were waited for; matrix products, arithmetic and copies ran while one was open for 1% of the time, Pallas kernels for 36%

profile of v6, /device:TPU:0, one launch (start us, length us, event | category | flops | bytes accessed | tf_op | source)
XLA Modules:
  0.0 221.4 jit_solution(7496082271253625933)
XLA Ops:
  1.0 3.1 %collective-permute-start = (f32[13,16,128]{2,1,0:T(8,128)S(1)}, f32[13,16,128]{2,1,0:T(8,128)S(1)}, u32[]{:S(2)}, u32[]{:S(2)}) collective-permute-start(f32[13,16,128]{2,1,0:T(8,128)S(1)} %moments.1), channel_id=1, source_target_pairs={{0,1},{1,0},{2,3},{3,2},{4,5},{5,4},{6,7},{7,6},{8,9},{9,8},{10,11... | collective-permute-start | bytes 319496 | tf_op jit(solution)/shard_map/ppermute | solution.py:356
  4.1 3.0 %collective-permute-done = f32[13,16,128]{2,1,0:T(8,128)S(1)} collective-permute-done((f32[13,16,128]{2,1,0:T(8,128)S(1)}, f32[13,16,128]{2,1,0:T(8,128)S(1)}, u32[]{:S(2)}, u32[]{:S(2)}) %collective-permute-start) | collective-permute-done | bytes 106528 | tf_op jit(solution)/shard_map/ppermute | solution.py:356
  7.1 2.8 %collective-permute-start.1 = (f32[13,16,128]{2,1,0:T(8,128)S(1)}, f32[13,16,128]{2,1,0:T(8,128)S(1)}, u32[]{:S(2)}, u32[]{:S(2)}) collective-permute-start(f32[13,16,128]{2,1,0:T(8,128)S(1)} %add.3.one_ref), channel_id=1, source_target_pairs={{0,2},{1,3},{2,0},{3,1},{4,6},{5,7},{6,4},{7,5},{8,10},{9,11},{10,... | collective-permute-start | bytes 319496 | tf_op jit(solution)/shard_map/ppermute | solution.py:356
  9.9 3.8 %rowphases.1 = (bf16[2,4,192,128]{3,2,1,0:T(8,128)(2,1)S(1)}, bf16[768,512]{1,0:T(8,128)(2,1)}, bf16[384,384]{1,0:T(8,128)(2,1)}) custom-call(s32[2,4]{1,0:T(2,128)} %bitcast.16), custom_call_target="tpu_custom_call" | custom-call | tf_op jit(solution)/shard_map/rowphases/pallas_call | solution.py:325
  13.7 2.8 %colphases.1 = bf16[16,128,768]{2,1,0:T(8,128)(2,1)S(1)} custom-call(s32[2,4]{1,0:T(2,128)} %bitcast.17), custom_call_target="tpu_custom_call" | custom-call | tf_op jit(solution)/shard_map/colphases/pallas_call | solution.py:342
  17.2 9.7 %all-gather = bf16[104,16,128]{2,1,0:T(8,128)(2,1)S(1)} all-gather(bf16[13,16,128]{2,1,0:T(8,128)(2,1)S(1)} %solve.1), channel_id=2, replica_groups=mesh['facet'=8,'freq'=4] {'facet'}, dimensions={0}, use_global_device_ids=true | all-gather | bytes 479232 | tf_op jit(solution)/shard_map/all_gather | solution.py:365
  27.2 8.5 %rows.11 = (bf16[1,192,512]{2,1,0:T(8,128)(2,1)}, bf16[1,192,512]{2,1,0:T(8,128)(2,1)}, bf16[1,192,512]{2,1,0:T(8,128)(2,1)}, bf16[1,192,512]{2,1,0:T(8,128)(2,1...) custom-call(s32[8]{0:T(128)S(1)} %fusion.psf_of_ref, ...), custom_call_target="tpu_custom_call" | custom-call | flops 2415919104 | bytes 5898240 | tf_op jit(solution)/shard_map/rows/pallas_call | solution.py:385
  36.1 1.5 collective-permute-start.40
  37.6 1.5 collective-permute-start.42
  41.0 8.5 %rows.10 = (bf16[1,192,512]{2,1,0:T(8,128)(2,1)}, bf16[1,192,512]{2,1,0:T(8,128)(2,1)}, bf16[1,192,512]{2,1,0:T(8,128)(2,1)}, bf16[1,192,512]{2,1,0:T(8,128)(2,1...) custom-call(s32[8]{0:T(128)S(1)} %fusion.psf_of_ref, ...), custom_call_target="tpu_custom_call" | custom-call | flops 2415919104 | bytes 5898240 | tf_op jit(solution)/shard_map/rows/pallas_call | solution.py:385
  51.2 1.5 collective-permute-start.33
  53.3 5.8 %collective-permute-start.34 = (bf16[1,192,512]{2,1,0:T(8,128)(2,1)}, bf16[1,192,512]{2,1,0:T(8,128)(2,1)S(1)}, u32[]{:S(2)}, u32[]{:S(2)}) collective-permute-start(bf16[1,192,512]{2,1,0:T(8,128)(2,1)} %get-tuple-element.94), channel_id=1, source_target_pairs={{0,12},{4,8},{8,4},{12,0},{16,28},{20,24},{24,20},{28,16},{1,13},{... | collective-permute-start | bytes 589832 | tf_op jit(solution)/shard_map/ppermute | solution.py:424
  61.7 2.0 collective-permute-start.2
  63.8 2.4 %collective-permute-done.34.refs_3_ = bf16[1,192,512]{2,1,0:T(8,128)(2,1)S(1)} collective-permute-done((bf16[1,192,512]{2,1,0:T(8,128)(2,1)}, bf16[1,192,512]{2,1,0:T(8,128)(2,1)S(1)}, u32[]{:S(2)}, u32[]{:S(2)}) %collective-permute-start.34) | collective-permute-done | bytes 196640 | tf_op jit(solution)/shard_map/ppermute | solution.py:424
  68.7 14.0 %rows.9 = (bf16[2,192,512]{2,1,0:T(8,128)(2,1)}, bf16[2,192,512]{2,1,0:T(8,128)(2,1)}, bf16[2,192,512]{2,1,0:T(8,128)(2,1)}, bf16[2,192,512]{2,1,0:T(8,128)(2,1)...) custom-call(s32[8]{0:T(128)S(1)} %fusion.psf_of_ref, ...), custom_call_target="tpu_custom_call" | custom-call | flops 4831838208 | bytes 8650752 | tf_op jit(solution)/shard_map/rows/pallas_call | solution.py:385
  82.7 21.4 %collective-permute-done.36.refs_5_ = bf16[1,192,512]{2,1,0:T(8,128)(2,1)S(1)} collective-permute-done((bf16[1,192,512]{2,1,0:T(8,128)(2,1)}, bf16[1,192,512]{2,1,0:T(8,128)(2,1)S(1)}, u32[]{:S(2)}, u32[]{:S(2)}) %collective-permute-start.36) | collective-permute-done | bytes 196640 | tf_op jit(solution)/shard_map/ppermute | solution.py:424
  107.5 14.0 %rows.8 = (bf16[2,192,512]{2,1,0:T(8,128)(2,1)}, bf16[2,192,512]{2,1,0:T(8,128)(2,1)}, bf16[2,192,512]{2,1,0:T(8,128)(2,1)}, bf16[2,192,512]{2,1,0:T(8,128)(2,1)...) custom-call(s32[8]{0:T(128)S(1)} %fusion.psf_of_ref, ...), custom_call_target="tpu_custom_call" | custom-call | flops 4831838208 | bytes 8650752 | tf_op jit(solution)/shard_map/rows/pallas_call | solution.py:385
  126.2 23.4 %collective-permute-done.29.refs_5_ = bf16[2,192,512]{2,1,0:T(8,128)(2,1)S(1)} collective-permute-done((bf16[2,192,512]{2,1,0:T(8,128)(2,1)S(1)}, bf16[2,192,512]{2,1,0:T(8,128)(2,1)S(1)}, u32[]{:S(2)}, u32[]{:S(2)}) %collective-permute-start.29) | collective-permute-done | bytes 393248 | tf_op jit(solution)/shard_map/ppermute | solution.py:424
  153.1 1.6 pixphases.3.refs_8_
  155.7 1.5 collective-permute-start.24
  157.3 3.2 %pixels.6.refs_10_ = f32[8,1,512,512]{3,2,1,0:T(8,128)} custom-call(bf16[1,192,512]{2,1,0:T(8,128)(2,1)S(1)} %copy-done.2, bf16[1,192,512]{2,1,0:T(8,128)(2,1)S(1)} %collective-permute-done.39.refs_1_, bf16[1,192,512]{2,1,0:T(8,128)(2,1)S(1)} %collective-permute-done.40.refs_2_, bf16[1,192,512]{2,1,0:T(8,128)(2,1)S(1)} %collective-permute-done.41.refs_3_, ...), custom_call_target="tpu_custom_call" | custom-call | flops 805306368 | bytes 3670016 | tf_op jit(solution)/shard_map/pixels/pallas_call | solution.py:430
  160.5 3.2 %pixels.7.refs_10_ = f32[8,1,512,512]{3,2,1,0:T(8,128)} custom-call(bf16[1,192,512]{2,1,0:T(8,128)(2,1)S(1)} %copy-done.3, bf16[1,192,512]{2,1,0:T(8,128)(2,1)S(1)} %collective-permute-done.32.refs_1_, bf16[1,192,512]{2,1,0:T(8,128)(2,1)S(1)} %collective-permute-done.33.refs_2_, ...), custom_call_target="tpu_custom_call", output_to_operand_aliasing={{}: (10, {})} | custom-call | flops 805306368 | bytes 3670016 | tf_op jit(solution)/shard_map/pixels/pallas_call | solution.py:430
  163.7 7.8 %rows.7 = (bf16[1,104,512]{2,1,0:T(8,128)(2,1)}, bf16[1,104,512]{2,1,0:T(8,128)(2,1)}, bf16[1,104,512]{2,1,0:T(8,128)(2,1)}, bf16[1,104,512]{2,1,0:T(8,128)(2,1)...) custom-call(s32[8]{0:T(128)S(1)} %fusion.psf_of_ref, ...), custom_call_target="tpu_custom_call" | custom-call | flops 1610612736 | bytes 5177344 | tf_op jit(solution)/shard_map/rows/pallas_call | solution.py:385
  171.7 7.6 %collective-permute-done.21.refs_4_ = bf16[2,192,512]{2,1,0:T(8,128)(2,1)S(1)} collective-permute-done((bf16[2,192,512]{2,1,0:T(8,128)(2,1)}, bf16[2,192,512]{2,1,0:T(8,128)(2,1)S(1)}, u32[]{:S(2)}, u32[]{:S(2)}) %collective-permute-start.21) | collective-permute-done | bytes 393248 | tf_op jit(solution)/shard_map/ppermute | solution.py:424
  180.6 5.3 %collective-permute-done.22.refs_5_ = bf16[2,192,512]{2,1,0:T(8,128)(2,1)S(1)} collective-permute-done((bf16[2,192,512]{2,1,0:T(8,128)(2,1)}, bf16[2,192,512]{2,1,0:T(8,128)(2,1)S(1)}, u32[]{:S(2)}, u32[]{:S(2)}) %collective-permute-start.22) | collective-permute-done | bytes 393248 | tf_op jit(solution)/shard_map/ppermute | solution.py:424
  185.9 1.8 collective-permute-start.13
  188.2 7.6 %rows.6 = (bf16[1,104,512]{2,1,0:T(8,128)(2,1)}, bf16[1,104,512]{2,1,0:T(8,128)(2,1)}, bf16[1,104,512]{2,1,0:T(8,128)(2,1)}, bf16[1,104,512]{2,1,0:T(8,128)(2,1)...) custom-call(s32[8]{0:T(128)S(1)} %fusion.psf_of_ref, ...), custom_call_target="tpu_custom_call" | custom-call | flops 1610612736 | bytes 5177344 | tf_op jit(solution)/shard_map/rows/pallas_call | solution.py:385
  198.1 1.6 collective-permute-start.17
  200.6 4.3 %pixels.8.refs_10_ = f32[8,1,512,512]{3,2,1,0:T(8,128)} custom-call(bf16[2,192,512]{2,1,0:T(8,128)(2,1)S(1)} %copy-done.1, bf16[2,192,512]{2,1,0:T(8,128)(2,1)S(1)} %collective-permute-done.25.refs_1_, bf16[2,192,512]{2,1,0:T(8,128)(2,1)S(1)} %collective-permute-done.26.refs_2_, ...), custom_call_target="tpu_custom_call", output_to_operand_aliasing={{}: (10, {})} | custom-call | flops 1610612736 | bytes 7340032 | tf_op jit(solution)/shard_map/pixels/pallas_call | solution.py:430
  211.1 4.2 %pixels.9.refs_10_ = f32[8,1,512,512]{3,2,1,0:T(8,128)} custom-call(bf16[2,192,512]{2,1,0:T(8,128)(2,1)S(1)} %copy-done, bf16[2,192,512]{2,1,0:T(8,128)(2,1)S(1)} %collective-permute-done.18.refs_1_, bf16[2,192,512]{2,1,0:T(8,128)(2,1)S(1)} %collective-permute-done.19.refs_2_, ...), custom_call_target="tpu_custom_call", output_to_operand_aliasing={{}: (10, {})} | custom-call | flops 1610612736 | bytes 7340032 | tf_op jit(solution)/shard_map/pixels/pallas_call | solution.py:430
  215.3 2.9 %pixels.10.refs_10_ = f32[8,1,512,512]{3,2,1,0:T(8,128)} custom-call(bf16[1,104,512]{2,1,0:T(8,128)(2,1)S(1)} %copy-done.4, bf16[1,104,512]{2,1,0:T(8,128)(2,1)S(1)} %collective-permute-done.11.refs_1_, bf16[1,104,512]{2,1,0:T(8,128)(2,1)S(1)} %collective-permute-done.12.refs_2_, ...), custom_call_target="tpu_custom_call", output_to_operand_aliasing={{}: (10, {})} | custom-call | flops 436207616 | bytes 2949120 | tf_op jit(solution)/shard_map/pixels/pallas_call | solution.py:430
  218.5 2.9 %pixels.11 = f32[8,1,512,512]{3,2,1,0:T(8,128)} custom-call(bf16[1,104,512]{2,1,0:T(8,128)(2,1)S(1)} %copy-done.5, bf16[1,104,512]{2,1,0:T(8,128)(2,1)S(1)} %collective-permute-done.3.refs_1_, bf16[1,104,512]{2,1,0:T(8,128)(2,1)S(1)} %collective-permute-done.4.refs_2_, ...), custom_call_target="tpu_custom_call", output_to_operand_aliasing={{}: (10, {})} | custom-call | flops 436207616 | bytes 2949120 | tf_op jit(solution)/shard_map/pixels/pallas_call | solution.py:430
  (118 shorter events, 35.3 us)
Async XLA Ops:
  36.1 13.5 %collective-permute-start.40 = (bf16[1,192,512]{2,1,0:T(8,128)(2,1)}, bf16[1,192,512]{2,1,0:T(8,128)(2,1)S(1)}, u32[]{:S(2)}, u32[]{:S(2)}) collective-permute-start(bf16[1,192,512]{2,1,0:T(8,128)(2,1)} %get-tuple-element.101), channel_id=1, source_target_pairs={{0,8},{4,12},{8,0},{12,4},{16,24},{20,28},{24,16},{28,20},{1,9},{5... | collective-permute-start | bytes 589832 | tf_op jit(solution)/shard_map/ppermute | solution.py:424
  37.6 13.0 %collective-permute-start.41 = (bf16[1,192,512]{2,1,0:T(8,128)(2,1)}, bf16[1,192,512]{2,1,0:T(8,128)(2,1)S(1)}, u32[]{:S(2)}, u32[]{:S(2)}) collective-permute-start(bf16[1,192,512]{2,1,0:T(8,128)(2,1)} %get-tuple-element.102), channel_id=1, source_target_pairs={{0,12},{4,8},{8,4},{12,0},{16,28},{20,24},{24,20},{28,16},{1,13},{... | collective-permute-start | bytes 589832 | tf_op jit(solution)/shard_map/ppermute | solution.py:424
  37.6 13.6 %collective-permute-start.42 = (bf16[1,192,512]{2,1,0:T(8,128)(2,1)}, bf16[1,192,512]{2,1,0:T(8,128)(2,1)S(1)}, u32[]{:S(2)}, u32[]{:S(2)}) collective-permute-start(bf16[1,192,512]{2,1,0:T(8,128)(2,1)} %get-tuple-element.103), channel_id=1, source_target_pairs={{0,16},{4,20},{8,24},{12,28},{16,0},{20,4},{24,8},{28,12},{1,17},{... | collective-permute-start | bytes 589832 | tf_op jit(solution)/shard_map/ppermute | solution.py:424
  39.1 14.3 %collective-permute-start.43 = (bf16[1,192,512]{2,1,0:T(8,128)(2,1)}, bf16[1,192,512]{2,1,0:T(8,128)(2,1)S(1)}, u32[]{:S(2)}, u32[]{:S(2)}) collective-permute-start(bf16[1,192,512]{2,1,0:T(8,128)(2,1)} %get-tuple-element.104), channel_id=1, source_target_pairs={{0,20},{4,16},{8,28},{12,24},{16,4},{20,0},{24,12},{28,8},{1,21},{... | collective-permute-start | bytes 589832 | tf_op jit(solution)/shard_map/ppermute | solution.py:424
  39.6 19.5 %collective-permute-start.44 = (bf16[1,192,512]{2,1,0:T(8,128)(2,1)}, bf16[1,192,512]{2,1,0:T(8,128)(2,1)S(1)}, u32[]{:S(2)}, u32[]{:S(2)}) collective-permute-start(bf16[1,192,512]{2,1,0:T(8,128)(2,1)} %get-tuple-element.105), channel_id=1, source_target_pairs={{0,24},{4,28},{8,16},{12,20},{16,8},{20,12},{24,0},{28,4},{1,25},{... | collective-permute-start | bytes 589832 | tf_op jit(solution)/shard_map/ppermute | solution.py:424
  51.2 12.5 %collective-permute-start.33 = (bf16[1,192,512]{2,1,0:T(8,128)(2,1)}, bf16[1,192,512]{2,1,0:T(8,128)(2,1)S(1)}, u32[]{:S(2)}, u32[]{:S(2)}) collective-permute-start(bf16[1,192,512]{2,1,0:T(8,128)(2,1)} %get-tuple-element.93), channel_id=1, source_target_pairs={{0,8},{4,12},{8,0},{12,4},{16,24},{20,28},{24,16},{28,20},{1,9},{5... | collective-permute-start | bytes 589832 | tf_op jit(solution)/shard_map/ppermute | solution.py:424
  53.3 12.8 %collective-permute-start.34 = (bf16[1,192,512]{2,1,0:T(8,128)(2,1)}, bf16[1,192,512]{2,1,0:T(8,128)(2,1)S(1)}, u32[]{:S(2)}, u32[]{:S(2)}) collective-permute-start(bf16[1,192,512]{2,1,0:T(8,128)(2,1)} %get-tuple-element.94), channel_id=1, source_target_pairs={{0,12},{4,8},{8,4},{12,0},{16,28},{20,24},{24,20},{28,16},{1,13},{... | collective-permute-start | bytes 589832 | tf_op jit(solution)/shard_map/ppermute | solution.py:424
  61.0 45.0 %collective-permute-start.10 = (bf16[4,1,2,48,768]{4,3,2,1,0:T(8,128)(2,1)S(1)}, bf16[4,1,2,48,768]{4,3,2,1,0:T(8,128)(2,1)S(1)}, u32[]{:S(2)}, u32[]{:S(2)}) collective-permute-start(bf16[4,1,2,48,768]{4,3,2,1,0:T(8,128)(2,1)S(1)} %get-tuple-element.107), channel_id=1, source_target_pairs={{0,28},{4,24},{8,20},{12,16},{16,12},{20,8},{24,4},{28,0},{1,29},{... | collective-permute-start | bytes 1769480 | tf_op jit(solution)/shard_map/ppermute | solution.py:316
  61.7 59.8 %collective-permute-start.2 = (bf16[4,1,2,48,768]{4,3,2,1,0:T(8,128)(2,1)S(1)}, bf16[4,1,2,48,768]{4,3,2,1,0:T(8,128)(2,1)S(1)}, u32[]{:S(2)}, u32[]{:S(2)}) collective-permute-start(bf16[4,1,2,48,768]{4,3,2,1,0:T(8,128)(2,1)S(1)} %get-tuple-element.108), channel_id=1, source_target_pairs={{0,28},{4,24},{8,20},{12,16},{16,12},{20,8},{24,4},{28,0},{1,29},{... | collective-permute-start | bytes 1769480 | tf_op jit(solution)/shard_map/ppermute | solution.py:316
  63.7 40.4 %collective-permute-start.36 = (bf16[1,192,512]{2,1,0:T(8,128)(2,1)}, bf16[1,192,512]{2,1,0:T(8,128)(2,1)S(1)}, u32[]{:S(2)}, u32[]{:S(2)}) collective-permute-start(bf16[1,192,512]{2,1,0:T(8,128)(2,1)} %get-tuple-element.96), channel_id=1, source_target_pairs={{0,20},{4,16},{8,28},{12,24},{16,4},{20,0},{24,12},{28,8},{1,21},{... | collective-permute-start | bytes 589832 | tf_op jit(solution)/shard_map/ppermute | solution.py:424
  66.2 38.1 %collective-permute-start.37 = (bf16[1,192,512]{2,1,0:T(8,128)(2,1)}, bf16[1,192,512]{2,1,0:T(8,128)(2,1)S(1)}, u32[]{:S(2)}, u32[]{:S(2)}) collective-permute-start(bf16[1,192,512]{2,1,0:T(8,128)(2,1)} %get-tuple-element.97), channel_id=1, source_target_pairs={{0,24},{4,28},{8,16},{12,20},{16,8},{20,12},{24,0},{28,4},{1,25},{... | collective-permute-start | bytes 589832 | tf_op jit(solution)/shard_map/ppermute | solution.py:424
  67.6 37.9 %collective-permute-start.38 = (bf16[1,192,512]{2,1,0:T(8,128)(2,1)}, bf16[1,192,512]{2,1,0:T(8,128)(2,1)S(1)}, u32[]{:S(2)}, u32[]{:S(2)}) collective-permute-start(bf16[1,192,512]{2,1,0:T(8,128)(2,1)} %get-tuple-element.98), channel_id=1, source_target_pairs={{0,28},{4,24},{8,20},{12,16},{16,12},{20,8},{24,4},{28,0},{1,29},{... | collective-permute-start | bytes 589832 | tf_op jit(solution)/shard_map/ppermute | solution.py:424
  104.1 17.8 %collective-permute-start.25 = (bf16[2,192,512]{2,1,0:T(8,128)(2,1)}, bf16[2,192,512]{2,1,0:T(8,128)(2,1)S(1)}, u32[]{:S(2)}, u32[]{:S(2)}) collective-permute-start(bf16[2,192,512]{2,1,0:T(8,128)(2,1)} %get-tuple-element.84), channel_id=1, source_target_pairs={{0,4},{4,0},{8,12},{12,8},{16,20},{20,16},{24,28},{28,24},{1,5},{5... | collective-permute-start | bytes 1179656 | tf_op jit(solution)/shard_map/ppermute | solution.py:424
  104.2 19.2 %collective-permute-start.26 = (bf16[2,192,512]{2,1,0:T(8,128)(2,1)}, bf16[2,192,512]{2,1,0:T(8,128)(2,1)S(1)}, u32[]{:S(2)}, u32[]{:S(2)}) collective-permute-start(bf16[2,192,512]{2,1,0:T(8,128)(2,1)} %get-tuple-element.85), channel_id=1, source_target_pairs={{0,8},{4,12},{8,0},{12,4},{16,24},{20,28},{24,16},{28,20},{1,9},{5... | collective-permute-start | bytes 1179656 | tf_op jit(solution)/shard_map/ppermute | solution.py:424
  105.5 19.1 %collective-permute-start.27 = (bf16[2,192,512]{2,1,0:T(8,128)(2,1)}, bf16[2,192,512]{2,1,0:T(8,128)(2,1)S(1)}, u32[]{:S(2)}, u32[]{:S(2)}) collective-permute-start(bf16[2,192,512]{2,1,0:T(8,128)(2,1)} %get-tuple-element.86), channel_id=1, source_target_pairs={{0,12},{4,8},{8,4},{12,0},{16,28},{20,24},{24,20},{28,16},{1,13},{... | collective-permute-start | bytes 1179656 | tf_op jit(solution)/shard_map/ppermute | solution.py:424
  106.0 19.0 %collective-permute-start.28 = (bf16[2,192,512]{2,1,0:T(8,128)(2,1)}, bf16[2,192,512]{2,1,0:T(8,128)(2,1)S(1)}, u32[]{:S(2)}, u32[]{:S(2)}) collective-permute-start(bf16[2,192,512]{2,1,0:T(8,128)(2,1)} %get-tuple-element.87), channel_id=1, source_target_pairs={{0,16},{4,20},{8,24},{12,28},{16,0},{20,4},{24,8},{28,12},{1,17},{... | collective-permute-start | bytes 1179656 | tf_op jit(solution)/shard_map/ppermute | solution.py:424
  121.5 28.1 %collective-permute-start.29 = (bf16[2,192,512]{2,1,0:T(8,128)(2,1)S(1)}, bf16[2,192,512]{2,1,0:T(8,128)(2,1)S(1)}, u32[]{:S(2)}, u32[]{:S(2)}) collective-permute-start(bf16[2,192,512]{2,1,0:T(8,128)(2,1)S(1)} %copy-done.8), channel_id=1, source_target_pairs={{0,20},{4,16},{8,28},{12,24},{16,4},{20,0},{24,12},{28,8},{1,21},{... | collective-permute-start | bytes 1179656 | tf_op jit(solution)/shard_map/ppermute | solution.py:424
  121.9 28.3 %collective-permute-start.30 = (bf16[2,192,512]{2,1,0:T(8,128)(2,1)S(1)}, bf16[2,192,512]{2,1,0:T(8,128)(2,1)S(1)}, u32[]{:S(2)}, u32[]{:S(2)}) collective-permute-start(bf16[2,192,512]{2,1,0:T(8,128)(2,1)S(1)} %copy-done.7), channel_id=1, source_target_pairs={{0,24},{4,28},{8,16},{12,20},{16,8},{20,12},{24,0},{28,4},{1,25},{... | collective-permute-start | bytes 1179656 | tf_op jit(solution)/shard_map/ppermute | solution.py:424
  123.4 28.2 %collective-permute-start.31 = (bf16[2,192,512]{2,1,0:T(8,128)(2,1)S(1)}, bf16[2,192,512]{2,1,0:T(8,128)(2,1)S(1)}, u32[]{:S(2)}, u32[]{:S(2)}) collective-permute-start(bf16[2,192,512]{2,1,0:T(8,128)(2,1)S(1)} %copy-done.6), channel_id=1, source_target_pairs={{0,28},{4,24},{8,20},{12,16},{16,12},{20,8},{24,4},{28,0},{1,29},{... | collective-permute-start | bytes 1179656 | tf_op jit(solution)/shard_map/ppermute | solution.py:424
  124.6 27.1 %collective-permute-start.18 = (bf16[2,192,512]{2,1,0:T(8,128)(2,1)}, bf16[2,192,512]{2,1,0:T(8,128)(2,1)S(1)}, u32[]{:S(2)}, u32[]{:S(2)}) collective-permute-start(bf16[2,192,512]{2,1,0:T(8,128)(2,1)} %get-tuple-element.76), channel_id=1, source_target_pairs={{0,4},{4,0},{8,12},{12,8},{16,20},{20,16},{24,28},{28,24},{1,5},{5... | collective-permute-start | bytes 1179656 | tf_op jit(solution)/shard_map/ppermute | solution.py:424
  125.0 30.8 %collective-permute-start.19 = (bf16[2,192,512]{2,1,0:T(8,128)(2,1)}, bf16[2,192,512]{2,1,0:T(8,128)(2,1)S(1)}, u32[]{:S(2)}, u32[]{:S(2)}) collective-permute-start(bf16[2,192,512]{2,1,0:T(8,128)(2,1)} %get-tuple-element.77), channel_id=1, source_target_pairs={{0,8},{4,12},{8,0},{12,4},{16,24},{20,28},{24,16},{28,20},{1,9},{5... | collective-permute-start | bytes 1179656 | tf_op jit(solution)/shard_map/ppermute | solution.py:424
  149.6 21.9 %collective-permute-start.20 = (bf16[2,192,512]{2,1,0:T(8,128)(2,1)}, bf16[2,192,512]{2,1,0:T(8,128)(2,1)S(1)}, u32[]{:S(2)}, u32[]{:S(2)}) collective-permute-start(bf16[2,192,512]{2,1,0:T(8,128)(2,1)} %get-tuple-element.78), channel_id=1, source_target_pairs={{0,12},{4,8},{8,4},{12,0},{16,28},{20,24},{24,20},{28,16},{1,13},{... | collective-permute-start | bytes 1179656 | tf_op jit(solution)/shard_map/ppermute | solution.py:424
  150.2 29.1 %collective-permute-start.21 = (bf16[2,192,512]{2,1,0:T(8,128)(2,1)}, bf16[2,192,512]{2,1,0:T(8,128)(2,1)S(1)}, u32[]{:S(2)}, u32[]{:S(2)}) collective-permute-start(bf16[2,192,512]{2,1,0:T(8,128)(2,1)} %get-tuple-element.79), channel_id=1, source_target_pairs={{0,16},{4,20},{8,24},{12,28},{16,0},{20,4},{24,8},{28,12},{1,17},{... | collective-permute-start | bytes 1179656 | tf_op jit(solution)/shard_map/ppermute | solution.py:424
  151.6 34.3 %collective-permute-start.22 = (bf16[2,192,512]{2,1,0:T(8,128)(2,1)}, bf16[2,192,512]{2,1,0:T(8,128)(2,1)S(1)}, u32[]{:S(2)}, u32[]{:S(2)}) collective-permute-start(bf16[2,192,512]{2,1,0:T(8,128)(2,1)} %get-tuple-element.80), channel_id=1, source_target_pairs={{0,20},{4,16},{8,28},{12,24},{16,4},{20,0},{24,12},{28,8},{1,21},{... | collective-permute-start | bytes 1179656 | tf_op jit(solution)/shard_map/ppermute | solution.py:424
  151.6 36.1 %collective-permute-start.23 = (bf16[2,192,512]{2,1,0:T(8,128)(2,1)}, bf16[2,192,512]{2,1,0:T(8,128)(2,1)S(1)}, u32[]{:S(2)}, u32[]{:S(2)}) collective-permute-start(bf16[2,192,512]{2,1,0:T(8,128)(2,1)} %get-tuple-element.81), channel_id=1, source_target_pairs={{0,24},{4,28},{8,16},{12,20},{16,8},{20,12},{24,0},{28,4},{1,25},{... | collective-permute-start | bytes 1179656 | tf_op jit(solution)/shard_map/ppermute | solution.py:424
  155.7 40.1 %collective-permute-start.24 = (bf16[2,192,512]{2,1,0:T(8,128)(2,1)}, bf16[2,192,512]{2,1,0:T(8,128)(2,1)S(1)}, u32[]{:S(2)}, u32[]{:S(2)}) collective-permute-start(bf16[2,192,512]{2,1,0:T(8,128)(2,1)} %get-tuple-element.82), channel_id=1, source_target_pairs={{0,28},{4,24},{8,20},{12,16},{16,12},{20,8},{24,4},{28,0},{1,29},{... | collective-permute-start | bytes 1179656 | tf_op jit(solution)/shard_map/ppermute | solution.py:424
  171.5 25.2 %collective-permute-start.11 = (bf16[1,104,512]{2,1,0:T(8,128)(2,1)}, bf16[1,104,512]{2,1,0:T(8,128)(2,1)S(1)}, u32[]{:S(2)}, u32[]{:S(2)}) collective-permute-start(bf16[1,104,512]{2,1,0:T(8,128)(2,1)} %get-tuple-element.68), channel_id=1, source_target_pairs={{0,4},{4,0},{8,12},{12,8},{16,20},{20,16},{24,28},{28,24},{1,5},{5... | collective-permute-start | bytes 319496 | tf_op jit(solution)/shard_map/ppermute | solution.py:424
  179.2 18.9 %collective-permute-start.12 = (bf16[1,104,512]{2,1,0:T(8,128)(2,1)}, bf16[1,104,512]{2,1,0:T(8,128)(2,1)S(1)}, u32[]{:S(2)}, u32[]{:S(2)}) collective-permute-start(bf16[1,104,512]{2,1,0:T(8,128)(2,1)} %get-tuple-element.69), channel_id=1, source_target_pairs={{0,8},{4,12},{8,0},{12,4},{16,24},{20,28},{24,16},{28,20},{1,9},{5... | collective-permute-start | bytes 319496 | tf_op jit(solution)/shard_map/ppermute | solution.py:424
  185.9 13.9 %collective-permute-start.13 = (bf16[1,104,512]{2,1,0:T(8,128)(2,1)}, bf16[1,104,512]{2,1,0:T(8,128)(2,1)S(1)}, u32[]{:S(2)}, u32[]{:S(2)}) collective-permute-start(bf16[1,104,512]{2,1,0:T(8,128)(2,1)} %get-tuple-element.70), channel_id=1, source_target_pairs={{0,12},{4,8},{8,4},{12,0},{16,28},{20,24},{24,20},{28,16},{1,13},{... | collective-permute-start | bytes 319496 | tf_op jit(solution)/shard_map/ppermute | solution.py:424
  187.7 12.1 %collective-permute-start.14 = (bf16[1,104,512]{2,1,0:T(8,128)(2,1)}, bf16[1,104,512]{2,1,0:T(8,128)(2,1)S(1)}, u32[]{:S(2)}, u32[]{:S(2)}) collective-permute-start(bf16[1,104,512]{2,1,0:T(8,128)(2,1)} %get-tuple-element.71), channel_id=1, source_target_pairs={{0,16},{4,20},{8,24},{12,28},{16,0},{20,4},{24,8},{28,12},{1,17},{... | collective-permute-start | bytes 319496 | tf_op jit(solution)/shard_map/ppermute | solution.py:424
  205.8 12.5 %collective-permute-start.5 = (bf16[1,104,512]{2,1,0:T(8,128)(2,1)S(1)}, bf16[1,104,512]{2,1,0:T(8,128)(2,1)S(1)}, u32[]{:S(2)}, u32[]{:S(2)}) collective-permute-start(bf16[1,104,512]{2,1,0:T(8,128)(2,1)S(1)} %copy-done.14), channel_id=1, source_target_pairs={{0,12},{4,8},{8,4},{12,0},{16,28},{20,24},{24,20},{28,16},{1,13},{... | collective-permute-start | bytes 319496 | tf_op jit(solution)/shard_map/ppermute | solution.py:424
  206.6 11.6 %collective-permute-start.6 = (bf16[1,104,512]{2,1,0:T(8,128)(2,1)S(1)}, bf16[1,104,512]{2,1,0:T(8,128)(2,1)S(1)}, u32[]{:S(2)}, u32[]{:S(2)}) collective-permute-start(bf16[1,104,512]{2,1,0:T(8,128)(2,1)S(1)} %copy-done.13), channel_id=1, source_target_pairs={{0,16},{4,20},{8,24},{12,28},{16,0},{20,4},{24,8},{28,12},{1,17},{... | collective-permute-start | bytes 319496 | tf_op jit(solution)/shard_map/ppermute | solution.py:424
  (32 other events, 404.8 us)

commit v7 on v6

--- a/solution.py
+++ b/solution.py
@@ -81,7 +81,22 @@
     return lax.broadcasted_iota(i32, shape, axis)
 
 
-def row_phases_kernel(frame, fs, pos_ref, row_ref, inv_ref, flip_ref):
+def inverse_phases_kernel(frame, fs, inv_ref):
+    half, quarter, pad = frame // 2, frame // 4, (frame - fs) // 2
+    place = (pad + lane((1, fs), 1)).astype(f32)
+    block = half // 4
+
+    def inverse(i, carry):
+        spot = i * block + lane((block, 1), 0)
+        freq = jnp.where(spot > half, spot - half, spot).astype(f32)
+        shift = jnp.where(spot > half, -quarter, 0).astype(f32)
+        inv_ref[pl.ds(i * block, block)] = cos_turn(freq * place + shift, frame).astype(bf16)
+        return carry
+
+    lax.fori_loop(0, 8, inverse, 0)
+
+
+def row_phases_kernel(frame, fs, pos_ref, row_ref, flip_ref):
     na, ntile, two_kb, ts = row_ref.shape
     kb = two_kb // 2
     half, quarter, pad = frame // 2, frame // 4, (frame - fs) // 2
@@ -96,17 +111,6 @@
             index = own * (oy + pixel).astype(f32)
             row_ref[a, t, :kb] = (cos_turn(index, frame) * ok).astype(bf16)
             row_ref[a, t, kb:] = (cos_turn(index + quarter, frame) * ok).astype(bf16)
-    place = (pad + lane((1, fs), 1)).astype(f32)
-    block = half // 4
-
-    def inverse(i, carry):
-        spot = i * block + lane((block, 1), 0)
-        freq = jnp.where(spot > half, spot - half, spot).astype(f32)
-        shift = jnp.where(spot > half, -quarter, 0).astype(f32)
-        inv_ref[pl.ds(i * block, block)] = cos_turn(freq * place + shift, frame).astype(bf16)
-        return carry
-
-    lax.fori_loop(0, 8, inverse, 0)
     source = lax.rem(half - lane((1, half), 1), half)
     flip_ref[...] = jnp.where(lane((half, half), 0) == source, 1.0, 0.0).astype(bf16)
 
@@ -322,23 +326,29 @@
         compiler_params=pltpu.CompilerParams(vmem_limit_bytes=SMALL_LIMIT),
         name="moments",
     )(in_hbm(chan_weight), in_hbm(components))
-    row_table, inv_table, flip = pl.pallas_call(
+    row_table, flip = pl.pallas_call(
         functools.partial(row_phases_kernel, frame, fs),
         out_shape=[
             jax.ShapeDtypeStruct((na, ntile, 2 * kb, ts), bf16),
-            pltpu.HBM((frame, fs), bf16),
             pltpu.HBM((half, half), bf16),
         ],
         grid=(1,),
         in_specs=[SMEM],
         out_specs=[
             VMEM,
-            pl.BlockSpec((frame, fs), lambda i: (0, 0)),
             pl.BlockSpec((half, half), lambda i: (0, 0)),
         ],
         compiler_params=pltpu.CompilerParams(vmem_limit_bytes=SMALL_LIMIT),
         name="rowphases",
     )(in_hbm(tile_pos.T))
+    inv_table = pl.pallas_call(
+        functools.partial(inverse_phases_kernel, frame, fs),
+        out_shape=pltpu.HBM((frame, fs), bf16),
+        grid=(1,),
+        out_specs=pl.BlockSpec((frame, fs), lambda i: (0, 0)),
+        compiler_params=pltpu.CompilerParams(vmem_limit_bytes=SMALL_LIMIT),
+        name="invphases",
+    )()
     col_table = pl.pallas_call(
         functools.partial(column_phases_kernel, frame, fs),
         out_shape=jax.ShapeDtypeStruct((FCOLS * ntile, ts, frame), bf16),

time: 222 us -> 222 us (level)
    pallas_call x1, Pallas kernels: 3.8 us -> 1.46 us  [shards(): pl.pallas_call(functools.partial(row_phases_kernel, frame, fs), out_shape...]
    pallas_call x0 -> x1, Pallas kernels: none -> 2.34 us  [shards(): pl.pallas_call(functools.partial(inverse_phases_kernel, frame, fs), out_s...]
where the time goes in v7:
time: 222 us; the launch traced here: 221 us
  Pallas kernels  91.5 us (41%)
  waiting for transfers between devices  65 us (29%)
  starting transfers between devices  52.8 us (24%)
  blocking collectives  9.72 us (4%)
    ppermute x42, waiting for transfers between devices, shards(): got[j] = lax.ppermute(w[j], 'facet', [(s, s ^ j) for s in range(nf)])  62 us
    pallas_call x6, Pallas kernels, shards(): pl.pallas_call(functools.partial(rows_kernel, total, nch, chan0, paired),...  60.5 us
    ppermute x42, starting transfers between devices, shards(): got[j] = lax.ppermute(w[j], 'facet', [(s, s ^ j) for s in range(nf)])  44.1 us
    pallas_call x6, Pallas kernels, shards(): pl.pallas_call(functools.partial(pixels_kernel, nf, 1.0 / (frame * frame)...  20.7 us
    all_gather x1, blocking collectives, shards(): fit = lax.all_gather(fit, 'facet', axis=0)  9.72 us
    ppermute x2, starting transfers between devices, shards(): other = lax.ppermute(sums, 'freq', [(s, s ^ 1 << i) for s in range(nz)])  5.93 us
  transfers between devices with their start and end apart: 46, of which 9 were waited for; matrix products, arithmetic and copies ran while one was open for 1% of the time, Pallas kernels for 36%

profile of v7, /device:TPU:0, one launch (start us, length us, event | category | flops | bytes accessed | tf_op | source)
XLA Modules:
  0.0 221.5 jit_solution(3371688690463743586)
XLA Ops:
  1.0 3.1 %collective-permute-start = (f32[13,16,128]{2,1,0:T(8,128)S(1)}, f32[13,16,128]{2,1,0:T(8,128)S(1)}, u32[]{:S(2)}, u32[]{:S(2)}) collective-permute-start(f32[13,16,128]{2,1,0:T(8,128)S(1)} %moments.1), channel_id=1, source_target_pairs={{0,1},{1,0},{2,3},{3,2},{4,5},{5,4},{6,7},{7,6},{8,9},{9,8},{10,11... | collective-permute-start | bytes 319496 | tf_op jit(solution)/shard_map/ppermute | solution.py:366
  4.1 3.0 %collective-permute-done = f32[13,16,128]{2,1,0:T(8,128)S(1)} collective-permute-done((f32[13,16,128]{2,1,0:T(8,128)S(1)}, f32[13,16,128]{2,1,0:T(8,128)S(1)}, u32[]{:S(2)}, u32[]{:S(2)}) %collective-permute-start) | collective-permute-done | bytes 106528 | tf_op jit(solution)/shard_map/ppermute | solution.py:366
  7.1 2.8 %collective-permute-start.1 = (f32[13,16,128]{2,1,0:T(8,128)S(1)}, f32[13,16,128]{2,1,0:T(8,128)S(1)}, u32[]{:S(2)}, u32[]{:S(2)}) collective-permute-start(f32[13,16,128]{2,1,0:T(8,128)S(1)} %add.3.one_ref), channel_id=1, source_target_pairs={{0,2},{1,3},{2,0},{3,1},{4,6},{5,7},{6,4},{7,5},{8,10},{9,11},{10,... | collective-permute-start | bytes 319496 | tf_op jit(solution)/shard_map/ppermute | solution.py:366
  11.4 2.8 %colphases.1 = bf16[16,128,768]{2,1,0:T(8,128)(2,1)S(1)} custom-call(s32[2,4]{1,0:T(2,128)} %bitcast.17), custom_call_target="tpu_custom_call" | custom-call | tf_op jit(solution)/shard_map/colphases/pallas_call | solution.py:352
  14.2 2.3 %invphases.1.inv_ref = bf16[768,512]{1,0:T(8,128)(2,1)} custom-call(), custom_call_target="tpu_custom_call" | custom-call | tf_op jit(solution)/shard_map/invphases/pallas_call | solution.py:344
  17.3 9.7 %all-gather = bf16[104,16,128]{2,1,0:T(8,128)(2,1)S(1)} all-gather(bf16[13,16,128]{2,1,0:T(8,128)(2,1)S(1)} %solve.1), channel_id=2, replica_groups=mesh['facet'=8,'freq'=4] {'facet'}, dimensions={0}, use_global_device_ids=true | all-gather | bytes 479232 | tf_op jit(solution)/shard_map/all_gather | solution.py:375
  27.2 8.5 %rows.11 = (bf16[1,192,512]{2,1,0:T(8,128)(2,1)}, bf16[1,192,512]{2,1,0:T(8,128)(2,1)}, bf16[1,192,512]{2,1,0:T(8,128)(2,1)}, bf16[1,192,512]{2,1,0:T(8,128)(2,1...) custom-call(s32[8]{0:T(128)S(1)} %fusion.psf_of_ref, ...), custom_call_target="tpu_custom_call" | custom-call | flops 2415919104 | bytes 5898240 | tf_op jit(solution)/shard_map/rows/pallas_call | solution.py:395
  36.1 1.5 collective-permute-start.40
  37.6 1.5 collective-permute-start.42
  41.0 8.5 %rows.10 = (bf16[1,192,512]{2,1,0:T(8,128)(2,1)}, bf16[1,192,512]{2,1,0:T(8,128)(2,1)}, bf16[1,192,512]{2,1,0:T(8,128)(2,1)}, bf16[1,192,512]{2,1,0:T(8,128)(2,1...) custom-call(s32[8]{0:T(128)S(1)} %fusion.psf_of_ref, ...), custom_call_target="tpu_custom_call" | custom-call | flops 2415919104 | bytes 5898240 | tf_op jit(solution)/shard_map/rows/pallas_call | solution.py:395
  51.2 1.5 collective-permute-start.33
  53.4 5.7 %collective-permute-start.34 = (bf16[1,192,512]{2,1,0:T(8,128)(2,1)}, bf16[1,192,512]{2,1,0:T(8,128)(2,1)S(1)}, u32[]{:S(2)}, u32[]{:S(2)}) collective-permute-start(bf16[1,192,512]{2,1,0:T(8,128)(2,1)} %get-tuple-element.92), channel_id=1, source_target_pairs={{0,12},{4,8},{8,4},{12,0},{16,28},{20,24},{24,20},{28,16},{1,13},{... | collective-permute-start | bytes 589832 | tf_op jit(solution)/shard_map/ppermute | solution.py:434
  61.7 2.0 collective-permute-start.2
  63.8 2.4 %collective-permute-done.34.refs_3_ = bf16[1,192,512]{2,1,0:T(8,128)(2,1)S(1)} collective-permute-done((bf16[1,192,512]{2,1,0:T(8,128)(2,1)}, bf16[1,192,512]{2,1,0:T(8,128)(2,1)S(1)}, u32[]{:S(2)}, u32[]{:S(2)}) %collective-permute-start.34) | collective-permute-done | bytes 196640 | tf_op jit(solution)/shard_map/ppermute | solution.py:434
  68.7 14.0 %rows.9 = (bf16[2,192,512]{2,1,0:T(8,128)(2,1)}, bf16[2,192,512]{2,1,0:T(8,128)(2,1)}, bf16[2,192,512]{2,1,0:T(8,128)(2,1)}, bf16[2,192,512]{2,1,0:T(8,128)(2,1)...) custom-call(s32[8]{0:T(128)S(1)} %fusion.psf_of_ref, ...), custom_call_target="tpu_custom_call" | custom-call | flops 4831838208 | bytes 8650752 | tf_op jit(solution)/shard_map/rows/pallas_call | solution.py:395
  82.7 21.4 %collective-permute-done.36.refs_5_ = bf16[1,192,512]{2,1,0:T(8,128)(2,1)S(1)} collective-permute-done((bf16[1,192,512]{2,1,0:T(8,128)(2,1)}, bf16[1,192,512]{2,1,0:T(8,128)(2,1)S(1)}, u32[]{:S(2)}, u32[]{:S(2)}) %collective-permute-start.36) | collective-permute-done | bytes 196640 | tf_op jit(solution)/shard_map/ppermute | solution.py:434
  107.5 14.0 %rows.8 = (bf16[2,192,512]{2,1,0:T(8,128)(2,1)}, bf16[2,192,512]{2,1,0:T(8,128)(2,1)}, bf16[2,192,512]{2,1,0:T(8,128)(2,1)}, bf16[2,192,512]{2,1,0:T(8,128)(2,1)...) custom-call(s32[8]{0:T(128)S(1)} %fusion.psf_of_ref, ...), custom_call_target="tpu_custom_call" | custom-call | flops 4831838208 | bytes 8650752 | tf_op jit(solution)/shard_map/rows/pallas_call | solution.py:395
  126.2 23.4 %collective-permute-done.29.refs_5_ = bf16[2,192,512]{2,1,0:T(8,128)(2,1)S(1)} collective-permute-done((bf16[2,192,512]{2,1,0:T(8,128)(2,1)S(1)}, bf16[2,192,512]{2,1,0:T(8,128)(2,1)S(1)}, u32[]{:S(2)}, u32[]{:S(2)}) %collective-permute-start.29) | collective-permute-done | bytes 393248 | tf_op jit(solution)/shard_map/ppermute | solution.py:434
  153.1 1.6 pixphases.3.refs_8_
  155.7 1.5 collective-permute-start.24
  157.3 3.2 %pixels.6.refs_10_ = f32[8,1,512,512]{3,2,1,0:T(8,128)} custom-call(bf16[1,192,512]{2,1,0:T(8,128)(2,1)S(1)} %copy-done.2, bf16[1,192,512]{2,1,0:T(8,128)(2,1)S(1)} %collective-permute-done.39.refs_1_, bf16[1,192,512]{2,1,0:T(8,128)(2,1)S(1)} %collective-permute-done.40.refs_2_, bf16[1,192,512]{2,1,0:T(8,128)(2,1)S(1)} %collective-permute-done.41.refs_3_, ...), custom_call_target="tpu_custom_call" | custom-call | flops 805306368 | bytes 3670016 | tf_op jit(solution)/shard_map/pixels/pallas_call | solution.py:440
  160.5 3.2 %pixels.7.refs_10_ = f32[8,1,512,512]{3,2,1,0:T(8,128)} custom-call(bf16[1,192,512]{2,1,0:T(8,128)(2,1)S(1)} %copy-done.3, bf16[1,192,512]{2,1,0:T(8,128)(2,1)S(1)} %collective-permute-done.32.refs_1_, bf16[1,192,512]{2,1,0:T(8,128)(2,1)S(1)} %collective-permute-done.33.refs_2_, ...), custom_call_target="tpu_custom_call", output_to_operand_aliasing={{}: (10, {})} | custom-call | flops 805306368 | bytes 3670016 | tf_op jit(solution)/shard_map/pixels/pallas_call | solution.py:440
  163.7 7.8 %rows.7 = (bf16[1,104,512]{2,1,0:T(8,128)(2,1)}, bf16[1,104,512]{2,1,0:T(8,128)(2,1)}, bf16[1,104,512]{2,1,0:T(8,128)(2,1)}, bf16[1,104,512]{2,1,0:T(8,128)(2,1)...) custom-call(s32[8]{0:T(128)S(1)} %fusion.psf_of_ref, ...), custom_call_target="tpu_custom_call" | custom-call | flops 1610612736 | bytes 5177344 | tf_op jit(solution)/shard_map/rows/pallas_call | solution.py:395
  171.7 7.6 %collective-permute-done.21.refs_4_ = bf16[2,192,512]{2,1,0:T(8,128)(2,1)S(1)} collective-permute-done((bf16[2,192,512]{2,1,0:T(8,128)(2,1)}, bf16[2,192,512]{2,1,0:T(8,128)(2,1)S(1)}, u32[]{:S(2)}, u32[]{:S(2)}) %collective-permute-start.21) | collective-permute-done | bytes 393248 | tf_op jit(solution)/shard_map/ppermute | solution.py:434
  180.6 5.3 %collective-permute-done.22.refs_5_ = bf16[2,192,512]{2,1,0:T(8,128)(2,1)S(1)} collective-permute-done((bf16[2,192,512]{2,1,0:T(8,128)(2,1)}, bf16[2,192,512]{2,1,0:T(8,128)(2,1)S(1)}, u32[]{:S(2)}, u32[]{:S(2)}) %collective-permute-start.22) | collective-permute-done | bytes 393248 | tf_op jit(solution)/shard_map/ppermute | solution.py:434
  185.9 1.8 collective-permute-start.13
  188.3 7.6 %rows.6 = (bf16[1,104,512]{2,1,0:T(8,128)(2,1)}, bf16[1,104,512]{2,1,0:T(8,128)(2,1)}, bf16[1,104,512]{2,1,0:T(8,128)(2,1)}, bf16[1,104,512]{2,1,0:T(8,128)(2,1)...) custom-call(s32[8]{0:T(128)S(1)} %fusion.psf_of_ref, ...), custom_call_target="tpu_custom_call" | custom-call | flops 1610612736 | bytes 5177344 | tf_op jit(solution)/shard_map/rows/pallas_call | solution.py:395
  198.2 1.6 collective-permute-start.17
  200.6 4.3 %pixels.8.refs_10_ = f32[8,1,512,512]{3,2,1,0:T(8,128)} custom-call(bf16[2,192,512]{2,1,0:T(8,128)(2,1)S(1)} %copy-done.1, bf16[2,192,512]{2,1,0:T(8,128)(2,1)S(1)} %collective-permute-done.25.refs_1_, bf16[2,192,512]{2,1,0:T(8,128)(2,1)S(1)} %collective-permute-done.26.refs_2_, ...), custom_call_target="tpu_custom_call", output_to_operand_aliasing={{}: (10, {})} | custom-call | flops 1610612736 | bytes 7340032 | tf_op jit(solution)/shard_map/pixels/pallas_call | solution.py:440
  211.1 4.2 %pixels.9.refs_10_ = f32[8,1,512,512]{3,2,1,0:T(8,128)} custom-call(bf16[2,192,512]{2,1,0:T(8,128)(2,1)S(1)} %copy-done, bf16[2,192,512]{2,1,0:T(8,128)(2,1)S(1)} %collective-permute-done.18.refs_1_, bf16[2,192,512]{2,1,0:T(8,128)(2,1)S(1)} %collective-permute-done.19.refs_2_, ...), custom_call_target="tpu_custom_call", output_to_operand_aliasing={{}: (10, {})} | custom-call | flops 1610612736 | bytes 7340032 | tf_op jit(solution)/shard_map/pixels/pallas_call | solution.py:440
  215.3 2.9 %pixels.10.refs_10_ = f32[8,1,512,512]{3,2,1,0:T(8,128)} custom-call(bf16[1,104,512]{2,1,0:T(8,128)(2,1)S(1)} %copy-done.4, bf16[1,104,512]{2,1,0:T(8,128)(2,1)S(1)} %collective-permute-done.11.refs_1_, bf16[1,104,512]{2,1,0:T(8,128)(2,1)S(1)} %collective-permute-done.12.refs_2_, ...), custom_call_target="tpu_custom_call", output_to_operand_aliasing={{}: (10, {})} | custom-call | flops 436207616 | bytes 2949120 | tf_op jit(solution)/shard_map/pixels/pallas_call | solution.py:440
  218.5 2.9 %pixels.11 = f32[8,1,512,512]{3,2,1,0:T(8,128)} custom-call(bf16[1,104,512]{2,1,0:T(8,128)(2,1)S(1)} %copy-done.5, bf16[1,104,512]{2,1,0:T(8,128)(2,1)S(1)} %collective-permute-done.3.refs_1_, bf16[1,104,512]{2,1,0:T(8,128)(2,1)S(1)} %collective-permute-done.4.refs_2_, ...), custom_call_target="tpu_custom_call", output_to_operand_aliasing={{}: (10, {})} | custom-call | flops 436207616 | bytes 2949120 | tf_op jit(solution)/shard_map/pixels/pallas_call | solution.py:440
  (119 shorter events, 36.7 us)
Async XLA Ops:
  36.1 13.5 %collective-permute-start.40 = (bf16[1,192,512]{2,1,0:T(8,128)(2,1)}, bf16[1,192,512]{2,1,0:T(8,128)(2,1)S(1)}, u32[]{:S(2)}, u32[]{:S(2)}) collective-permute-start(bf16[1,192,512]{2,1,0:T(8,128)(2,1)} %get-tuple-element.99), channel_id=1, source_target_pairs={{0,8},{4,12},{8,0},{12,4},{16,24},{20,28},{24,16},{28,20},{1,9},{5... | collective-permute-start | bytes 589832 | tf_op jit(solution)/shard_map/ppermute | solution.py:434
  37.6 13.0 %collective-permute-start.41 = (bf16[1,192,512]{2,1,0:T(8,128)(2,1)}, bf16[1,192,512]{2,1,0:T(8,128)(2,1)S(1)}, u32[]{:S(2)}, u32[]{:S(2)}) collective-permute-start(bf16[1,192,512]{2,1,0:T(8,128)(2,1)} %get-tuple-element.100), channel_id=1, source_target_pairs={{0,12},{4,8},{8,4},{12,0},{16,28},{20,24},{24,20},{28,16},{1,13},{... | collective-permute-start | bytes 589832 | tf_op jit(solution)/shard_map/ppermute | solution.py:434
  37.6 13.6 %collective-permute-start.42 = (bf16[1,192,512]{2,1,0:T(8,128)(2,1)}, bf16[1,192,512]{2,1,0:T(8,128)(2,1)S(1)}, u32[]{:S(2)}, u32[]{:S(2)}) collective-permute-start(bf16[1,192,512]{2,1,0:T(8,128)(2,1)} %get-tuple-element.101), channel_id=1, source_target_pairs={{0,16},{4,20},{8,24},{12,28},{16,0},{20,4},{24,8},{28,12},{1,17},{... | collective-permute-start | bytes 589832 | tf_op jit(solution)/shard_map/ppermute | solution.py:434
  39.1 14.3 %collective-permute-start.43 = (bf16[1,192,512]{2,1,0:T(8,128)(2,1)}, bf16[1,192,512]{2,1,0:T(8,128)(2,1)S(1)}, u32[]{:S(2)}, u32[]{:S(2)}) collective-permute-start(bf16[1,192,512]{2,1,0:T(8,128)(2,1)} %get-tuple-element.102), channel_id=1, source_target_pairs={{0,20},{4,16},{8,28},{12,24},{16,4},{20,0},{24,12},{28,8},{1,21},{... | collective-permute-start | bytes 589832 | tf_op jit(solution)/shard_map/ppermute | solution.py:434
  39.6 19.5 %collective-permute-start.44 = (bf16[1,192,512]{2,1,0:T(8,128)(2,1)}, bf16[1,192,512]{2,1,0:T(8,128)(2,1)S(1)}, u32[]{:S(2)}, u32[]{:S(2)}) collective-permute-start(bf16[1,192,512]{2,1,0:T(8,128)(2,1)} %get-tuple-element.103), channel_id=1, source_target_pairs={{0,24},{4,28},{8,16},{12,20},{16,8},{20,12},{24,0},{28,4},{1,25},{... | collective-permute-start | bytes 589832 | tf_op jit(solution)/shard_map/ppermute | solution.py:434
  51.2 12.5 %collective-permute-start.33 = (bf16[1,192,512]{2,1,0:T(8,128)(2,1)}, bf16[1,192,512]{2,1,0:T(8,128)(2,1)S(1)}, u32[]{:S(2)}, u32[]{:S(2)}) collective-permute-start(bf16[1,192,512]{2,1,0:T(8,128)(2,1)} %get-tuple-element.91), channel_id=1, source_target_pairs={{0,8},{4,12},{8,0},{12,4},{16,24},{20,28},{24,16},{28,20},{1,9},{5... | collective-permute-start | bytes 589832 | tf_op jit(solution)/shard_map/ppermute | solution.py:434
  53.4 12.8 %collective-permute-start.34 = (bf16[1,192,512]{2,1,0:T(8,128)(2,1)}, bf16[1,192,512]{2,1,0:T(8,128)(2,1)S(1)}, u32[]{:S(2)}, u32[]{:S(2)}) collective-permute-start(bf16[1,192,512]{2,1,0:T(8,128)(2,1)} %get-tuple-element.92), channel_id=1, source_target_pairs={{0,12},{4,8},{8,4},{12,0},{16,28},{20,24},{24,20},{28,16},{1,13},{... | collective-permute-start | bytes 589832 | tf_op jit(solution)/shard_map/ppermute | solution.py:434
  61.0 45.0 %collective-permute-start.10 = (bf16[4,1,2,48,768]{4,3,2,1,0:T(8,128)(2,1)S(1)}, bf16[4,1,2,48,768]{4,3,2,1,0:T(8,128)(2,1)S(1)}, u32[]{:S(2)}, u32[]{:S(2)}) collective-permute-start(bf16[4,1,2,48,768]{4,3,2,1,0:T(8,128)(2,1)S(1)} %get-tuple-element.105), channel_id=1, source_target_pairs={{0,28},{4,24},{8,20},{12,16},{16,12},{20,8},{24,4},{28,0},{1,29},{... | collective-permute-start | bytes 1769480 | tf_op jit(solution)/shard_map/ppermute | solution.py:320
  61.7 59.8 %collective-permute-start.2 = (bf16[4,1,2,48,768]{4,3,2,1,0:T(8,128)(2,1)S(1)}, bf16[4,1,2,48,768]{4,3,2,1,0:T(8,128)(2,1)S(1)}, u32[]{:S(2)}, u32[]{:S(2)}) collective-permute-start(bf16[4,1,2,48,768]{4,3,2,1,0:T(8,128)(2,1)S(1)} %get-tuple-element.106), channel_id=1, source_target_pairs={{0,28},{4,24},{8,20},{12,16},{16,12},{20,8},{24,4},{28,0},{1,29},{... | collective-permute-start | bytes 1769480 | tf_op jit(solution)/shard_map/ppermute | solution.py:320
  63.7 40.4 %collective-permute-start.36 = (bf16[1,192,512]{2,1,0:T(8,128)(2,1)}, bf16[1,192,512]{2,1,0:T(8,128)(2,1)S(1)}, u32[]{:S(2)}, u32[]{:S(2)}) collective-permute-start(bf16[1,192,512]{2,1,0:T(8,128)(2,1)} %get-tuple-element.94), channel_id=1, source_target_pairs={{0,20},{4,16},{8,28},{12,24},{16,4},{20,0},{24,12},{28,8},{1,21},{... | collective-permute-start | bytes 589832 | tf_op jit(solution)/shard_map/ppermute | solution.py:434
  66.2 38.0 %collective-permute-start.37 = (bf16[1,192,512]{2,1,0:T(8,128)(2,1)}, bf16[1,192,512]{2,1,0:T(8,128)(2,1)S(1)}, u32[]{:S(2)}, u32[]{:S(2)}) collective-permute-start(bf16[1,192,512]{2,1,0:T(8,128)(2,1)} %get-tuple-element.95), channel_id=1, source_target_pairs={{0,24},{4,28},{8,16},{12,20},{16,8},{20,12},{24,0},{28,4},{1,25},{... | collective-permute-start | bytes 589832 | tf_op jit(solution)/shard_map/ppermute | solution.py:434
  67.6 37.9 %collective-permute-start.38 = (bf16[1,192,512]{2,1,0:T(8,128)(2,1)}, bf16[1,192,512]{2,1,0:T(8,128)(2,1)S(1)}, u32[]{:S(2)}, u32[]{:S(2)}) collective-permute-start(bf16[1,192,512]{2,1,0:T(8,128)(2,1)} %get-tuple-element.96), channel_id=1, source_target_pairs={{0,28},{4,24},{8,20},{12,16},{16,12},{20,8},{24,4},{28,0},{1,29},{... | collective-permute-start | bytes 589832 | tf_op jit(solution)/shard_map/ppermute | solution.py:434
  104.1 17.8 %collective-permute-start.25 = (bf16[2,192,512]{2,1,0:T(8,128)(2,1)}, bf16[2,192,512]{2,1,0:T(8,128)(2,1)S(1)}, u32[]{:S(2)}, u32[]{:S(2)}) collective-permute-start(bf16[2,192,512]{2,1,0:T(8,128)(2,1)} %get-tuple-element.82), channel_id=1, source_target_pairs={{0,4},{4,0},{8,12},{12,8},{16,20},{20,16},{24,28},{28,24},{1,5},{5... | collective-permute-start | bytes 1179656 | tf_op jit(solution)/shard_map/ppermute | solution.py:434
  104.2 19.2 %collective-permute-start.26 = (bf16[2,192,512]{2,1,0:T(8,128)(2,1)}, bf16[2,192,512]{2,1,0:T(8,128)(2,1)S(1)}, u32[]{:S(2)}, u32[]{:S(2)}) collective-permute-start(bf16[2,192,512]{2,1,0:T(8,128)(2,1)} %get-tuple-element.83), channel_id=1, source_target_pairs={{0,8},{4,12},{8,0},{12,4},{16,24},{20,28},{24,16},{28,20},{1,9},{5... | collective-permute-start | bytes 1179656 | tf_op jit(solution)/shard_map/ppermute | solution.py:434
  105.5 19.1 %collective-permute-start.27 = (bf16[2,192,512]{2,1,0:T(8,128)(2,1)}, bf16[2,192,512]{2,1,0:T(8,128)(2,1)S(1)}, u32[]{:S(2)}, u32[]{:S(2)}) collective-permute-start(bf16[2,192,512]{2,1,0:T(8,128)(2,1)} %get-tuple-element.84), channel_id=1, source_target_pairs={{0,12},{4,8},{8,4},{12,0},{16,28},{20,24},{24,20},{28,16},{1,13},{... | collective-permute-start | bytes 1179656 | tf_op jit(solution)/shard_map/ppermute | solution.py:434
  106.0 19.0 %collective-permute-start.28 = (bf16[2,192,512]{2,1,0:T(8,128)(2,1)}, bf16[2,192,512]{2,1,0:T(8,128)(2,1)S(1)}, u32[]{:S(2)}, u32[]{:S(2)}) collective-permute-start(bf16[2,192,512]{2,1,0:T(8,128)(2,1)} %get-tuple-element.85), channel_id=1, source_target_pairs={{0,16},{4,20},{8,24},{12,28},{16,0},{20,4},{24,8},{28,12},{1,17},{... | collective-permute-start | bytes 1179656 | tf_op jit(solution)/shard_map/ppermute | solution.py:434
  121.5 28.2 %collective-permute-start.29 = (bf16[2,192,512]{2,1,0:T(8,128)(2,1)S(1)}, bf16[2,192,512]{2,1,0:T(8,128)(2,1)S(1)}, u32[]{:S(2)}, u32[]{:S(2)}) collective-permute-start(bf16[2,192,512]{2,1,0:T(8,128)(2,1)S(1)} %copy-done.8), channel_id=1, source_target_pairs={{0,20},{4,16},{8,28},{12,24},{16,4},{20,0},{24,12},{28,8},{1,21},{... | collective-permute-start | bytes 1179656 | tf_op jit(solution)/shard_map/ppermute | solution.py:434
  121.9 28.3 %collective-permute-start.30 = (bf16[2,192,512]{2,1,0:T(8,128)(2,1)S(1)}, bf16[2,192,512]{2,1,0:T(8,128)(2,1)S(1)}, u32[]{:S(2)}, u32[]{:S(2)}) collective-permute-start(bf16[2,192,512]{2,1,0:T(8,128)(2,1)S(1)} %copy-done.7), channel_id=1, source_target_pairs={{0,24},{4,28},{8,16},{12,20},{16,8},{20,12},{24,0},{28,4},{1,25},{... | collective-permute-start | bytes 1179656 | tf_op jit(solution)/shard_map/ppermute | solution.py:434
  123.4 28.2 %collective-permute-start.31 = (bf16[2,192,512]{2,1,0:T(8,128)(2,1)S(1)}, bf16[2,192,512]{2,1,0:T(8,128)(2,1)S(1)}, u32[]{:S(2)}, u32[]{:S(2)}) collective-permute-start(bf16[2,192,512]{2,1,0:T(8,128)(2,1)S(1)} %copy-done.6), channel_id=1, source_target_pairs={{0,28},{4,24},{8,20},{12,16},{16,12},{20,8},{24,4},{28,0},{1,29},{... | collective-permute-start | bytes 1179656 | tf_op jit(solution)/shard_map/ppermute | solution.py:434
  124.6 27.1 %collective-permute-start.18 = (bf16[2,192,512]{2,1,0:T(8,128)(2,1)}, bf16[2,192,512]{2,1,0:T(8,128)(2,1)S(1)}, u32[]{:S(2)}, u32[]{:S(2)}) collective-permute-start(bf16[2,192,512]{2,1,0:T(8,128)(2,1)} %get-tuple-element.74), channel_id=1, source_target_pairs={{0,4},{4,0},{8,12},{12,8},{16,20},{20,16},{24,28},{28,24},{1,5},{5... | collective-permute-start | bytes 1179656 | tf_op jit(solution)/shard_map/ppermute | solution.py:434
  125.0 30.8 %collective-permute-start.19 = (bf16[2,192,512]{2,1,0:T(8,128)(2,1)}, bf16[2,192,512]{2,1,0:T(8,128)(2,1)S(1)}, u32[]{:S(2)}, u32[]{:S(2)}) collective-permute-start(bf16[2,192,512]{2,1,0:T(8,128)(2,1)} %get-tuple-element.75), channel_id=1, source_target_pairs={{0,8},{4,12},{8,0},{12,4},{16,24},{20,28},{24,16},{28,20},{1,9},{5... | collective-permute-start | bytes 1179656 | tf_op jit(solution)/shard_map/ppermute | solution.py:434
  149.6 21.9 %collective-permute-start.20 = (bf16[2,192,512]{2,1,0:T(8,128)(2,1)}, bf16[2,192,512]{2,1,0:T(8,128)(2,1)S(1)}, u32[]{:S(2)}, u32[]{:S(2)}) collective-permute-start(bf16[2,192,512]{2,1,0:T(8,128)(2,1)} %get-tuple-element.76), channel_id=1, source_target_pairs={{0,12},{4,8},{8,4},{12,0},{16,28},{20,24},{24,20},{28,16},{1,13},{... | collective-permute-start | bytes 1179656 | tf_op jit(solution)/shard_map/ppermute | solution.py:434
  150.2 29.1 %collective-permute-start.21 = (bf16[2,192,512]{2,1,0:T(8,128)(2,1)}, bf16[2,192,512]{2,1,0:T(8,128)(2,1)S(1)}, u32[]{:S(2)}, u32[]{:S(2)}) collective-permute-start(bf16[2,192,512]{2,1,0:T(8,128)(2,1)} %get-tuple-element.77), channel_id=1, source_target_pairs={{0,16},{4,20},{8,24},{12,28},{16,0},{20,4},{24,8},{28,12},{1,17},{... | collective-permute-start | bytes 1179656 | tf_op jit(solution)/shard_map/ppermute | solution.py:434
  151.6 34.3 %collective-permute-start.22 = (bf16[2,192,512]{2,1,0:T(8,128)(2,1)}, bf16[2,192,512]{2,1,0:T(8,128)(2,1)S(1)}, u32[]{:S(2)}, u32[]{:S(2)}) collective-permute-start(bf16[2,192,512]{2,1,0:T(8,128)(2,1)} %get-tuple-element.78), channel_id=1, source_target_pairs={{0,20},{4,16},{8,28},{12,24},{16,4},{20,0},{24,12},{28,8},{1,21},{... | collective-permute-start | bytes 1179656 | tf_op jit(solution)/shard_map/ppermute | solution.py:434
  151.6 36.1 %collective-permute-start.23 = (bf16[2,192,512]{2,1,0:T(8,128)(2,1)}, bf16[2,192,512]{2,1,0:T(8,128)(2,1)S(1)}, u32[]{:S(2)}, u32[]{:S(2)}) collective-permute-start(bf16[2,192,512]{2,1,0:T(8,128)(2,1)} %get-tuple-element.79), channel_id=1, source_target_pairs={{0,24},{4,28},{8,16},{12,20},{16,8},{20,12},{24,0},{28,4},{1,25},{... | collective-permute-start | bytes 1179656 | tf_op jit(solution)/shard_map/ppermute | solution.py:434
  155.7 40.1 %collective-permute-start.24 = (bf16[2,192,512]{2,1,0:T(8,128)(2,1)}, bf16[2,192,512]{2,1,0:T(8,128)(2,1)S(1)}, u32[]{:S(2)}, u32[]{:S(2)}) collective-permute-start(bf16[2,192,512]{2,1,0:T(8,128)(2,1)} %get-tuple-element.80), channel_id=1, source_target_pairs={{0,28},{4,24},{8,20},{12,16},{16,12},{20,8},{24,4},{28,0},{1,29},{... | collective-permute-start | bytes 1179656 | tf_op jit(solution)/shard_map/ppermute | solution.py:434
  171.5 25.2 %collective-permute-start.11 = (bf16[1,104,512]{2,1,0:T(8,128)(2,1)}, bf16[1,104,512]{2,1,0:T(8,128)(2,1)S(1)}, u32[]{:S(2)}, u32[]{:S(2)}) collective-permute-start(bf16[1,104,512]{2,1,0:T(8,128)(2,1)} %get-tuple-element.66), channel_id=1, source_target_pairs={{0,4},{4,0},{8,12},{12,8},{16,20},{20,16},{24,28},{28,24},{1,5},{5... | collective-permute-start | bytes 319496 | tf_op jit(solution)/shard_map/ppermute | solution.py:434
  179.2 18.9 %collective-permute-start.12 = (bf16[1,104,512]{2,1,0:T(8,128)(2,1)}, bf16[1,104,512]{2,1,0:T(8,128)(2,1)S(1)}, u32[]{:S(2)}, u32[]{:S(2)}) collective-permute-start(bf16[1,104,512]{2,1,0:T(8,128)(2,1)} %get-tuple-element.67), channel_id=1, source_target_pairs={{0,8},{4,12},{8,0},{12,4},{16,24},{20,28},{24,16},{28,20},{1,9},{5... | collective-permute-start | bytes 319496 | tf_op jit(solution)/shard_map/ppermute | solution.py:434
  185.9 13.9 %collective-permute-start.13 = (bf16[1,104,512]{2,1,0:T(8,128)(2,1)}, bf16[1,104,512]{2,1,0:T(8,128)(2,1)S(1)}, u32[]{:S(2)}, u32[]{:S(2)}) collective-permute-start(bf16[1,104,512]{2,1,0:T(8,128)(2,1)} %get-tuple-element.68), channel_id=1, source_target_pairs={{0,12},{4,8},{8,4},{12,0},{16,28},{20,24},{24,20},{28,16},{1,13},{... | collective-permute-start | bytes 319496 | tf_op jit(solution)/shard_map/ppermute | solution.py:434
  187.7 12.1 %collective-permute-start.14 = (bf16[1,104,512]{2,1,0:T(8,128)(2,1)}, bf16[1,104,512]{2,1,0:T(8,128)(2,1)S(1)}, u32[]{:S(2)}, u32[]{:S(2)}) collective-permute-start(bf16[1,104,512]{2,1,0:T(8,128)(2,1)} %get-tuple-element.69), channel_id=1, source_target_pairs={{0,16},{4,20},{8,24},{12,28},{16,0},{20,4},{24,8},{28,12},{1,17},{... | collective-permute-start | bytes 319496 | tf_op jit(solution)/shard_map/ppermute | solution.py:434
  205.8 12.5 %collective-permute-start.5 = (bf16[1,104,512]{2,1,0:T(8,128)(2,1)S(1)}, bf16[1,104,512]{2,1,0:T(8,128)(2,1)S(1)}, u32[]{:S(2)}, u32[]{:S(2)}) collective-permute-start(bf16[1,104,512]{2,1,0:T(8,128)(2,1)S(1)} %copy-done.14), channel_id=1, source_target_pairs={{0,12},{4,8},{8,4},{12,0},{16,28},{20,24},{24,20},{28,16},{1,13},{... | collective-permute-start | bytes 319496 | tf_op jit(solution)/shard_map/ppermute | solution.py:434
  206.6 11.6 %collective-permute-start.6 = (bf16[1,104,512]{2,1,0:T(8,128)(2,1)S(1)}, bf16[1,104,512]{2,1,0:T(8,128)(2,1)S(1)}, u32[]{:S(2)}, u32[]{:S(2)}) collective-permute-start(bf16[1,104,512]{2,1,0:T(8,128)(2,1)S(1)} %copy-done.13), channel_id=1, source_target_pairs={{0,16},{4,20},{8,24},{12,28},{16,0},{20,4},{24,8},{28,12},{1,17},{... | collective-permute-start | bytes 319496 | tf_op jit(solution)/shard_map/ppermute | solution.py:434
  (32 other events, 404.8 us)
